TPU v7x, 256 devices: a whole 4x4x8 slice. The times are simulated.
256 devices in a mesh: ctx: 64 (over x, z, y_lo), tp: 4 (over y_hi, core).
Axes of the slice: x: 4, y: 4 (y_hi: 2, y_lo: 2; y = y_hi * 2 + y_lo), z: 8, core: 2. Of those that a mesh axis runs over, the one named last changes fastest.
Arguments:
- pre: float32 [3, 1024, 16384], P(None, 'tp', 'ctx'), may hold values from -6 to 6
- raw_filter: float32 [1024, 16384], P('tp', 'ctx'), may hold values from -6 to 6
- decay: float32 [1024], P('tp'), may hold values from 0 to 1, as said below
- taps: float32 [3, 3, 1024], P(None, None, 'tp'), may hold values from -3.5 to 3.5
- grad_out: float32 [1024, 16384], P(None, ('ctx', 'tp')), may hold values from -6 to 6
Outputs:
- grad_pre: float32 [3, 1024, 16384], P(None, 'tp', 'ctx')
- grad_filter: float32 [1024, 16384], P('tp', 'ctx')
- grad_taps: float32 [3, 3, 1024], P(None, None, 'tp')
Inputs may be any that keep to these rules, and one draw needn't show every extreme that they name: `decay`: rates per token between 0.3 / 16384 and 1 / 40.
All inputs are finite; a program needn't handle non-finite values.
Results may differ from a plain program's by a relative error of at most 0.00013.
Values sent between devices are 32-bit elements; how exact they have to be, the bound alone decides.
No kernel may reach another device: no remote copies, remote signals or barrier semaphores. Data moves between devices by JAX's collectives and lax.ppermute only.
A program may use at most 128 MiB of HBM per device.

v0:
```python
import math

import jax
import jax.numpy as jnp
from jax import lax
from jax.sharding import PartitionSpec as P


def passed_along(x, axis, by):
    devices = lax.axis_size(axis)
    pairs = [(i, i + by) for i in range(devices) if 0 <= i + by < devices]
    return lax.ppermute(x, axis, pairs)


def make_tables(outer_len, inner_len):
    total_len = outer_len * inner_len
    outer_index = jnp.arange(outer_len, dtype=jnp.int32)
    inner_index = jnp.arange(inner_len, dtype=jnp.int32)
    outer_angle = (outer_index[:, None] * outer_index[None, :] % outer_len).astype(jnp.float32) * (
        2.0 * math.pi / outer_len
    )
    inner_angle = (inner_index[:, None] * inner_index[None, :] % inner_len).astype(jnp.float32) * (
        2.0 * math.pi / inner_len
    )
    twist_angle = (outer_index[:, None] * inner_index[None, :] % total_len).astype(jnp.float32) * (
        2.0 * math.pi / total_len
    )
    return (
        jnp.cos(outer_angle),
        jnp.sin(outer_angle),
        jnp.cos(inner_angle),
        jnp.sin(inner_angle),
        jnp.cos(twist_angle),
        jnp.sin(twist_angle),
    )


def matmul_inner(blocks, table):
    return jnp.einsum("ncb,be->nce", blocks, table, precision=lax.Precision.HIGHEST)


def forward_spectrum(signal, tables, outer_len, inner_len):
    cos_outer, sin_outer, cos_inner, sin_inner, cos_twist, sin_twist = tables
    half_rows = outer_len // 2
    blocks = signal.reshape(signal.shape[0], half_rows, inner_len)
    real_a = jnp.einsum(
        "ca,nab->ncb", cos_outer[:, :half_rows], blocks, precision=lax.Precision.HIGHEST
    )
    imag_a = -jnp.einsum(
        "ca,nab->ncb", sin_outer[:, :half_rows], blocks, precision=lax.Precision.HIGHEST
    )
    real_b = real_a * cos_twist + imag_a * sin_twist
    imag_b = imag_a * cos_twist - real_a * sin_twist
    real_r = matmul_inner(real_b, cos_inner) + matmul_inner(imag_b, sin_inner)
    imag_r = matmul_inner(imag_b, cos_inner) - matmul_inner(real_b, sin_inner)
    return (real_r, imag_r)


def inverse_signal(real_r, imag_r, tables, outer_len, inner_len):
    cos_outer, sin_outer, cos_inner, sin_inner, cos_twist, sin_twist = tables
    half_rows = outer_len // 2
    real_s = matmul_inner(real_r, cos_inner) - matmul_inner(imag_r, sin_inner)
    imag_s = matmul_inner(imag_r, cos_inner) + matmul_inner(real_r, sin_inner)
    real_t = real_s * cos_twist - imag_s * sin_twist
    imag_t = imag_s * cos_twist + real_s * sin_twist
    signal = jnp.einsum(
        "ac,ncb->nab", cos_outer[:half_rows], real_t, precision=lax.Precision.HIGHEST
    )
    signal = signal - jnp.einsum(
        "ac,ncb->nab", sin_outer[:half_rows], imag_t, precision=lax.Precision.HIGHEST
    )
    signal = signal * (1.0 / (outer_len * inner_len))
    return signal.reshape(signal.shape[0], half_rows * inner_len)


def long_terms(product, kernel, grad_gate, outer_len, inner_len):
    tables = make_tables(outer_len, inner_len)
    kernel_re, kernel_im = forward_spectrum(kernel, tables, outer_len, inner_len)
    product_re, product_im = forward_spectrum(product, tables, outer_len, inner_len)
    gate_re, gate_im = forward_spectrum(grad_gate, tables, outer_len, inner_len)
    mixed_long = inverse_signal(
        kernel_re * product_re - kernel_im * product_im,
        kernel_re * product_im + kernel_im * product_re,
        tables,
        outer_len,
        inner_len,
    )
    grad_product = inverse_signal(
        kernel_re * gate_re + kernel_im * gate_im,
        kernel_re * gate_im - kernel_im * gate_re,
        tables,
        outer_len,
        inner_len,
    )
    grad_kernel = inverse_signal(
        product_re * gate_re + product_im * gate_im,
        product_re * gate_im - product_im * gate_re,
        tables,
        outer_len,
        inner_len,
    )
    return (mixed_long, grad_product, grad_kernel)


def local(pre, raw_filter, decay, taps, grad_out):
    tap_count = taps.shape[1]
    reach = tap_count - 1
    tok_dev = pre.shape[2]
    ctx_count = lax.axis_size("ctx")
    seq_len = tok_dev * ctx_count
    outer_len = 4 * ctx_count
    inner_len = tok_dev // 2
    before = passed_along(pre[:, :, tok_dev - reach :], "ctx", 1)
    extended = jnp.concatenate([before, pre], axis=2)
    featured = taps[:, 0, :, None] * extended[:, :, reach : reach + tok_dev]
    for j in range(1, tap_count):
        featured = featured + taps[:, j, :, None] * extended[:, :, reach - j : reach - j + tok_dev]
    query_post, key_post, value_post = (featured[0], featured[1], featured[2])
    offset = lax.axis_index("ctx") * tok_dev
    positions = (offset + jnp.arange(tok_dev, dtype=jnp.int32)).astype(jnp.float32)
    envelope = jnp.exp(-decay[:, None] * positions[None, :]) * (1.0 / math.sqrt(seq_len))
    kernel = raw_filter * envelope
    tp_count = lax.axis_size("tp")
    sliver_width = grad_out.shape[0] // (tp_count * ctx_count)
    arranged = grad_out.reshape(tp_count, ctx_count, sliver_width, grad_out.shape[1])
    grad_sliver = lax.all_to_all(
        lax.all_to_all(arranged, "tp", split_axis=0, concat_axis=3, tiled=True),
        "ctx",
        split_axis=1,
        concat_axis=3,
        tiled=True,
    ).reshape(sliver_width, seq_len)
    packed = jnp.stack([query_post, key_post, value_post, kernel])
    slivers = lax.all_to_all(packed, "ctx", split_axis=1, concat_axis=2, tiled=True)
    product = slivers[1] * slivers[2]
    grad_gate = grad_sliver * slivers[0]
    mixed_long, grad_product, grad_kernel = long_terms(
        product, slivers[3], grad_gate, outer_len, inner_len
    )
    results = jnp.stack(
        [
            grad_sliver * mixed_long,
            grad_product * slivers[2],
            grad_product * slivers[1],
            grad_kernel,
        ]
    )
    returned = lax.all_to_all(results, "ctx", split_axis=2, concat_axis=1, tiled=True)
    grad_featured = returned[:3]
    kernel_grad_tok = returned[3]
    after = passed_along(grad_featured[:, :, :reach], "ctx", -1)
    grad_extended = jnp.concatenate([grad_featured, after], axis=2)
    grad_pre = taps[:, 0, :, None] * grad_extended[:, :, 0:tok_dev]
    for j in range(1, tap_count):
        grad_pre = grad_pre + taps[:, j, :, None] * grad_extended[:, :, j : j + tok_dev]
    tap_terms = [
        jnp.sum(grad_featured * extended[:, :, reach - j : reach - j + tok_dev], axis=2)
        for j in range(tap_count)
    ]
    local_taps = jnp.stack(tap_terms, axis=1)
    grad_taps = lax.psum(local_taps, "ctx") * (1.0 / math.sqrt(seq_len))
    grad_filter = kernel_grad_tok * envelope
    return (grad_pre, grad_filter, grad_taps)


def solution(mesh):
    in_specs = (
        P(None, "tp", "ctx"),
        P("tp", "ctx"),
        P("tp"),
        P(None, None, "tp"),
        P(None, ("ctx", "tp")),
    )
    out_specs = (P(None, "tp", "ctx"), P("tp", "ctx"), P(None, None, "tp"))
    return jax.shard_map(local, mesh=mesh, in_specs=in_specs, out_specs=out_specs, check_vma=False)
```

profile of v0, /device:TPU:8, one launch (start us, length us, event | category | flops | bytes accessed | tf_op | source)
XLA Modules:
  0.0 625.3 jit_solution(6635581628537031192)
XLA Ops:
  2.0 3.7 collective-permute-start
  8.1 3.9 all-to-all-start
  12.1 7.4 %all-to-all-done = f32[4,1,16384]{2,1,0:T(1,128)S(1)} async-done(((f32[4,1,16384]{2,1,0:T(1,128)}), f32[4,1,16384]{2,1,0:T(1,128)S(1)}, u32[]{:S(2)}, u32[]{:S(2)}) %all-to-all-start) | async-done | bytes 262176 | tf_op jit(solution)/shard_map/all_to_all | solution.py:127
  23.2 12.0 %all-to-all-start.1 = ((f32[1,64,4,256]{3,2,0,1:T(4,128)}), f32[1,64,4,256]{3,2,0,1:T(4,128)S(1)}, u32[]{:S(2)}, u32[]{:S(2)}) async-start(f32[1,64,4,256]{3,2,0,1:T(4,128)} %reshape.147), calls=%async_computation.1 | async-start | bytes 524288 | tf_op jit(solution)/shard_map/all_to_all | solution.py:126
  36.8 2.5 multiply_add_fusion
  40.8 5.8 all-to-all-done.1
  46.6 6.5 %all-to-all-start.2 = ((f32[4,256,256]{2,0,1:T(4,128)}), f32[4,256,256]{2,0,1:T(4,128)S(1)}, u32[]{:S(2)}, u32[]{:S(2)}) async-start(f32[4,256,256]{2,0,1:T(4,128)} %pad_maximum_fusion.2), calls=%async_computation.2 | async-start | bytes 2097152 | tf_op jit(solution)/shard_map/all_to_all | solution.py:134
  55.8 24.3 %all-to-all-done.2 = f32[4,256,256]{2,0,1:T(4,128)S(1)} async-done(((f32[4,256,256]{2,0,1:T(4,128)}), f32[4,256,256]{2,0,1:T(4,128)S(1)}, u32[]{:S(2)}, u32[]{:S(2)}) %all-to-all-start.2) | async-done | bytes 1048608 | tf_op jit(solution)/shard_map/all_to_all | solution.py:134
  88.1 2.0 fusion.96
  90.1 2.0 fusion.100
  94.1 2.2 fusion.90
  96.3 2.0 fusion.98
  98.3 2.0 fusion.102
  103.9 2.3 convolution_subtract_fusion.4
  131.1 20.5 %copy.280 = f32[4,4,16384]{1,0,2:T(4,128)} copy(f32[4,4,16384]{2,1,0:T(4,128)S(1)} %pad_maximum_fusion.3) | data formatting | bytes 2097152 | tf_op jit(solution)/shard_map/stack | solution.py:140
  151.6 40.5 %reshape.150 = f32[64,1,4096]{2,1,0:T(1,128)S(1)} reshape(f32[16384,4,4]{2,1,0:T(4,128)} %bitcast.144) | data formatting | bytes 2097152
  192.1 34.0 %all_to_all.63 = f32[64,1,4096]{2,1,0:T(1,128)S(1)} all-to-all(f32[64,1,4096]{2,1,0:T(1,128)S(1)} %reshape.150), channel_id=1, replica_groups=mesh['ctx'=64,'tp'=4] {'ctx'}, dimensions={0} | all-to-all | bytes 2097152 | tf_op jit(solution)/shard_map/all_to_all | solution.py:148
  226.1 3.3 reduce.1
  229.4 45.5 %reshape.151 = f32[16384,4,4]{2,1,0:T(4,128)} reshape(f32[64,4096]{1,0:T(8,128)S(1)} %reduce.1) | data formatting | bytes 2097152
  274.9 24.2 %copy.281 = f32[4,4,64,256]{3,1,2,0:T(4,128)S(1)} copy(f32[4,4,64,256]{1,0,3,2:T(4,128)} %bitcast.145) | data formatting | bytes 2097152 | tf_op jit(solution)/shard_map/all_to_all | solution.py:148
  302.7 3.8 collective-permute-start.1
  311.0 8.9 %multiply_reduce_fusion.1 = (f32[3,256]{0,1:T(8,128)}, f32[3,256]{0,1:T(8,128)}, f32[3,256]{0,1:T(8,128)}, f32[3,256,256]{2,0,1:T(4,128)}) fusion(f32[3,256,256]{2,0,1:T(4,128)S(1)} %bitcast.147, f32[3,256,256]{2,0,1:T(4,128)S(1)} %copy-done.1, f32[3,256,2]{2,0,1:T(4,128)S(1)} %copy-done.5, f32[3,256,256]{2,1,0:T(8,128)S(1)} %copy-done.3, ...), kind=kLoop, calls=%fused_computation.46 | loop fusion | flops 2946816 | bytes 3176448 | tf_op jit(solution)/shard_map/reduce_sum | solution.py:157
  322.8 299.3 %psum.7 = f32[3,3,256]{2,0,1:T(4,128)S(1)} all-reduce(f32[3,3,256]{2,0,1:T(4,128)S(1)} %pad_maximum_fusion.4), channel_id=1, replica_groups=mesh['ctx'=64,'tp'=4] {'ctx'}, use_global_device_ids=true, to_apply=%region_3.4 | all-reduce | flops 2304 | bytes 18432 | tf_op jit(solution)/shard_map/psum | solution.py:161
  622.8 2.3 copy.289
  (149 shorter events, 62.7 us)
Async XLA Ops:
  0.6 11.3 %copy-start.30 = (f32[256]{0:T(256)S(1)}, f32[256]{0:T(256)}, u32[]{:S(2)}) copy-start(f32[256]{0:T(256)} %param.7) | copy-start | bytes 3076
  0.6 11.4 %copy-start.28 = (f32[256,256]{1,0:T(8,128)S(1)}, f32[256,256]{1,0:T(8,128)}, u32[]{:S(2)}) copy-start(f32[256,256]{1,0:T(8,128)} %param.6) | copy-start | bytes 786436
  2.0 34.5 %collective-permute-start = (f32[3,256,2]{1,0,2:T(4,128)S(1)}, f32[3,256,2]{1,0,2:T(4,128)S(1)}, u32[]{:S(2)}, u32[]{:S(2)}) collective-permute-start(f32[3,256,2]{1,0,2:T(4,128)S(1)} %copy.326), channel_id=1, source_target_pairs={{0,4},{4,8},{8,12},{12,16},{16,20},{20,24},{24,28},{28,32},{32,36}... | collective-permute-start | bytes 18440 | tf_op jit(solution)/shard_map/ppermute | solution.py:12
  8.1 11.4 %all-to-all-start = ((f32[4,1,16384]{2,1,0:T(1,128)}), f32[4,1,16384]{2,1,0:T(1,128)S(1)}, u32[]{:S(2)}, u32[]{:S(2)}) async-start(f32[4,1,16384]{2,1,0:T(1,128)} %reshape.148), calls=%async_computation | async-start | bytes 524288 | tf_op jit(solution)/shard_map/all_to_all | solution.py:127
  21.4 13.9 %copy-start.29 = (f32[3,3,256]{2,1,0:T(4,128)S(1)}, f32[3,3,256]{2,1,0:T(4,128)}, u32[]{:S(2)}) copy-start(f32[3,3,256]{2,1,0:T(4,128)} %param.8) | copy-start | bytes 27652
  21.4 13.9 %copy-start.2 = (f32[3,256,256]{2,1,0:T(8,128)S(1)}, f32[3,256,256]{2,1,0:T(8,128)}, u32[]{:S(2)}) copy-start(f32[3,256,256]{2,1,0:T(8,128)} %param.5) | copy-start | bytes 2359300
  23.2 23.4 %all-to-all-start.1 = ((f32[1,64,4,256]{3,2,0,1:T(4,128)}), f32[1,64,4,256]{3,2,0,1:T(4,128)S(1)}, u32[]{:S(2)}, u32[]{:S(2)}) async-start(f32[1,64,4,256]{3,2,0,1:T(4,128)} %reshape.147), calls=%async_computation.1 | async-start | bytes 524288 | tf_op jit(solution)/shard_map/all_to_all | solution.py:126
  35.8 3.5 copy-start
  36.1 3.2 copy-start.22
  36.3 3.1 copy-start.23
  36.8 4.0 copy-start.4
  46.6 9.1 %copy-start.14 = (f32[1,64,4,256]{3,2,0,1:T(4,128)}, f32[1,64,4,256]{3,2,0,1:T(4,128)S(1)}, u32[]{:S(2)}) copy-start(f32[1,64,4,256]{3,2,0,1:T(4,128)S(1)} %all-to-all-done.1) | copy-start | bytes 786436
  46.6 33.4 %all-to-all-start.2 = ((f32[4,256,256]{2,0,1:T(4,128)}), f32[4,256,256]{2,0,1:T(4,128)S(1)}, u32[]{:S(2)}, u32[]{:S(2)}) async-start(f32[4,256,256]{2,0,1:T(4,128)} %pad_maximum_fusion.2), calls=%async_computation.2 | async-start | bytes 2097152 | tf_op jit(solution)/shard_map/all_to_all | solution.py:134
  54.1 29.4 %copy-start.6 = (f32[256,256]{1,0:T(8,128)}, f32[256,256]{1,0:T(8,128)S(1)}, u32[]{:S(2)}) copy-start(f32[256,256]{1,0:T(8,128)S(1)} %fusion.61) | copy-start | bytes 786436
  55.1 30.0 %copy-start.10 = (f32[256,256]{1,0:T(8,128)}, f32[256,256]{1,0:T(8,128)S(1)}, u32[]{:S(2)}) copy-start(f32[256,256]{1,0:T(8,128)S(1)} %fusion.60) | copy-start | bytes 786436
  82.9 2.2 copy-start.27
  103.9 2.3 copy-start.20
  114.7 1.8 copy-start.7
  122.0 1.8 copy-start.8
  127.0 1.8 copy-start.9
  300.6 10.4 %copy-start.1 = (f32[3,256,256]{2,0,1:T(4,128)S(1)}, f32[3,256,256]{2,0,1:T(4,128)}, u32[]{:S(2)}) copy-start(f32[3,256,256]{2,0,1:T(4,128)} %copy-done) | copy-start | bytes 2359300
  300.6 10.4 %copy-start.3 = (f32[3,256,256]{2,1,0:T(8,128)S(1)}, f32[3,256,256]{2,1,0:T(8,128)}, u32[]{:S(2)}) copy-start(f32[3,256,256]{2,1,0:T(8,128)} %param.5) | copy-start | bytes 2359300
  300.6 10.4 %copy-start.5 = (f32[3,256,2]{2,0,1:T(4,128)S(1)}, f32[3,256,2]{2,0,1:T(4,128)}, u32[]{:S(2)}) copy-start(f32[3,256,2]{2,0,1:T(4,128)} %copy-done.4) | copy-start | bytes 18436
  302.7 6.6 %collective-permute-start.1 = (f32[3,256,2]{1,0,2:T(4,128)S(1)}, f32[3,256,2]{1,0,2:T(4,128)}, u32[]{:S(2)}, u32[]{:S(2)}) collective-permute-start(f32[3,256,2]{1,0,2:T(4,128)S(1)} %copy.283), channel_id=1, source_target_pairs={{4,0},{8,4},{12,8},{16,12},{20,16},{24,20},{28,24},{32,28},{36,32}... | collective-permute-start | bytes 18440 | tf_op jit(solution)/shard_map/ppermute | solution.py:12
  (12 other events, 14.1 us)
where the time goes:
time: 636 us; the launch traced here: 625 us
  blocking collectives  333 us (52%)
  local copies, waits for them, and re-layouts  157 us (25%)
  matrix products  41.7 us (7%)
  waiting for transfers between devices  38.3 us (6%)
  starting transfers between devices  30 us (5%)
  other arithmetic  23.2 us (4%)
    psum x1, blocking collectives, local(): grad_taps = lax.psum(local_taps, 'ctx') * (1.0 / math.sqrt(seq_len))  299 us
    unnamed x71, local copies, waits for them, and re-layouts  93.3 us
    all_to_all x1, blocking collectives, local(): lax.all_to_all(results, 'ctx', split_axis=2, concat_axis=1, tiled=True)  34 us
    dot_general x24, matrix products, matmul_inner(): jnp.einsum('ncb,be->nce', blocks, table, precision=lax.Precision.HIGHEST)  31.6 us
    all_to_all x1, waiting for transfers between devices, local(): lax.all_to_all(packed, 'ctx', split_axis=1, concat_axis=2, tiled=True)  24.3 us
    all_to_all x1, local copies, waits for them, and re-layouts, local(): lax.all_to_all(results, 'ctx', split_axis=2, concat_axis=1, tiled=True)  24.2 us
    another operation x2, local copies, waits for them, and re-layouts, local(): jnp.stack([grad_sliver * mixed_long, grad_product * slivers[2], grad_prod...  20.6 us
  transfers between devices with their start and end apart: 5, of which 4 were waited for; matrix products, arithmetic and copies ran while one was open for 3% of the time, Pallas kernels for 0%

commit v1 on v0

v1 whole, which is shorter than its diff:
```python
import functools
import math

import jax
import jax.numpy as jnp
import numpy as np
from jax import lax
from jax.experimental import pallas as pl
from jax.experimental.pallas import tpu as pltpu
from jax.sharding import Mesh
from jax.sharding import PartitionSpec as P

CTX = ("x", "z", "y")
PEERS = 64
SIDE = 128
CH = 4
HALVES = 2
BLOCK = 24
REACH = 2
VMEM_LIMIT = 56 * 1024 * 1024


def rounded_pair(table):
    high = table.astype(np.float32).astype(jnp.bfloat16)
    low = (table - high.astype(np.float64)).astype(np.float32).astype(jnp.bfloat16)
    return high, low


def make_tables():
    length = SIDE * SIDE
    row = np.arange(SIDE)
    token_row = HALVES * (row % PEERS) + row // PEERS
    freq = np.arange(SIDE) + 0.25
    outer = 2.0 * np.pi * freq[:, None] * token_row[None, :] / SIDE
    outer_table = np.concatenate([np.cos(outer), np.sin(outer)], axis=0)
    inner = 2.0 * np.pi * ((row[:, None] * row[None, :]) % SIDE) / SIDE
    cos_i, sin_i = np.cos(inner), np.sin(inner)
    inner_table = np.block([[cos_i, sin_i], [-sin_i, cos_i]])
    twist = 2.0 * np.pi * freq[:, None] * row[None, :] / length
    pairs = []
    for table in (outer_table, inner_table, inner_table.T, outer_table.T / length):
        pairs.extend(rounded_pair(table))
    return pairs + [np.cos(twist).astype(np.float32), np.sin(twist).astype(np.float32)]


def halves_of(value):
    high = value.astype(jnp.bfloat16)
    return high, (value - high.astype(jnp.float32)).astype(jnp.bfloat16)


def product_left(high_ref, low_ref, value):
    high, low = halves_of(value)
    dot = functools.partial(jnp.dot, preferred_element_type=jnp.float32)
    return dot(high_ref[...], high) + (dot(high_ref[...], low) + dot(low_ref[...], high))


def product_right(value, high_ref, low_ref):
    high, low = halves_of(value)
    dot = functools.partial(jnp.dot, preferred_element_type=jnp.float32)
    return dot(high, high_ref[...]) + (dot(low, high_ref[...]) + dot(high, low_ref[...]))


def rows_of(part, half, c):
    return pl.ds(part * HALVES * CH + half * CH + c, PEERS, stride=BLOCK)


def put_rows(ref, part, value):
    for half in range(HALVES):
        for c in range(CH):
            ref[rows_of(part, half, c), :] = value[c * PEERS : (c + 1) * PEERS, half * SIDE : (half + 1) * SIDE]


def get_rows(ref, part):
    return jnp.concatenate(
        [
            jnp.concatenate([ref[rows_of(part, half, c), :] for c in range(CH)], axis=0)
            for half in range(HALVES)
        ],
        axis=1,
    )


def delayed(value, older, newer):
    lane = lax.broadcasted_iota(jnp.int32, value.shape, 1)
    one = jnp.where(lane == 0, newer, pltpu.roll(value, 1, axis=1))
    two = jnp.where(lane == 0, older, jnp.where(lane == 1, newer, pltpu.roll(value, 2, axis=1)))
    return one, two


def column(cols, k):
    return cols[:, k : k + 1]


def feature_body(offset_ref, pre_ref, before_ref, raw_ref, decay_ref, taps_ref, gate_ref,
                 send_ref, pair_ref, grad_ref, env_ref, cols_ref):
    cols_ref[...] = jnp.zeros_like(cols_ref)
    for i in range(3):
        cols_ref[3 * i : 3 * i + 3, :] = taps_ref[i]
        cols_ref[10 + 2 * i : 12 + 2 * i, :] = before_ref[i]
    cols_ref[9:10, :] = decay_ref[...]
    cols = cols_ref[...].T
    width = raw_ref.shape[1]
    positions = (offset_ref[0] + lax.broadcasted_iota(jnp.int32, raw_ref.shape, 1)).astype(jnp.float32)
    envelope = jnp.exp(-column(cols, 9) * positions) * (1.0 / SIDE)
    env_ref[...] = envelope
    put_rows(send_ref, 0, raw_ref[...] * envelope)
    featured = []
    for i in range(3):
        value = pre_ref[i]
        one, two = delayed(value, column(cols, 10 + 2 * i), column(cols, 11 + 2 * i))
        featured.append(
            column(cols, 3 * i) * value + column(cols, 3 * i + 1) * one + column(cols, 3 * i + 2) * two
        )
    pair_ref[0] = featured[1]
    pair_ref[1] = featured[2]
    put_rows(send_ref, 1, featured[1] * featured[2])
    grad = gate_ref[...].T
    grad_ref[...] = grad
    put_rows(send_ref, 2, grad * featured[0])


def long_body(recv_ref, outer_h, outer_l, inner_h, inner_l, back_h, back_l, last_h, last_l,
              cos_ref, sin_ref, ret_ref, spec_ref, wide_ref):
    cos_t, sin_t = cos_ref[...], sin_ref[...]
    for part in range(3):
        blocks = jnp.concatenate(
            [
                jnp.concatenate([recv_ref[rows_of(part, half, c), :] for half in range(HALVES)], axis=0)
                for c in range(CH)
            ],
            axis=1,
        )
        wide = product_left(outer_h, outer_l, blocks)
        turned = []
        for c in range(CH):
            re = wide[:SIDE, c * SIDE : (c + 1) * SIDE]
            im = wide[SIDE:, c * SIDE : (c + 1) * SIDE]
            turned.append(jnp.concatenate([re * cos_t - im * sin_t, re * sin_t + im * cos_t], axis=1))
        spec_ref[part] = product_right(jnp.concatenate(turned, axis=0), inner_h, inner_l)
    k_re, k_im = spec_ref[0][:, :SIDE], spec_ref[0][:, SIDE:]
    p_re, p_im = spec_ref[1][:, :SIDE], spec_ref[1][:, SIDE:]
    g_re, g_im = spec_ref[2][:, :SIDE], spec_ref[2][:, SIDE:]
    mixes = (
        lambda: (k_re * p_re - k_im * p_im, k_re * p_im + k_im * p_re),
        lambda: (k_re * g_re + k_im * g_im, k_re * g_im - k_im * g_re),
        lambda: (p_re * g_re + p_im * g_im, p_re * g_im - p_im * g_re),
    )
    for part in range(3):
        back = product_right(jnp.concatenate(mixes[part](), axis=1), back_h, back_l)
        for c in range(CH):
            re = back[c * SIDE : (c + 1) * SIDE, :SIDE]
            im = back[c * SIDE : (c + 1) * SIDE, SIDE:]
            wide_ref[:SIDE, c * SIDE : (c + 1) * SIDE] = re * cos_t + im * sin_t
            wide_ref[SIDE:, c * SIDE : (c + 1) * SIDE] = im * cos_t - re * sin_t
        signal = product_left(last_h, last_l, wide_ref[...])
        for c in range(CH):
            for half in range(HALVES):
                ret_ref[rows_of(part, half, c), :] = signal[
                    half * PEERS : (half + 1) * PEERS, c * SIDE : (c + 1) * SIDE
                ]


def grads_body(ret_ref, pre_ref, before_ref, taps_ref, pair_ref, grad_ref, env_ref,
               gpre_ref, gfilter_ref, part_ref, halo_ref, cols_ref):
    cols_ref[...] = jnp.zeros_like(cols_ref)
    for i in range(3):
        cols_ref[3 * i : 3 * i + 3, :] = taps_ref[i]
        cols_ref[10 + 2 * i : 12 + 2 * i, :] = before_ref[i]
    cols = cols_ref[...].T
    mixed = get_rows(ret_ref, 0)
    grad_product = get_rows(ret_ref, 1)
    gfilter_ref[...] = get_rows(ret_ref, 2) * env_ref[...]
    grads = (grad_ref[...] * mixed, grad_product * pair_ref[1], grad_product * pair_ref[0])
    width = mixed.shape[1]
    lane = lax.broadcasted_iota(jnp.int32, mixed.shape, 1)
    lane_s = lax.broadcasted_iota(jnp.int32, (mixed.shape[0], SIDE), 1)
    sums = jnp.zeros((mixed.shape[0], SIDE), jnp.float32)
    for i in range(3):
        value = pre_ref[i]
        grad = grads[i]
        one, two = delayed(value, column(cols, 10 + 2 * i), column(cols, 11 + 2 * i))
        for j, shifted in enumerate((value, one, two)):
            total = jnp.sum(grad * shifted, axis=1, keepdims=True)
            sums = jnp.where(lane_s == 3 * i + j, total, sums)
        for k in range(REACH):
            sums = jnp.where(lane_s == 10 + 2 * i + k, grad[:, k : k + 1], sums)
        next_one = jnp.where(lane == width - 1, 0.0, pltpu.roll(grad, width - 1, axis=1))
        next_two = jnp.where(lane >= width - 2, 0.0, pltpu.roll(grad, width - 2, axis=1))
        gpre_ref[i] = (
            column(cols, 3 * i) * grad + column(cols, 3 * i + 1) * next_one + column(cols, 3 * i + 2) * next_two
        )
    rows = sums.T
    for k in range(9):
        for half in range(HALVES):
            part_ref[2 * k + half : 2 * k + half + 1, :] = rows[k : k + 1, half * SIDE : (half + 1) * SIDE]
    for i in range(3):
        halo_ref[i] = rows[10 + 2 * i : 12 + 2 * i, :]


def edge_body(gpre_ref, after_ref, taps_ref, out_ref, cols_ref):
    cols_ref[...] = jnp.zeros_like(cols_ref)
    for i in range(3):
        cols_ref[3 * i : 3 * i + 3, :] = taps_ref[i]
        cols_ref[10 + 2 * i : 12 + 2 * i, :] = after_ref[i]
    cols = cols_ref[...].T
    lane = lax.broadcasted_iota(jnp.int32, gpre_ref.shape[1:], 1)
    for i in range(3):
        first, second = column(cols, 10 + 2 * i), column(cols, 11 + 2 * i)
        one, two = column(cols, 3 * i + 1), column(cols, 3 * i + 2)
        extra = jnp.where(
            lane == SIDE - 1, one * first + two * second, jnp.where(lane == SIDE - 2, two * first, 0.0)
        )
        out_ref[i] = gpre_ref[i] + extra


def call(body, outs, scratch, name, **more):
    return pl.pallas_call(
        body,
        out_shape=tuple(jax.ShapeDtypeStruct(s, jnp.float32) for s in outs),
        scratch_shapes=[pltpu.VMEM(s, jnp.float32) for s in scratch],
        compiler_params=pltpu.CompilerParams(vmem_limit_bytes=VMEM_LIMIT),
        name=name,
        **more,
    )


def exchange(blocks):
    shaped = blocks.reshape(PEERS, BLOCK, SIDE)
    moved = lax.all_to_all(shaped, CTX, 0, 0, tiled=True)
    return moved.reshape(PEERS * BLOCK, SIDE)


def summed(part, axes, count):
    copies = jnp.broadcast_to(part[None], (count,) + part.shape)
    return jnp.sum(lax.all_to_all(copies, axes, 0, 0, tiled=True), axis=0)


def along(value, by):
    pairs = [(i, i + by) for i in range(PEERS) if 0 <= i + by < PEERS]
    return lax.ppermute(value, CTX, pairs)


def local(pre, raw_filter, decay, taps, grad_out):
    chans, tok = raw_filter.shape
    tp_count = lax.axis_size("tp")
    tables = [jnp.asarray(t) for t in make_tables()]
    offset = (lax.axis_index(CTX) * tok).astype(jnp.int32).reshape(1)
    decay_row = decay.reshape(1, chans)
    turned = grad_out.T.reshape(grad_out.shape[1], tp_count, chans).transpose(1, 0, 2)
    gate = lax.all_to_all(turned, "tp", 0, 0, tiled=True).reshape(tok, chans)
    before = along(pre[:, :, tok - REACH :].transpose(0, 2, 1), 1)
    whole = pl.BlockSpec(memory_space=pltpu.VMEM)
    send, pair, grad, env = call(
        feature_body,
        ((PEERS * BLOCK, SIDE), (2, chans, tok), (chans, tok), (chans, tok)),
        [(SIDE, chans)],
        "feature",
        in_specs=[pl.BlockSpec(memory_space=pltpu.SMEM)] + [whole] * 6,
    )(offset, pre, before, raw_filter, decay_row, taps, gate)
    (ret,) = call(
        long_body,
        ((PEERS * BLOCK, SIDE),),
        [(3, CH * SIDE, 2 * SIDE), (2 * SIDE, CH * SIDE)],
        "long",
    )(exchange(send), *tables)
    gpre, gfilter, part, halo = call(
        grads_body,
        ((3, chans, tok), (chans, tok), (18, SIDE), (3, REACH, chans)),
        [(SIDE, chans)],
        "grads",
    )(exchange(ret), pre, before, taps, pair, grad, env)
    after = along(halo, -1)
    total = summed(summed(part, "z", 8), ("x", "y"), 8)
    grad_taps = total.reshape(3, 3, chans) * (1.0 / SIDE)
    last = tok // SIDE - 1
    block = pl.BlockSpec((3, chans, SIDE), lambda i: (0, 0, last))
    (grad_pre,) = call(
        edge_body,
        ((3, chans, tok),),
        [(SIDE, chans)],
        "edge",
        grid=(1,),
        in_specs=[
            block,
            pl.BlockSpec((3, REACH, chans), lambda i: (0, 0, 0)),
            pl.BlockSpec((3, 3, chans), lambda i: (0, 0, 0)),
        ],
        out_specs=(block,),
        input_output_aliases={0: 0},
    )(gpre, after, taps)
    return grad_pre, gfilter, grad_taps


def solution(mesh):
    split = Mesh(mesh.devices.reshape(4, 8, 2, 4), CTX + ("tp",))
    in_specs = (
        P(None, "tp", CTX),
        P("tp", CTX),
        P("tp"),
        P(None, None, "tp"),
        P(None, CTX + ("tp",)),
    )
    out_specs = (P(None, "tp", CTX), P("tp", CTX), P(None, None, "tp"))
    return jax.shard_map(local, mesh=split, in_specs=in_specs, out_specs=out_specs, check_vma=False)
```

time: 636 us -> 122 us (0.19); the launches traced: 625 us -> 122 us
  blocking collectives: 333 us -> 76.9 us
  local copies, waits for them, and re-layouts: 157 us -> 5.33 us
  matrix products: 41.7 us -> 0 us
  waiting for transfers between devices: 38.3 us -> 6.94 us
  other arithmetic: 23.2 us -> 0.03 us
  Pallas kernels: 0 us -> 16.8 us
  starting transfers between devices: 30 us -> 15.1 us
    psum x1 -> x0, blocking collectives: 299 us -> none  [local(): grad_taps = lax.psum(local_taps, 'ctx') * (1.0 / math.sqrt(seq_len))]
    unnamed x71 -> x11, local copies, waits for them, and re-layouts: 93.3 us -> 1.46 us
    all_to_all x1 -> x3, blocking collectives: 34 us -> 76.9 us  [the longest x2 64.1 us: exchange(): moved = lax.all_to_all(shaped, CTX, 0, 0, tiled=True)]
    dot_general x36 -> x0, matrix products: 41.7 us -> none  [the longest x24 31.6 us: matmul_inner(): jnp.einsum('ncb,be->nce', blocks, table, precision=lax.Precision.HIGHEST)]
    all_to_all x3 -> x2, waiting for transfers between devices: 37.4 us -> 1.04 us  [the longest x1 1.03 us: local(): gate = lax.all_to_all(turned, 'tp', 0, 0, tiled=True).reshape(tok, chans)]
    all_to_all x6 -> x0, local copies, waits for them, and re-layouts: 26.7 us -> none  [the longest x1 24.2 us: local(): lax.all_to_all(results, 'ctx', split_axis=2, concat_axis=1, tiled=True)]
    another operation x4 -> x0, local copies, waits for them, and re-layouts: 20.9 us -> none  [the longest x2 20.6 us: local(): jnp.stack([grad_sliver * mixed_long, grad_product * slivers[2], grad_prod...]
    pallas_call x0 -> x4, Pallas kernels: none -> 16.8 us  [the longest x1 5.69 us: local(): call(long_body, ((PEERS * BLOCK, SIDE),), [(3, CH * SIDE, 2 * SIDE), (2 *...]
  transfers between devices with their start and end apart: 5 -> 4, of which waited for: 4 -> 3; matrix products, arithmetic and copies ran while one was open for 3% -> 0% of each run, Pallas kernels for 0% -> 2%
where the time goes in v1:
time: 122 us
  blocking collectives  76.9 us (63%)
  Pallas kernels  16.8 us (14%)
  starting transfers between devices  15.1 us (12%)
  waiting for transfers between devices  6.94 us (6%)
  local copies, waits for them, and re-layouts  5.33 us (4%)
    all_to_all x2, blocking collectives, exchange(): moved = lax.all_to_all(shaped, CTX, 0, 0, tiled=True)  64.1 us
    all_to_all x1, blocking collectives, summed(): return jnp.sum(lax.all_to_all(copies, axes, 0, 0, tiled=True), axis=0)  12.8 us
    ppermute x2, starting transfers between devices, along(): return lax.ppermute(value, CTX, pairs)  6.63 us
    ppermute x2, waiting for transfers between devices, along(): return lax.ppermute(value, CTX, pairs)  5.91 us
    pallas_call x1, Pallas kernels, local(): call(long_body, ((PEERS * BLOCK, SIDE),), [(3, CH * SIDE, 2 * SIDE), (2 *...  5.69 us
    pallas_call x1, Pallas kernels, local(): call(grads_body, ((3, chans, tok), (chans, tok), (18, SIDE), (3, REACH, c...  4.91 us
    all_to_all x1, starting transfers between devices, summed(): return jnp.sum(lax.all_to_all(copies, axes, 0, 0, tiled=True), axis=0)  4.88 us
    pallas_call x1, Pallas kernels, local(): call(feature_body, ((PEERS * BLOCK, SIDE), (2, chans, tok), (chans, tok),...  3.73 us
  transfers between devices with their start and end apart: 4, of which 3 were waited for; matrix products, arithmetic and copies ran while one was open for 0% of the time, Pallas kernels for 2%

profile of v1, /device:TPU:8, one launch (start us, length us, event | category | flops | bytes accessed | tf_op | source)
XLA Modules:
  0.0 121.8 jit_solution(12726878699923680722)
XLA Ops:
  0.6 0.0 copy-start
  0.6 1.7 %copy.32 = f32[8,4,8,256]{3,2,0,1:T(8,128)} copy(f32[8,4,8,256]{3,2,1,0:T(8,128)} %bitcast.21) | data formatting | bytes 524288 | tf_op jit(solution)/shard_map/reshape | solution.py:249
  2.4 3.6 %all-to-all-start = ((f32[4,64,256]{2,1,0:T(8,128)}), f32[4,64,256]{2,1,0:T(8,128)S(1)}, u32[]{:S(2)}, u32[]{:S(2)}) async-start(f32[4,64,256]{2,1,0:T(8,128)} %bitcast.15), calls=%async_computation | async-start | bytes 524288 | tf_op jit(solution)/shard_map/all_to_all | solution.py:250
  6.0 0.2 slice.3
  6.1 0.2 copy.29
  6.3 4.6 %collective-permute-start = (f32[3,2,256]{2,1,0:T(2,128)S(1)}, f32[3,2,256]{2,1,0:T(2,128)S(1)}, u32[]{:S(2)}, u32[]{:S(2)}) collective-permute-start(f32[3,2,256]{2,1,0:T(2,128)S(1)} %bitcast.22), channel_id=1, source_target_pairs={{0,4},{4,8},{8,12},{12,16},{16,20},{20,24},{24,28},{28,32},{32,36}... | collective-permute-start | bytes 18440 | tf_op jit(solution)/shard_map/ppermute | solution.py:240
  10.9 1.5 %collective-permute-done.before_ref = f32[3,2,256]{2,1,0:T(2,128)S(1)} collective-permute-done((f32[3,2,256]{2,1,0:T(2,128)S(1)}, f32[3,2,256]{2,1,0:T(2,128)S(1)}, u32[]{:S(2)}, u32[]{:S(2)}) %collective-permute-start) | collective-permute-done | bytes 6176 | tf_op jit(solution)/shard_map/ppermute | solution.py:240
  12.4 1.0 all-to-all-done
  13.5 0.7 copy-done.1
  14.2 3.7 %feature.1 = (f32[1536,128]{1,0:T(8,128)}, f32[2,256,256]{2,1,0:T(8,128)}, f32[256,256]{1,0:T(8,128)}, f32[256,256]{1,0:T(8,128)}) custom-call(s32[1]{0:T(128)} %bitcast.offset_ref, f32[3,256,256]{2,1,0:T(8,128)} %pre_ref.3, f32[3,2,256]{2,1,0:T(2,128)} %copy-done.2, f32[256,256]{1,0:T(8,128)} %raw_ref.1, f32[1,256]{1,0:T(1,128)} %bitcast.23, ...), custom_call_target="tpu_custom_call" | custom-call | tf_op jit(solution)/shard_map/feature/pallas_call | solution.py:253
  17.9 35.3 %all_to_all.25 = f32[64,24,128]{2,1,0:T(8,128)} all-to-all(f32[64,24,128]{2,1,0:T(8,128)} %bitcast.20), channel_id=1, replica_groups=mesh['x'=4,'z'=8,'y'=2,'tp'=4] {'x','z','y'}, dimensions={0} | all-to-all | bytes 1572864 | tf_op jit(solution)/shard_map/all_to_all | solution.py:229
  53.2 5.7 %long.1 = f32[1536,128]{1,0:T(8,128)} custom-call(f32[1536,128]{1,0:T(8,128)} %bitcast.16, bf16[256,128]{1,0:T(8,128)(2,1)} %constant.45.clone.outer_h, bf16[256,128]{1,0:T(8,128)(2,1)} %constant.46.clone.outer_l, bf16[256,256]{1,0:T(8,128)(2,1)} %constant.47.clone.inner_h, bf16[256,256]{1,0:T(8,128)(2,1)} %constant.48.clone.inner_l, ...), custom_call_target="tpu_custom_call" | custom-call | tf_op jit(solution)/shard_map/long/pallas_call | solution.py:260
  58.9 28.8 %all_to_all.26 = f32[64,24,128]{2,1,0:T(8,128)} all-to-all(f32[64,24,128]{2,1,0:T(8,128)} %bitcast.17), channel_id=1, replica_groups=mesh['x'=4,'z'=8,'y'=2,'tp'=4] {'x','z','y'}, dimensions={0} | all-to-all | bytes 1572864 | tf_op jit(solution)/shard_map/all_to_all | solution.py:229
  87.7 4.9 %grads.1 = (f32[3,256,256]{2,1,0:T(8,128)}, f32[256,256]{1,0:T(8,128)}, f32[18,128]{1,0:T(8,128)}, f32[3,2,256]{2,1,0:T(2,128)}) custom-call(f32[1536,128]{1,0:T(8,128)} %bitcast.18, f32[3,256,256]{2,1,0:T(8,128)} %pre_ref.3, f32[3,2,256]{2,1,0:T(2,128)} %copy-done.2, f32[3,3,256]{2,1,0:T(4,128)} %taps_ref.5, f32[2,256,256]{2,1,0:T(8,128)} %get-tuple-element.12.pair_ref, ...), custom_call_target="tpu_custom_call" | custom-call | tf_op jit(solution)/shard_map/grads/pallas_call | solution.py:266
  92.6 0.7 broadcast_in_dim.4
  93.3 12.8 %all_to_all.27 = f32[8,18,128]{2,1,0:T(8,128)S(1)} all-to-all(f32[8,18,128]{2,1,0:T(8,128)S(1)} %broadcast_in_dim.4), channel_id=1, replica_groups=mesh['x'=4,'z'=8,'y'=2,'tp'=4] {'z'}, dimensions={0} | all-to-all | bytes 147456 | tf_op jit(solution)/shard_map/all_to_all | solution.py:235
  106.2 0.6 broadcast_in_dim.5
  106.8 4.9 %all-to-all-start.4 = ((f32[8,18,128]{2,1,0:T(8,128)}), f32[8,18,128]{2,1,0:T(8,128)S(1)}, u32[]{:S(2)}, u32[]{:S(2)}) async-start(f32[8,18,128]{2,1,0:T(8,128)} %broadcast_in_dim.5), calls=%async_computation.4 | async-start | bytes 196608 | tf_op jit(solution)/shard_map/all_to_all | solution.py:235
  111.7 2.0 %collective-permute-start.1 = (f32[3,2,256]{2,1,0:T(2,128)S(1)}, f32[3,2,256]{2,1,0:T(2,128)S(1)}, u32[]{:S(2)}, u32[]{:S(2)}) collective-permute-start(f32[3,2,256]{2,1,0:T(2,128)S(1)} %copy-done.4), channel_id=1, source_target_pairs={{4,0},{8,4},{12,8},{16,12},{20,16},{24,20},{28,24},{32,28},{36,32}... | collective-permute-start | bytes 18440 | tf_op jit(solution)/shard_map/ppermute | solution.py:240
  113.7 4.4 %collective-permute-done.1.after_ref = f32[3,2,256]{2,1,0:T(2,128)S(1)} collective-permute-done((f32[3,2,256]{2,1,0:T(2,128)S(1)}, f32[3,2,256]{2,1,0:T(2,128)S(1)}, u32[]{:S(2)}, u32[]{:S(2)}) %collective-permute-start.1) | collective-permute-done | bytes 6176 | tf_op jit(solution)/shard_map/ppermute | solution.py:240
  118.1 0.6 copy-done.3
  118.7 2.4 %edge.1 = f32[3,256,256]{2,1,0:T(8,128)} custom-call(f32[3,256,256]{2,1,0:T(8,128)} %get-tuple-element.15.gpre_ref, f32[3,2,256]{2,1,0:T(2,128)} %copy-done.3, f32[3,3,256]{2,1,0:T(4,128)} %taps_ref.5), custom_call_target="tpu_custom_call", output_to_operand_aliasing={{}: (0, {})} | custom-call | tf_op jit(solution)/shard_map/edge/pallas_call | solution.py:277
  121.1 0.0 all-to-all-done.4
  121.2 0.6 mul.23
  (10 shorter events, 0.0 us)
Async XLA Ops:
  0.6 5.3 %copy-start = (f32[3,256,256]{2,1,0:T(8,128)S(1)}, f32[3,256,256]{2,1,0:T(8,128)}, u32[]{:S(2)}) copy-start(f32[3,256,256]{2,1,0:T(8,128)} %pre_ref.3) | copy-start | bytes 2359300
  2.4 11.1 %all-to-all-start = ((f32[4,64,256]{2,1,0:T(8,128)}), f32[4,64,256]{2,1,0:T(8,128)S(1)}, u32[]{:S(2)}, u32[]{:S(2)}) async-start(f32[4,64,256]{2,1,0:T(8,128)} %bitcast.15), calls=%async_computation | async-start | bytes 524288 | tf_op jit(solution)/shard_map/all_to_all | solution.py:250
  6.3 6.2 %collective-permute-start = (f32[3,2,256]{2,1,0:T(2,128)S(1)}, f32[3,2,256]{2,1,0:T(2,128)S(1)}, u32[]{:S(2)}, u32[]{:S(2)}) collective-permute-start(f32[3,2,256]{2,1,0:T(2,128)S(1)} %bitcast.22), channel_id=1, source_target_pairs={{0,4},{4,8},{8,12},{12,16},{16,20},{20,24},{24,28},{28,32},{32,36}... | collective-permute-start | bytes 18440 | tf_op jit(solution)/shard_map/ppermute | solution.py:240
  12.4 1.0 copy-start.2
  13.5 0.7 copy-start.1
  106.8 4.9 %copy-start.4 = (f32[3,2,256]{2,1,0:T(2,128)S(1)}, f32[3,2,256]{2,1,0:T(2,128)}, u32[]{:S(2)}) copy-start(f32[3,2,256]{2,1,0:T(2,128)} %get-tuple-element.16) | copy-start | bytes 18436
  106.8 14.3 %all-to-all-start.4 = ((f32[8,18,128]{2,1,0:T(8,128)}), f32[8,18,128]{2,1,0:T(8,128)S(1)}, u32[]{:S(2)}, u32[]{:S(2)}) async-start(f32[8,18,128]{2,1,0:T(8,128)} %broadcast_in_dim.5), calls=%async_computation.4 | async-start | bytes 196608 | tf_op jit(solution)/shard_map/all_to_all | solution.py:235
  111.7 6.4 %collective-permute-start.1 = (f32[3,2,256]{2,1,0:T(2,128)S(1)}, f32[3,2,256]{2,1,0:T(2,128)S(1)}, u32[]{:S(2)}, u32[]{:S(2)}) collective-permute-start(f32[3,2,256]{2,1,0:T(2,128)S(1)} %copy-done.4), channel_id=1, source_target_pairs={{4,0},{8,4},{12,8},{16,12},{20,16},{24,20},{28,24},{32,28},{36,32}... | collective-permute-start | bytes 18440 | tf_op jit(solution)/shard_map/ppermute | solution.py:240
  118.1 0.6 copy-start.3

commit v2 on v1

v2 whole, which is shorter than its diff:
```python
import functools
import math

import jax
import jax.numpy as jnp
import numpy as np
from jax import lax
from jax.experimental import pallas as pl
from jax.experimental.pallas import tpu as pltpu
from jax.sharding import Mesh
from jax.sharding import PartitionSpec as P

CTX = ("x", "z", "y")
PEERS = 64
SIDE = 128
CH = 4
HALVES = 2
SENT = 32
BACK = 32
TAPS_ROW = 24
AFTER_ROW = 25
FIRST_ROW = 26
GROUP = 16
VMEM_LIMIT = 56 * 1024 * 1024


def rounded_pair(table):
    high = table.astype(np.float32).astype(jnp.bfloat16)
    low = (table - high.astype(np.float64)).astype(np.float32).astype(jnp.bfloat16)
    return high, low


def make_tables():
    length = SIDE * SIDE
    row = np.arange(SIDE)
    token_row = HALVES * (row % PEERS) + row // PEERS
    freq = np.arange(SIDE) + 0.25
    outer = 2.0 * np.pi * freq[:, None] * token_row[None, :] / SIDE
    outer_table = np.concatenate([np.cos(outer), np.sin(outer)], axis=0)
    inner = 2.0 * np.pi * ((row[:, None] * row[None, :]) % SIDE) / SIDE
    cos_i, sin_i = np.cos(inner), np.sin(inner)
    inner_table = np.block([[cos_i, sin_i], [-sin_i, cos_i]])
    twist = 2.0 * np.pi * freq[:, None] * row[None, :] / length
    pairs = []
    for table in (outer_table, inner_table, inner_table.T, outer_table.T / length):
        pairs.extend(rounded_pair(table))
    return pairs + [np.cos(twist).astype(np.float32), np.sin(twist).astype(np.float32)]


def halves_of(value):
    high = value.astype(jnp.bfloat16)
    return high, (value - high.astype(jnp.float32)).astype(jnp.bfloat16)


def product_left(high_ref, low_ref, value):
    high, low = halves_of(value)
    dot = functools.partial(jnp.dot, preferred_element_type=jnp.float32)
    return dot(high_ref[...], high) + (dot(high_ref[...], low) + dot(low_ref[...], high))


def product_right(value, high_ref, low_ref):
    high, low = halves_of(value)
    dot = functools.partial(jnp.dot, preferred_element_type=jnp.float32)
    return dot(high, high_ref[...]) + (dot(low, high_ref[...]) + dot(high, low_ref[...]))


def rows_of(row, block):
    return pl.ds(row, PEERS, stride=block)


def put_rows(ref, part, block, value):
    for half in range(HALVES):
        for c in range(CH):
            ref[rows_of((part * HALVES + half) * CH + c, block), :] = value[
                c * PEERS : (c + 1) * PEERS, half * SIDE : (half + 1) * SIDE
            ]


def get_rows(ref, part, block):
    return jnp.concatenate(
        [
            jnp.concatenate([ref[rows_of((part * HALVES + half) * CH + c, block), :] for c in range(CH)], axis=0)
            for half in range(HALVES)
        ],
        axis=1,
    )


def channel_of(ref, part, c, block):
    return jnp.concatenate(
        [ref[rows_of((part * HALVES + half) * CH + c, block), :] for half in range(HALVES)], axis=0
    )


def lanes_of(c):
    return slice(c * SIDE, (c + 1) * SIDE)


def column(cols, k):
    return cols[:, k : k + 1]


def lane_index(shape):
    return lax.broadcasted_iota(jnp.int32, shape, 1)


def row_index(shape):
    return lax.broadcasted_iota(jnp.int32, shape, 0)


def pack_body(place_ref, pre_ref, raw_ref, decay_ref, send_ref, env_ref, cols_ref):
    cols_ref[...] = jnp.zeros_like(cols_ref)
    cols_ref[0:1, :] = decay_ref[...]
    cols = cols_ref[...].T
    tok = raw_ref.shape[1]
    positions = (place_ref[0] * tok + lane_index(raw_ref.shape)).astype(jnp.float32)
    envelope = jnp.exp(-column(cols, 0) * positions) * (1.0 / SIDE)
    env_ref[...] = envelope
    put_rows(send_ref, 0, SENT, raw_ref[...] * envelope)
    for i in range(3):
        put_rows(send_ref, 1 + i, SENT, pre_ref[i])


def prepare_body(pre_ref, taps_ref, pair_ref, cols_out_ref, cols_ref):
    cols_ref[...] = jnp.zeros_like(cols_ref)
    for i in range(3):
        cols_ref[3 * i : 3 * i + 3, :] = taps_ref[i]
    cols = cols_ref[...].T
    cols_out_ref[...] = cols
    for i in (1, 2):
        value = pre_ref[i]
        pair_ref[i - 1] = (
            column(cols, 3 * i) * value
            + column(cols, 3 * i + 1) * pltpu.roll(value, 1, axis=1)
            + column(cols, 3 * i + 2) * pltpu.roll(value, 2, axis=1)
        )


def gate_body(place_ref, own_ref, one_ref, two_ref, three_ref, send_ref, grad_ref, rows_ref):
    count = own_ref.shape[0]
    for d, ref in enumerate((own_ref, one_ref, two_ref, three_ref)):
        base = pl.multiple_of(((place_ref[1] + 4 - d) % 4) * count, count)
        rows_ref[pl.ds(base, count), :] = ref[...]
    grad = rows_ref[...].T
    grad_ref[...] = grad
    put_rows(send_ref, 0, HALVES * CH, grad)


def spectrum(signals, outer_h, outer_l, inner_h, inner_l, cos_t, sin_t):
    wide = product_left(outer_h, outer_l, signals)
    turned = []
    for c in range(CH):
        re = wide[:SIDE, lanes_of(c)]
        im = wide[SIDE:, lanes_of(c)]
        turned.append(jnp.concatenate([re * cos_t - im * sin_t, re * sin_t + im * cos_t], axis=1))
    return product_right(jnp.concatenate(turned, axis=0), inner_h, inner_l)


def first_body(place_ref, recv_ref, taps_ref, outer_h, outer_l, inner_h, inner_l, cos_ref, sin_ref,
               spec_ref, shift_ref, feat_ref, first_ref, work_ref):
    cos_t, sin_t = cos_ref[...], sin_ref[...]
    lane = lane_index((SIDE, SIDE))
    row_h = row_index((PEERS, SIDE))
    lane_h = lane_index((PEERS, SIDE))
    lane_t = lane_index(taps_ref.shape[1:])
    for c in range(CH):
        work_ref[:, lanes_of(c)] = channel_of(recv_ref, 0, c, SENT)
    spec_ref[0] = spectrum(work_ref[...], outer_h, outer_l, inner_h, inner_l, cos_t, sin_t)
    for c in range(CH):
        for i in range(3):
            tap = jnp.sum(
                jnp.where(lane_t == c * PEERS + place_ref[0], taps_ref[i], 0.0), axis=1, keepdims=True
            )
            value = channel_of(recv_ref, 1 + i, c, SENT)
            low, high = value[:PEERS], value[PEERS:]
            carry = jnp.concatenate(
                [jnp.where(row_h == 0, 0.0, pltpu.roll(high, 1, axis=0)), low], axis=0
            )
            one = pltpu.roll(jnp.where(lane >= SIDE - 1, carry, value), 1, axis=1)
            two = pltpu.roll(jnp.where(lane >= SIDE - 2, carry, value), 2, axis=1)
            for j, moved in enumerate((value, one, two)):
                shift_ref[3 * i + j, :, lanes_of(c)] = moved
            feat_ref[i, :, lanes_of(c)] = tap[0:1] * value + tap[1:2] * one + tap[2:3] * two
    first = jnp.zeros((PEERS, SIDE), jnp.float32)
    for i in (1, 2):
        for c in range(CH):
            at = 2 * ((i - 1) * CH + c)
            moved = feat_ref[i, :PEERS, lanes_of(c)]
            moved = pltpu.roll(moved, at, axis=1) if at else moved
            first = jnp.where((lane_h == at) | (lane_h == at + 1), moved, first)
    first_ref[...] = first
    spec_ref[1] = spectrum(feat_ref[1] * feat_ref[2], outer_h, outer_l, inner_h, inner_l, cos_t, sin_t)


def second_body(recv_ref, spec_ref, shift_ref, feat_ref, first_ref, outer_h, outer_l, inner_h, inner_l,
                back_h, back_l, last_h, last_l, cos_ref, sin_ref, ret_ref, gate_ref, wide_ref, sums_ref):
    cos_t, sin_t = cos_ref[...], sin_ref[...]
    for c in range(CH):
        gate_ref[:, lanes_of(c)] = channel_of(recv_ref, 0, c, HALVES * CH)
    grad_spec = spectrum(gate_ref[...] * feat_ref[0], outer_h, outer_l, inner_h, inner_l, cos_t, sin_t)
    k_re, k_im = spec_ref[0, :, :SIDE], spec_ref[0, :, SIDE:]
    p_re, p_im = spec_ref[1, :, :SIDE], spec_ref[1, :, SIDE:]
    g_re, g_im = grad_spec[:, :SIDE], grad_spec[:, SIDE:]
    mixes = (
        lambda: (k_re * p_re - k_im * p_im, k_re * p_im + k_im * p_re),
        lambda: (k_re * g_re + k_im * g_im, k_re * g_im - k_im * g_re),
        lambda: (p_re * g_re + p_im * g_im, p_re * g_im - p_im * g_re),
    )
    lane_h = lane_index((PEERS, SIDE))
    row_h = row_index((PEERS, SIDE))
    after = jnp.zeros((PEERS, SIDE), jnp.float32)
    sums_ref[...] = jnp.zeros_like(sums_ref)
    for part in range(3):
        back = product_right(jnp.concatenate(mixes[part](), axis=1), back_h, back_l)
        for c in range(CH):
            re = back[c * SIDE : (c + 1) * SIDE, :SIDE]
            im = back[c * SIDE : (c + 1) * SIDE, SIDE:]
            wide_ref[:SIDE, lanes_of(c)] = re * cos_t + im * sin_t
            wide_ref[SIDE:, lanes_of(c)] = im * cos_t - re * sin_t
        signal = product_left(last_h, last_l, wide_ref[...])
        for c in range(CH):
            for half in range(HALVES):
                ret_ref[rows_of((part * HALVES + half) * CH + c, BACK), :] = signal[
                    half * PEERS : (half + 1) * PEERS, lanes_of(c)
                ]
        grads = {0: ((0, gate_ref[...]),), 1: ((1, feat_ref[2]), (2, feat_ref[1])), 2: ()}[part]
        for i, factor in grads:
            grad = signal * factor
            for j in range(3):
                total = jnp.sum(grad * shift_ref[3 * i + j], axis=0, keepdims=True)
                for c in range(CH):
                    at = c * GROUP + 3 * i + j
                    sums_ref[at : at + 1, :] = total[:, lanes_of(c)]
            for c in range(CH):
                at = 2 * (i * CH + c)
                moved = grad[:PEERS, lanes_of(c)]
                moved = pltpu.roll(moved, at, axis=1) if at else moved
                after = jnp.where((lane_h == at) | (lane_h == at + 1), moved, after)
    totals = jnp.sum(sums_ref[...].T, axis=0, keepdims=True) * (1.0 / SIDE)
    ret_ref[rows_of(TAPS_ROW, BACK), :] = jnp.broadcast_to(totals, (PEERS, SIDE))
    ret_ref[rows_of(AFTER_ROW, BACK), :] = jnp.where(
        row_h == PEERS - 1, 0.0, pltpu.roll(after, PEERS - 1, axis=0)
    )
    ret_ref[rows_of(FIRST_ROW, BACK), :] = first_ref[...]
    for spare in range(FIRST_ROW + 1, BACK):
        ret_ref[rows_of(spare, BACK), :] = jnp.zeros((PEERS, SIDE), jnp.float32)


def finish_body(ret_ref, pair_ref, cols_in_ref, grad_ref, env_ref, gpre_ref, gfilter_ref, gtaps_ref, turn_ref):
    cols = cols_in_ref[...]
    after = ret_ref[rows_of(AFTER_ROW, BACK), :]
    first = ret_ref[rows_of(FIRST_ROW, BACK), :]
    gfilter_ref[...] = get_rows(ret_ref, 2, BACK) * env_ref[...]
    mixed = get_rows(ret_ref, 0, BACK)
    grad_product = get_rows(ret_ref, 1, BACK)
    lane = lane_index(mixed.shape)
    width = mixed.shape[1]

    def stacked(values, at):
        return jnp.concatenate([column(values, at + 2 * c) for c in range(CH)], axis=0)

    pair = []
    for i in range(2):
        pair.append(
            jnp.where(
                lane == 0,
                stacked(first, 2 * i * CH),
                jnp.where(lane == 1, stacked(first, 2 * i * CH + 1), pair_ref[i]),
            )
        )
    grads = (grad_ref[...] * mixed, grad_product * pair[1], grad_product * pair[0])
    for i in range(3):
        grad = grads[i]
        near, far = stacked(after, 2 * i * CH), stacked(after, 2 * i * CH + 1)
        one = jnp.where(lane == width - 1, near, pltpu.roll(grad, width - 1, axis=1))
        two = jnp.where(
            lane == width - 1, far, jnp.where(lane == width - 2, near, pltpu.roll(grad, width - 2, axis=1))
        )
        gpre_ref[i] = column(cols, 3 * i) * grad + column(cols, 3 * i + 1) * one + column(cols, 3 * i + 2) * two
    turn_ref[...] = jnp.zeros_like(turn_ref)
    turn_ref[:PEERS, :] = ret_ref[rows_of(TAPS_ROW, BACK), :]
    rows = turn_ref[...].T
    for i in range(3):
        gtaps_ref[i] = jnp.concatenate(
            [rows[c * GROUP + 3 * i : c * GROUP + 3 * i + 3, :PEERS] for c in range(CH)], axis=1
        )


def call(body, outs, scratch, name, place=0, operands=0):
    whole = pl.BlockSpec(memory_space=pltpu.VMEM)
    return pl.pallas_call(
        body,
        out_shape=tuple(jax.ShapeDtypeStruct(s, jnp.float32) for s in outs),
        in_specs=[pl.BlockSpec(memory_space=pltpu.SMEM)] * place + [whole] * operands,
        scratch_shapes=[pltpu.VMEM(s, jnp.float32) for s in scratch],
        compiler_params=pltpu.CompilerParams(vmem_limit_bytes=VMEM_LIMIT),
        name=name,
    )


def exchange(blocks):
    rows = blocks.shape[0] // PEERS
    moved = lax.all_to_all(blocks.reshape(PEERS, rows, SIDE), CTX, 0, 0, tiled=True)
    return moved.reshape(PEERS * rows, SIDE)


def local(pre, raw_filter, decay, taps, grad_out):
    chans, tok = raw_filter.shape
    wide = CH * SIDE
    tables = [jnp.asarray(t) for t in make_tables()]
    outer, inner, back, last, twist = tables[0:2], tables[2:4], tables[4:6], tables[6:8], tables[8:10]
    tp_at = lax.axis_index("tp")
    place = jnp.stack([lax.axis_index(CTX), tp_at]).astype(jnp.int32)
    send, env = call(pack_body, ((PEERS * SENT, SIDE), (chans, tok)), [(SIDE, chans)], "pack", 1, 3)(
        place, pre, raw_filter, decay.reshape(1, chans)
    )
    recv = exchange(send)
    turned = grad_out.T
    pieces = []
    for d in range(4):
        piece = lax.dynamic_slice_in_dim(turned, (tp_at + d) % 4 * chans, chans, axis=1)
        pieces.append(lax.ppermute(piece, "tp", [(k, (k + d) % 4) for k in range(4)]) if d else piece)
    pair, cols = call(prepare_body, ((2, chans, tok), (chans, SIDE)), [(SIDE, chans)], "prepare", 0, 2)(pre, taps)
    send_grad, grad = call(
        gate_body, ((PEERS * HALVES * CH, SIDE), (chans, tok)), [(tok, chans)], "gate", 1, 4
    )(place, *pieces)
    send_grad, recv = lax.optimization_barrier((send_grad, recv))
    recv_grad = exchange(send_grad)
    spec, shift, feat, first = call(
        first_body,
        ((2, wide, 2 * SIDE), (9, SIDE, wide), (3, SIDE, wide), (PEERS, SIDE)),
        [(SIDE, wide)],
        "first",
        1,
        8,
    )(place, recv, taps, *outer, *inner, *twist)
    (ret,) = call(
        second_body,
        ((PEERS * BACK, SIDE),),
        [(SIDE, wide), (2 * SIDE, wide), (SIDE, SIDE)],
        "second",
        0,
        15,
    )(recv_grad, spec, shift, feat, first, *outer, *inner, *back, *last, *twist)
    return call(
        finish_body, ((3, chans, tok), (chans, tok), (3, 3, chans)), [(SIDE, SIDE)], "finish", 0, 5
    )(exchange(ret), pair, cols, grad, env)


def solution(mesh):
    split = Mesh(mesh.devices.reshape(4, 8, 2, 4), CTX + ("tp",))
    in_specs = (
        P(None, "tp", CTX),
        P("tp", CTX),
        P("tp"),
        P(None, None, "tp"),
        P(None, CTX + ("tp",)),
    )
    out_specs = (P(None, "tp", CTX), P("tp", CTX), P(None, None, "tp"))
    return jax.shard_map(local, mesh=split, in_specs=in_specs, out_specs=out_specs, check_vma=False)
```

time: 122 us -> 111 us (0.910); the launches traced: 122 us -> 109 us
  blocking collectives: 76.9 us -> 0 us
  waiting for transfers between devices: 6.94 us -> 50.3 us
  starting transfers between devices: 15.1 us -> 31.8 us
  Pallas kernels: 16.8 us -> 22.8 us
  local copies, waits for them, and re-layouts: 5.33 us -> 2.99 us
    all_to_all x3 -> x0, blocking collectives: 76.9 us -> none  [the longest x2 64.1 us: exchange(): moved = lax.all_to_all(shaped, CTX, 0, 0, tiled=True)]
    all_to_all x2 -> x3, waiting for transfers between devices: 1.04 us -> 47.9 us  [exchange(): lax.all_to_all(blocks.reshape(PEERS, rows, SIDE), CTX, 0, 0, tiled=True)]
    all_to_all x2 -> x3, starting transfers between devices: 8.44 us -> 26.6 us  [exchange(): lax.all_to_all(blocks.reshape(PEERS, rows, SIDE), CTX, 0, 0, tiled=True)]
    pallas_call x4 -> x6, Pallas kernels: 16.8 us -> 22.8 us  [the longest x1 6.55 us: local(): call(second_body, ((PEERS * BACK, SIDE),), [(SIDE, wide), (2 * SIDE, wide...]
    ppermute x2 -> x3, waiting for transfers between devices: 5.91 us -> 2.33 us  [local(): lax.ppermute(piece, 'tp', [(k, (k + d) % 4) for k in range(4)])]
    reshape x1 -> x0, local copies, waits for them, and re-layouts: 1.75 us -> none  [local(): grad_out.T.reshape(grad_out.shape[1], tp_count, chans).transpose(1, 0, 2)]
    ppermute x2 -> x3, starting transfers between devices: 6.63 us -> 5.27 us  [local(): lax.ppermute(piece, 'tp', [(k, (k + d) % 4) for k in range(4)])]
    broadcast_in_dim x2 -> x0, local copies, waits for them, and re-layouts: 1.36 us -> none  [summed(): copies = jnp.broadcast_to(part[None], (count,) + part.shape)]
  transfers between devices with their start and end apart: 4 -> 6, of which waited for: 3 -> 6; matrix products, arithmetic and copies ran while one was open for 0% -> 1% of each run, Pallas kernels for 2% -> 8%
where the time goes in v2:
time: 111 us; the launch traced here: 109 us
  waiting for transfers between devices  50.3 us (45%)
  starting transfers between devices  31.8 us (29%)
  Pallas kernels  22.8 us (21%)
  local copies, waits for them, and re-layouts  2.99 us (3%)
    all_to_all x3, waiting for transfers between devices, exchange(): lax.all_to_all(blocks.reshape(PEERS, rows, SIDE), CTX, 0, 0, tiled=True)  47.9 us
    all_to_all x3, starting transfers between devices, exchange(): lax.all_to_all(blocks.reshape(PEERS, rows, SIDE), CTX, 0, 0, tiled=True)  26.6 us
    pallas_call x1, Pallas kernels, local(): call(second_body, ((PEERS * BACK, SIDE),), [(SIDE, wide), (2 * SIDE, wide...  6.55 us
    ppermute x3, starting transfers between devices, local(): lax.ppermute(piece, 'tp', [(k, (k + d) % 4) for k in range(4)])  5.27 us
    pallas_call x1, Pallas kernels, local(): call(first_body, ((2, wide, 2 * SIDE), (9, SIDE, wide), (3, SIDE, wide),...  4.51 us
    pallas_call x1, Pallas kernels, local(): call(finish_body, ((3, chans, tok), (chans, tok), (3, 3, chans)), [(SIDE,...  4.01 us
    pallas_call x1, Pallas kernels, local(): call(pack_body, ((PEERS * SENT, SIDE), (chans, tok)), [(SIDE, chans)], 'p...  3.18 us
    pallas_call x1, Pallas kernels, local(): call(prepare_body, ((2, chans, tok), (chans, SIDE)), [(SIDE, chans)], 'pr...  2.61 us
  transfers between devices with their start and end apart: 6, of which 6 were waited for; matrix products, arithmetic and copies ran while one was open for 1% of the time, Pallas kernels for 8%

profile of v2, /device:TPU:8, one launch (start us, length us, event | category | flops | bytes accessed | tf_op | source)
XLA Modules:
  0.0 109.3 jit_solution(11106603680790138956)
XLA Ops:
  0.6 0.0 copy-start.3
  0.6 0.7 pad_add_fusion.place_ref
  1.3 3.2 %pack.1 = (f32[2048,128]{1,0:T(8,128)}, f32[256,256]{1,0:T(8,128)}) custom-call(s32[2]{0:T(128)} %pad_add_fusion.place_ref, f32[3,256,256]{2,1,0:T(8,128)} %pre_ref.3, f32[256,256]{1,0:T(8,128)} %raw_ref.1, f32[1,256]{1,0:T(1,128)} %bitcast.23), custom_call_target="tpu_custom_call" | custom-call | tf_op jit(solution)/shard_map/pack/pallas_call | solution.py:314
  4.5 12.9 %all-to-all-start = ((f32[64,32,128]{2,1,0:T(8,128)}), f32[64,32,128]{2,1,0:T(8,128)S(1)}, u32[]{:S(2)}, u32[]{:S(2)}) async-start(f32[64,32,128]{2,1,0:T(8,128)} %bitcast.21), calls=%async_computation | async-start | bytes 2097152 | tf_op jit(solution)/shard_map/all_to_all | solution.py:303
  17.5 0.7 dynamic-slice_bitcast_fusion
  18.2 0.0 collective-permute-start
  18.2 2.3 %collective-permute-start.1 = (f32[64,256]{1,0:T(8,128)S(1)}, f32[64,256]{1,0:T(8,128)S(1)}, u32[]{:S(2)}, u32[]{:S(2)}) collective-permute-start(f32[64,256]{1,0:T(8,128)S(1)} %get-tuple-element.30), channel_id=1, source_target_pairs={{0,2},{1,3},{2,0},{3,1},{4,6},{5,7},{6,4},{7,5},{8,10},{9,11},{10,... | collective-permute-start | bytes 196616 | tf_op jit(solution)/shard_map/ppermute | solution.py:322
  20.5 3.0 %collective-permute-start.2 = (f32[64,256]{1,0:T(8,128)S(1)}, f32[64,256]{1,0:T(8,128)S(1)}, u32[]{:S(2)}, u32[]{:S(2)}) collective-permute-start(f32[64,256]{1,0:T(8,128)S(1)} %get-tuple-element.27), channel_id=1, source_target_pairs={{0,3},{1,0},{2,1},{3,2},{4,7},{5,4},{6,5},{7,6},{8,11},{9,8},{10,9... | collective-permute-start | bytes 196616 | tf_op jit(solution)/shard_map/ppermute | solution.py:322
  23.4 1.2 %collective-permute-done.one_ref = f32[64,256]{1,0:T(8,128)S(1)} collective-permute-done((f32[64,256]{1,0:T(8,128)S(1)}, f32[64,256]{1,0:T(8,128)S(1)}, u32[]{:S(2)}, u32[]{:S(2)}) %collective-permute-start) | collective-permute-done | bytes 65568 | tf_op jit(solution)/shard_map/ppermute | solution.py:322
  24.6 0.5 collective-permute-done.1.two_ref
  25.1 0.6 collective-permute-done.2.three_ref
  25.8 0.6 copy-done.6
  26.4 1.9 %gate.1 = (f32[512,128]{1,0:T(8,128)}, f32[256,256]{1,0:T(8,128)}) custom-call(s32[2]{0:T(128)} %pad_add_fusion.place_ref, f32[64,256]{1,0:T(8,128)} %get-tuple-element.29.own_ref, f32[64,256]{1,0:T(8,128)} %copy-done.4, f32[64,256]{1,0:T(8,128)} %copy-done.5, f32[64,256]{1,0:T(8,128)} %copy-done.6), custom_call_target="tpu_custom_call" | custom-call | tf_op jit(solution)/shard_map/gate/pallas_call | solution.py:324
  28.3 16.8 %all-to-all-done = f32[64,32,128]{2,1,0:T(8,128)S(1)} async-done(((f32[64,32,128]{2,1,0:T(8,128)}), f32[64,32,128]{2,1,0:T(8,128)S(1)}, u32[]{:S(2)}, u32[]{:S(2)}) %all-to-all-start) | async-done | bytes 1048608 | tf_op jit(solution)/shard_map/all_to_all | solution.py:303
  45.1 7.3 %all-to-all-start.1 = ((f32[64,8,128]{2,1,0:T(8,128)}), f32[64,8,128]{2,1,0:T(8,128)S(1)}, u32[]{:S(2)}, u32[]{:S(2)}) async-start(f32[64,8,128]{2,1,0:T(8,128)} %bitcast.22), calls=%async_computation.1 | async-start | bytes 524288 | tf_op jit(solution)/shard_map/all_to_all | solution.py:303
  52.4 4.5 %first.1 = (f32[2,512,256]{2,1,0:T(8,128)}, f32[9,128,512]{2,1,0:T(8,128)}, f32[3,128,512]{2,1,0:T(8,128)}, f32[64,128]{1,0:T(8,128)}) custom-call(s32[2]{0:T(128)} %pad_add_fusion.place_ref, f32[2048,128]{1,0:T(8,128)} %bitcast.18, f32[3,3,256]{2,1,0:T(4,128)} %taps_ref.3, bf16[256,128]{1,0:T(8,128)(2,1)} %constant.74.clone.outer_h, ...), custom_call_target="tpu_custom_call" | custom-call | tf_op jit(solution)/shard_map/first/pallas_call | solution.py:329
  56.9 6.8 %all-to-all-done.1 = f32[64,8,128]{2,1,0:T(8,128)S(1)} async-done(((f32[64,8,128]{2,1,0:T(8,128)}), f32[64,8,128]{2,1,0:T(8,128)S(1)}, u32[]{:S(2)}, u32[]{:S(2)}) %all-to-all-start.1) | async-done | bytes 262176 | tf_op jit(solution)/shard_map/all_to_all | solution.py:303
  63.7 0.7 copy-done.2
  64.4 6.6 %second.1 = f32[2048,128]{1,0:T(8,128)} custom-call(f32[512,128]{1,0:T(8,128)} %bitcast.20, f32[2,512,256]{2,1,0:T(8,128)} %get-tuple-element.19.spec_ref, f32[9,128,512]{2,1,0:T(8,128)} %get-tuple-element.20.shift_ref, f32[3,128,512]{2,1,0:T(8,128)} %get-tuple-element.21.feat_ref, f32[64,128]{1,0:T(8,128)} %get-tuple-element.22.first_ref, ...), custom_call_target="tpu_custom_call" | custom-call | tf_op jit(solution)/shard_map/second/pallas_call | solution.py:337
  70.9 6.4 %all-to-all-start.2 = ((f32[64,32,128]{2,1,0:T(8,128)}), f32[64,32,128]{2,1,0:T(8,128)S(1)}, u32[]{:S(2)}, u32[]{:S(2)}) async-start(f32[64,32,128]{2,1,0:T(8,128)} %bitcast.17), calls=%async_computation.2 | async-start | bytes 2097152 | tf_op jit(solution)/shard_map/all_to_all | solution.py:303
  77.3 2.6 %prepare.1 = (f32[2,256,256]{2,1,0:T(8,128)}, f32[256,128]{1,0:T(8,128)}) custom-call(f32[3,256,256]{2,1,0:T(8,128)} %pre_ref.3, f32[3,3,256]{2,1,0:T(4,128)} %taps_ref.3), custom_call_target="tpu_custom_call" | custom-call | tf_op jit(solution)/shard_map/prepare/pallas_call | solution.py:323
  79.9 24.4 %all-to-all-done.2 = f32[64,32,128]{2,1,0:T(8,128)S(1)} async-done(((f32[64,32,128]{2,1,0:T(8,128)}), f32[64,32,128]{2,1,0:T(8,128)S(1)}, u32[]{:S(2)}, u32[]{:S(2)}) %all-to-all-start.2) | async-done | bytes 1048608 | tf_op jit(solution)/shard_map/all_to_all | solution.py:303
  104.3 1.0 copy-done.1
  105.3 4.0 %finish.1 = (f32[3,256,256]{2,1,0:T(8,128)}, f32[256,256]{1,0:T(8,128)}, f32[3,3,256]{2,1,0:T(4,128)}) custom-call(f32[2048,128]{1,0:T(8,128)} %bitcast.19, f32[2,256,256]{2,1,0:T(8,128)} %get-tuple-element.23.pair_ref, f32[256,128]{1,0:T(8,128)} %get-tuple-element.24.cols_in_ref, f32[256,256]{1,0:T(8,128)} %get-tuple-element.25.grad_ref, ...), custom_call_target="tpu_custom_call" | custom-call | tf_op jit(solution)/shard_map/finish/pallas_call | solution.py:345
  (10 shorter events, 0.0 us)
Async XLA Ops:
  0.6 16.9 %copy-start.3 = (f32[1024,64]{0,1:T(8,128)S(1)}, f32[1024,64]{0,1:T(8,128)}, u32[]{:S(2)}) copy-start(f32[1024,64]{0,1:T(8,128)} %param.19) | copy-start | bytes 786436
  4.5 40.6 %all-to-all-start = ((f32[64,32,128]{2,1,0:T(8,128)}), f32[64,32,128]{2,1,0:T(8,128)S(1)}, u32[]{:S(2)}, u32[]{:S(2)}) async-start(f32[64,32,128]{2,1,0:T(8,128)} %bitcast.21), calls=%async_computation | async-start | bytes 2097152 | tf_op jit(solution)/shard_map/all_to_all | solution.py:303
  18.2 6.4 %collective-permute-start = (f32[64,256]{1,0:T(8,128)S(1)}, f32[64,256]{1,0:T(8,128)S(1)}, u32[]{:S(2)}, u32[]{:S(2)}) collective-permute-start(f32[64,256]{1,0:T(8,128)S(1)} %get-tuple-element.28), channel_id=1, source_target_pairs={{0,1},{1,2},{2,3},{3,0},{4,5},{5,6},{6,7},{7,4},{8,9},{9,10},{10,1... | collective-permute-start | bytes 196616 | tf_op jit(solution)/shard_map/ppermute | solution.py:322
  18.2 7.0 %collective-permute-start.1 = (f32[64,256]{1,0:T(8,128)S(1)}, f32[64,256]{1,0:T(8,128)S(1)}, u32[]{:S(2)}, u32[]{:S(2)}) collective-permute-start(f32[64,256]{1,0:T(8,128)S(1)} %get-tuple-element.30), channel_id=1, source_target_pairs={{0,2},{1,3},{2,0},{3,1},{4,6},{5,7},{6,4},{7,5},{8,10},{9,11},{10,... | collective-permute-start | bytes 196616 | tf_op jit(solution)/shard_map/ppermute | solution.py:322
  20.5 5.3 %collective-permute-start.2 = (f32[64,256]{1,0:T(8,128)S(1)}, f32[64,256]{1,0:T(8,128)S(1)}, u32[]{:S(2)}, u32[]{:S(2)}) collective-permute-start(f32[64,256]{1,0:T(8,128)S(1)} %get-tuple-element.27), channel_id=1, source_target_pairs={{0,3},{1,0},{2,1},{3,2},{4,7},{5,4},{6,5},{7,6},{8,11},{9,8},{10,9... | collective-permute-start | bytes 196616 | tf_op jit(solution)/shard_map/ppermute | solution.py:322
  24.6 1.2 %copy-start.4 = (f32[64,256]{1,0:T(8,128)}, f32[64,256]{1,0:T(8,128)S(1)}, u32[]{:S(2)}) copy-start(f32[64,256]{1,0:T(8,128)S(1)} %collective-permute-done.one_ref) | copy-start | bytes 196612
  25.1 0.6 copy-start.5
  25.8 0.6 copy-start.6
  45.1 7.3 %copy-start = (f32[64,32,128]{2,1,0:T(8,128)}, f32[64,32,128]{2,1,0:T(8,128)S(1)}, u32[]{:S(2)}) copy-start(f32[64,32,128]{2,1,0:T(8,128)S(1)} %all-to-all-done) | copy-start | bytes 3145732
  45.1 18.6 %all-to-all-start.1 = ((f32[64,8,128]{2,1,0:T(8,128)}), f32[64,8,128]{2,1,0:T(8,128)S(1)}, u32[]{:S(2)}, u32[]{:S(2)}) async-start(f32[64,8,128]{2,1,0:T(8,128)} %bitcast.22), calls=%async_computation.1 | async-start | bytes 524288 | tf_op jit(solution)/shard_map/all_to_all | solution.py:303
  63.7 0.7 copy-start.2
  70.9 33.4 %all-to-all-start.2 = ((f32[64,32,128]{2,1,0:T(8,128)}), f32[64,32,128]{2,1,0:T(8,128)S(1)}, u32[]{:S(2)}, u32[]{:S(2)}) async-start(f32[64,32,128]{2,1,0:T(8,128)} %bitcast.17), calls=%async_computation.2 | async-start | bytes 2097152 | tf_op jit(solution)/shard_map/all_to_all | solution.py:303
  104.3 1.0 copy-start.1

commit v3 on v2

--- a/solution.py
+++ b/solution.py
@@ -15,12 +15,12 @@
 SIDE = 128
 CH = 4
 HALVES = 2
-SENT = 32
-BACK = 32
-TAPS_ROW = 24
-AFTER_ROW = 25
-FIRST_ROW = 26
+SENT = 40
+BACK = 25
+EXTRA_ROW = 24
 GROUP = 16
+AFTER = 64
+FIRST = 88
 VMEM_LIMIT = 56 * 1024 * 1024
 
 
@@ -136,14 +136,17 @@
         )
 
 
-def gate_body(place_ref, own_ref, one_ref, two_ref, three_ref, send_ref, grad_ref, rows_ref):
+def gate_body(place_ref, own_ref, one_ref, two_ref, three_ref, partial_ref, send_ref, rows_ref, block_ref, done):
     count = own_ref.shape[0]
     for d, ref in enumerate((own_ref, one_ref, two_ref, three_ref)):
-        base = pl.multiple_of(((place_ref[1] + 4 - d) % 4) * count, count)
+        base = pl.multiple_of((place_ref[1] ^ d) * count, count)
         rows_ref[pl.ds(base, count), :] = ref[...]
-    grad = rows_ref[...].T
-    grad_ref[...] = grad
-    put_rows(send_ref, 0, HALVES * CH, grad)
+    put_rows(block_ref, 0, HALVES * CH, rows_ref[...].T)
+    move = pltpu.make_async_copy(
+        block_ref.reshape(PEERS, HALVES * CH, SIDE), send_ref.at[:, SENT - HALVES * CH :, :], done
+    )
+    move.start()
+    move.wait()
 
 
 def spectrum(signals, outer_h, outer_l, inner_h, inner_l, cos_t, sin_t):
@@ -156,16 +159,22 @@
     return product_right(jnp.concatenate(turned, axis=0), inner_h, inner_l)
 
 
-def first_body(place_ref, recv_ref, taps_ref, outer_h, outer_l, inner_h, inner_l, cos_ref, sin_ref,
-               spec_ref, shift_ref, feat_ref, first_ref, work_ref):
+def long_body(place_ref, recv_ref, taps_ref, outer_h, outer_l, inner_h, inner_l, back_h, back_l, last_h, last_l,
+              cos_ref, sin_ref, ret_ref, spec_ref, shift_ref, feat_ref, gate_ref, wide_ref, sums_ref):
     cos_t, sin_t = cos_ref[...], sin_ref[...]
+    tables = (outer_h, outer_l, inner_h, inner_l, cos_t, sin_t)
     lane = lane_index((SIDE, SIDE))
     row_h = row_index((PEERS, SIDE))
     lane_h = lane_index((PEERS, SIDE))
     lane_t = lane_index(taps_ref.shape[1:])
+
+    def placed(value, at, into):
+        moved = pltpu.roll(value, at, axis=1)
+        return jnp.where((lane_h == at) | (lane_h == at + 1), moved, into)
+
     for c in range(CH):
-        work_ref[:, lanes_of(c)] = channel_of(recv_ref, 0, c, SENT)
-    spec_ref[0] = spectrum(work_ref[...], outer_h, outer_l, inner_h, inner_l, cos_t, sin_t)
+        gate_ref[:, lanes_of(c)] = channel_of(recv_ref, 0, c, SENT)
+    spec_ref[0] = spectrum(gate_ref[...], *tables)
     for c in range(CH):
         for i in range(3):
             tap = jnp.sum(
@@ -181,33 +190,21 @@
             for j, moved in enumerate((value, one, two)):
                 shift_ref[3 * i + j, :, lanes_of(c)] = moved
             feat_ref[i, :, lanes_of(c)] = tap[0:1] * value + tap[1:2] * one + tap[2:3] * two
-    first = jnp.zeros((PEERS, SIDE), jnp.float32)
+        gate_ref[:, lanes_of(c)] = channel_of(recv_ref, 4, c, SENT)
+    edges = jnp.zeros((PEERS, SIDE), jnp.float32)
     for i in (1, 2):
         for c in range(CH):
-            at = 2 * ((i - 1) * CH + c)
-            moved = feat_ref[i, :PEERS, lanes_of(c)]
-            moved = pltpu.roll(moved, at, axis=1) if at else moved
-            first = jnp.where((lane_h == at) | (lane_h == at + 1), moved, first)
-    first_ref[...] = first
-    spec_ref[1] = spectrum(feat_ref[1] * feat_ref[2], outer_h, outer_l, inner_h, inner_l, cos_t, sin_t)
-
-
-def second_body(recv_ref, spec_ref, shift_ref, feat_ref, first_ref, outer_h, outer_l, inner_h, inner_l,
-                back_h, back_l, last_h, last_l, cos_ref, sin_ref, ret_ref, gate_ref, wide_ref, sums_ref):
-    cos_t, sin_t = cos_ref[...], sin_ref[...]
-    for c in range(CH):
-        gate_ref[:, lanes_of(c)] = channel_of(recv_ref, 0, c, HALVES * CH)
-    grad_spec = spectrum(gate_ref[...] * feat_ref[0], outer_h, outer_l, inner_h, inner_l, cos_t, sin_t)
+            edges = placed(feat_ref[i, :PEERS, lanes_of(c)], FIRST + 2 * ((i - 1) * CH + c), edges)
+    spec_ref[1] = spectrum(feat_ref[1] * feat_ref[2], *tables)
+    spec_ref[2] = spectrum(gate_ref[...] * feat_ref[0], *tables)
     k_re, k_im = spec_ref[0, :, :SIDE], spec_ref[0, :, SIDE:]
     p_re, p_im = spec_ref[1, :, :SIDE], spec_ref[1, :, SIDE:]
-    g_re, g_im = grad_spec[:, :SIDE], grad_spec[:, SIDE:]
+    g_re, g_im = spec_ref[2, :, :SIDE], spec_ref[2, :, SIDE:]
     mixes = (
         lambda: (k_re * p_re - k_im * p_im, k_re * p_im + k_im * p_re),
         lambda: (k_re * g_re + k_im * g_im, k_re * g_im - k_im * g_re),
         lambda: (p_re * g_re + p_im * g_im, p_re * g_im - p_im * g_re),
     )
-    lane_h = lane_index((PEERS, SIDE))
-    row_h = row_index((PEERS, SIDE))
     after = jnp.zeros((PEERS, SIDE), jnp.float32)
     sums_ref[...] = jnp.zeros_like(sums_ref)
     for part in range(3):
@@ -218,67 +215,62 @@
             wide_ref[:SIDE, lanes_of(c)] = re * cos_t + im * sin_t
             wide_ref[SIDE:, lanes_of(c)] = im * cos_t - re * sin_t
         signal = product_left(last_h, last_l, wide_ref[...])
+        if part == 0:
+            signal = signal * gate_ref[...]
         for c in range(CH):
             for half in range(HALVES):
                 ret_ref[rows_of((part * HALVES + half) * CH + c, BACK), :] = signal[
                     half * PEERS : (half + 1) * PEERS, lanes_of(c)
                 ]
-        grads = {0: ((0, gate_ref[...]),), 1: ((1, feat_ref[2]), (2, feat_ref[1])), 2: ()}[part]
+        grads = {0: ((0, None),), 1: ((1, 2), (2, 1)), 2: ()}[part]
         for i, factor in grads:
-            grad = signal * factor
+            grad = signal if factor is None else signal * feat_ref[factor]
             for j in range(3):
                 total = jnp.sum(grad * shift_ref[3 * i + j], axis=0, keepdims=True)
                 for c in range(CH):
                     at = c * GROUP + 3 * i + j
                     sums_ref[at : at + 1, :] = total[:, lanes_of(c)]
             for c in range(CH):
-                at = 2 * (i * CH + c)
-                moved = grad[:PEERS, lanes_of(c)]
-                moved = pltpu.roll(moved, at, axis=1) if at else moved
-                after = jnp.where((lane_h == at) | (lane_h == at + 1), moved, after)
+                after = placed(grad[:PEERS, lanes_of(c)], AFTER + 2 * (i * CH + c), after)
     totals = jnp.sum(sums_ref[...].T, axis=0, keepdims=True) * (1.0 / SIDE)
-    ret_ref[rows_of(TAPS_ROW, BACK), :] = jnp.broadcast_to(totals, (PEERS, SIDE))
-    ret_ref[rows_of(AFTER_ROW, BACK), :] = jnp.where(
-        row_h == PEERS - 1, 0.0, pltpu.roll(after, PEERS - 1, axis=0)
-    )
-    ret_ref[rows_of(FIRST_ROW, BACK), :] = first_ref[...]
-    for spare in range(FIRST_ROW + 1, BACK):
-        ret_ref[rows_of(spare, BACK), :] = jnp.zeros((PEERS, SIDE), jnp.float32)
-
-
-def finish_body(ret_ref, pair_ref, cols_in_ref, grad_ref, env_ref, gpre_ref, gfilter_ref, gtaps_ref, turn_ref):
+    after = jnp.where(row_h == PEERS - 1, 0.0, pltpu.roll(after, PEERS - 1, axis=0))
+    ret_ref[rows_of(EXTRA_ROW, BACK), :] = jnp.where(
+        lane_h < AFTER, jnp.broadcast_to(totals, (PEERS, SIDE)), jnp.where(lane_h < FIRST, after, edges)
+    )
+
+
+def finish_body(ret_ref, pair_ref, cols_in_ref, env_ref, gpre_ref, gfilter_ref, gtaps_ref, turn_ref):
     cols = cols_in_ref[...]
-    after = ret_ref[rows_of(AFTER_ROW, BACK), :]
-    first = ret_ref[rows_of(FIRST_ROW, BACK), :]
+    extra = ret_ref[rows_of(EXTRA_ROW, BACK), :]
     gfilter_ref[...] = get_rows(ret_ref, 2, BACK) * env_ref[...]
-    mixed = get_rows(ret_ref, 0, BACK)
+    grad_query = get_rows(ret_ref, 0, BACK)
     grad_product = get_rows(ret_ref, 1, BACK)
-    lane = lane_index(mixed.shape)
-    width = mixed.shape[1]
-
-    def stacked(values, at):
-        return jnp.concatenate([column(values, at + 2 * c) for c in range(CH)], axis=0)
+    lane = lane_index(grad_query.shape)
+    width = grad_query.shape[1]
+
+    def stacked(at):
+        return jnp.concatenate([column(extra, at + 2 * c) for c in range(CH)], axis=0)
 
     pair = []
     for i in range(2):
         pair.append(
             jnp.where(
                 lane == 0,
-                stacked(first, 2 * i * CH),
-                jnp.where(lane == 1, stacked(first, 2 * i * CH + 1), pair_ref[i]),
+                stacked(FIRST + 2 * i * CH),
+                jnp.where(lane == 1, stacked(FIRST + 2 * i * CH + 1), pair_ref[i]),
             )
         )
-    grads = (grad_ref[...] * mixed, grad_product * pair[1], grad_product * pair[0])
+    grads = (grad_query, grad_product * pair[1], grad_product * pair[0])
     for i in range(3):
         grad = grads[i]
-        near, far = stacked(after, 2 * i * CH), stacked(after, 2 * i * CH + 1)
+        near, far = stacked(AFTER + 2 * i * CH), stacked(AFTER + 2 * i * CH + 1)
         one = jnp.where(lane == width - 1, near, pltpu.roll(grad, width - 1, axis=1))
         two = jnp.where(
             lane == width - 1, far, jnp.where(lane == width - 2, near, pltpu.roll(grad, width - 2, axis=1))
         )
         gpre_ref[i] = column(cols, 3 * i) * grad + column(cols, 3 * i + 1) * one + column(cols, 3 * i + 2) * two
     turn_ref[...] = jnp.zeros_like(turn_ref)
-    turn_ref[:PEERS, :] = ret_ref[rows_of(TAPS_ROW, BACK), :]
+    turn_ref[:PEERS, :] = extra
     rows = turn_ref[...].T
     for i in range(3):
         gtaps_ref[i] = jnp.concatenate(
@@ -298,53 +290,50 @@
     )
 
 
-def exchange(blocks):
-    rows = blocks.shape[0] // PEERS
-    moved = lax.all_to_all(blocks.reshape(PEERS, rows, SIDE), CTX, 0, 0, tiled=True)
-    return moved.reshape(PEERS * rows, SIDE)
-
-
 def local(pre, raw_filter, decay, taps, grad_out):
     chans, tok = raw_filter.shape
     wide = CH * SIDE
+    own = HALVES * CH
     tables = [jnp.asarray(t) for t in make_tables()]
-    outer, inner, back, last, twist = tables[0:2], tables[2:4], tables[4:6], tables[6:8], tables[8:10]
     tp_at = lax.axis_index("tp")
     place = jnp.stack([lax.axis_index(CTX), tp_at]).astype(jnp.int32)
-    send, env = call(pack_body, ((PEERS * SENT, SIDE), (chans, tok)), [(SIDE, chans)], "pack", 1, 3)(
-        place, pre, raw_filter, decay.reshape(1, chans)
-    )
-    recv = exchange(send)
     turned = grad_out.T
     pieces = []
     for d in range(4):
-        piece = lax.dynamic_slice_in_dim(turned, (tp_at + d) % 4 * chans, chans, axis=1)
-        pieces.append(lax.ppermute(piece, "tp", [(k, (k + d) % 4) for k in range(4)]) if d else piece)
+        piece = lax.dynamic_slice_in_dim(turned, (tp_at ^ d) * chans, chans, axis=1)
+        pieces.append(lax.ppermute(piece, "tp", [(k, k ^ d) for k in range(4)]) if d else piece)
+    partial, env = call(pack_body, ((PEERS * SENT, SIDE), (chans, tok)), [(SIDE, chans)], "pack", 1, 3)(
+        place, pre, raw_filter, decay.reshape(1, chans)
+    )
+    vmem = pl.BlockSpec(memory_space=pltpu.VMEM)
+    send = pl.pallas_call(
+        gate_body,
+        out_shape=jax.ShapeDtypeStruct((PEERS, SENT, SIDE), jnp.float32),
+        in_specs=[pl.BlockSpec(memory_space=pltpu.SMEM)] + [vmem] * 4 + [pl.BlockSpec(memory_space=pl.ANY)],
+        out_specs=pl.BlockSpec(memory_space=pl.ANY),
+        scratch_shapes=[
+            pltpu.VMEM((tok, chans), jnp.float32),
+            pltpu.VMEM((PEERS * own, SIDE), jnp.float32),
+            pltpu.SemaphoreType.DMA(()),
+        ],
+        input_output_aliases={5: 0},
+        compiler_params=pltpu.CompilerParams(vmem_limit_bytes=VMEM_LIMIT),
+        name="gate",
+    )(place, *pieces, partial.reshape(PEERS, SENT, SIDE))
+    recv = lax.all_to_all(send, CTX, 0, 0, tiled=True).reshape(PEERS * SENT, SIDE)
+    (ret,) = call(
+        long_body,
+        ((PEERS * BACK, SIDE),),
+        [(3, wide, 2 * SIDE), (9, SIDE, wide), (3, SIDE, wide), (SIDE, wide), (2 * SIDE, wide), (SIDE, SIDE)],
+        "long",
+        1,
+        12,
+    )(place, recv, taps, *tables)
+    back = lax.all_to_all(ret.reshape(PEERS, BACK, 1, SIDE), CTX, 0, 0, tiled=True).reshape(PEERS * BACK, SIDE)
     pair, cols = call(prepare_body, ((2, chans, tok), (chans, SIDE)), [(SIDE, chans)], "prepare", 0, 2)(pre, taps)
-    send_grad, grad = call(
-        gate_body, ((PEERS * HALVES * CH, SIDE), (chans, tok)), [(tok, chans)], "gate", 1, 4
-    )(place, *pieces)
-    send_grad, recv = lax.optimization_barrier((send_grad, recv))
-    recv_grad = exchange(send_grad)
-    spec, shift, feat, first = call(
-        first_body,
-        ((2, wide, 2 * SIDE), (9, SIDE, wide), (3, SIDE, wide), (PEERS, SIDE)),
-        [(SIDE, wide)],
-        "first",
-        1,
-        8,
-    )(place, recv, taps, *outer, *inner, *twist)
-    (ret,) = call(
-        second_body,
-        ((PEERS * BACK, SIDE),),
-        [(SIDE, wide), (2 * SIDE, wide), (SIDE, SIDE)],
-        "second",
-        0,
-        15,
-    )(recv_grad, spec, shift, feat, first, *outer, *inner, *back, *last, *twist)
     return call(
-        finish_body, ((3, chans, tok), (chans, tok), (3, 3, chans)), [(SIDE, SIDE)], "finish", 0, 5
-    )(exchange(ret), pair, cols, grad, env)
+        finish_body, ((3, chans, tok), (chans, tok), (3, 3, chans)), [(SIDE, SIDE)], "finish", 0, 4
+    )(back, pair, cols, env)
 
 
 def solution(mesh):

time: 111 us -> 100 us (0.901); the launches traced: 109 us -> 99.4 us
  blocking collectives: 0 us -> 46.7 us
  waiting for transfers between devices: 50.3 us -> 20.8 us
  starting transfers between devices: 31.8 us -> 10.7 us
  Pallas kernels: 22.8 us -> 16.9 us
    all_to_all x0 -> x1, blocking collectives: none -> 46.7 us  [local(): lax.all_to_all(send, CTX, 0, 0, tiled=True).reshape(PEERS * SENT, SIDE)]
    all_to_all x3 -> x1, waiting for transfers between devices: 47.9 us -> 19.7 us  [local(): lax.all_to_all(ret.reshape(PEERS, BACK, 1, SIDE), CTX, 0, 0, tiled=True)]
    all_to_all x3 -> x1, starting transfers between devices: 26.6 us -> 7.29 us  [local(): lax.all_to_all(ret.reshape(PEERS, BACK, 1, SIDE), CTX, 0, 0, tiled=True)]
    pallas_call x3 -> x2, Pallas kernels: 13 us -> 7.96 us  [the longest x1 6.1 us: local(): call(long_body, ((PEERS * BACK, SIDE),), [(3, wide, 2 * SIDE), (9, SIDE,...]
    ppermute x3, starting transfers between devices: 5.27 us -> 3.36 us  [local(): lax.ppermute(piece, 'tp', [(k, k ^ d) for k in range(4)])]
    ppermute x3, waiting for transfers between devices: 2.33 us -> 1.14 us  [local(): lax.ppermute(piece, 'tp', [(k, k ^ d) for k in range(4)])]
    unnamed x14 -> x8, local copies, waits for them, and re-layouts: 2.33 us -> 1.53 us
  transfers between devices with their start and end apart: 6 -> 4, of which waited for: 6 -> 2; matrix products, arithmetic and copies ran while one was open for 1% -> 1% of each run, Pallas kernels for 8% -> 5%
where the time goes in v3:
time: 100 us; the launch traced here: 99.4 us
  blocking collectives  46.7 us (47%)
  waiting for transfers between devices  20.8 us (21%)
  Pallas kernels  16.9 us (17%)
  starting transfers between devices  10.7 us (11%)
  local copies, waits for them, and re-layouts  3.12 us (3%)
    all_to_all x1, blocking collectives, local(): lax.all_to_all(send, CTX, 0, 0, tiled=True).reshape(PEERS * SENT, SIDE)  46.7 us
    all_to_all x1, waiting for transfers between devices, local(): lax.all_to_all(ret.reshape(PEERS, BACK, 1, SIDE), CTX, 0, 0, tiled=True)  19.7 us
    all_to_all x1, starting transfers between devices, local(): lax.all_to_all(ret.reshape(PEERS, BACK, 1, SIDE), CTX, 0, 0, tiled=True)  7.29 us
    pallas_call x1, Pallas kernels, local(): call(long_body, ((PEERS * BACK, SIDE),), [(3, wide, 2 * SIDE), (9, SIDE,...  6.1 us
    pallas_call x1, Pallas kernels, local(): call(finish_body, ((3, chans, tok), (chans, tok), (3, 3, chans)), [(SIDE,...  3.62 us
    ppermute x3, starting transfers between devices, local(): lax.ppermute(piece, 'tp', [(k, k ^ d) for k in range(4)])  3.36 us
    pallas_call x1, Pallas kernels, local(): call(pack_body, ((PEERS * SENT, SIDE), (chans, tok)), [(SIDE, chans)], 'p...  2.67 us
    pallas_call x1, Pallas kernels, local(): call(prepare_body, ((2, chans, tok), (chans, SIDE)), [(SIDE, chans)], 'pr...  2.61 us
  transfers between devices with their start and end apart: 4, of which 2 were waited for; matrix products, arithmetic and copies ran while one was open for 1% of the time, Pallas kernels for 5%

profile of v3, /device:TPU:8, one launch (start us, length us, event | category | flops | bytes accessed | tf_op | source)
XLA Modules:
  0.0 99.4 jit_solution(3928931071465684617)
XLA Ops:
  0.7 1.6 %dynamic-slice_bitcast_fusion = (f32[64,256]{1,0:T(8,128)S(1)}, f32[64,256]{1,0:T(8,128)S(1)}, f32[64,256]{1,0:T(8,128)}, f32[64,256]{1,0:T(8,128)S(1)}) fusion(f32[1024,64]{0,1:T(8,128)} %param.19, s32[]{:T(128)S(6)} %select_n.15, s32[]{:T(128)S(6)} %select_n.13, s32[]{:T(128)S(6)} %select_n.12, s32[]{:T(128)S(6)} %select_n.14), kind=kLoop, calls=%fused_computation | loop fusion | bytes 524304 | tf_op jit(solution)/shard_map/dynamic_slice | solution.py:303
  2.2 0.0 collective-permute-start
  2.3 2.3 %collective-permute-start.1 = (f32[64,256]{1,0:T(8,128)S(1)}, f32[64,256]{1,0:T(8,128)S(1)}, u32[]{:S(2)}, u32[]{:S(2)}) collective-permute-start(f32[64,256]{1,0:T(8,128)S(1)} %get-tuple-element.14), channel_id=1, source_target_pairs={{0,2},{1,3},{2,0},{3,1},{4,6},{5,7},{6,4},{7,5},{8,10},{9,11},{10,... | collective-permute-start | bytes 196616 | tf_op jit(solution)/shard_map/ppermute | solution.py:304
  4.5 1.1 %collective-permute-start.2 = (f32[64,256]{1,0:T(8,128)S(1)}, f32[64,256]{1,0:T(8,128)S(1)}, u32[]{:S(2)}, u32[]{:S(2)}) collective-permute-start(f32[64,256]{1,0:T(8,128)S(1)} %get-tuple-element.11), channel_id=1, source_target_pairs={{0,3},{1,2},{2,1},{3,0},{4,7},{5,6},{6,5},{7,4},{8,11},{9,10},{10,... | collective-permute-start | bytes 196616 | tf_op jit(solution)/shard_map/ppermute | solution.py:304
  5.6 0.6 pad_add_fusion.place_ref
  6.2 2.7 %pack.1 = (f32[2560,128]{1,0:T(8,128)}, f32[256,256]{1,0:T(8,128)}) custom-call(s32[2]{0:T(128)} %pad_add_fusion.place_ref, f32[3,256,256]{2,1,0:T(8,128)} %pre_ref.3, f32[256,256]{1,0:T(8,128)} %raw_ref.1, f32[1,256]{1,0:T(1,128)} %bitcast.19), custom_call_target="tpu_custom_call" | custom-call | tf_op jit(solution)/shard_map/pack/pallas_call | solution.py:305
  8.9 0.0 collective-permute-done.one_ref
  8.9 0.0 copy-start.1
  8.9 0.0 collective-permute-done.1.two_ref
  8.9 0.0 copy-start.2
  8.9 1.1 %collective-permute-done.2.three_ref = f32[64,256]{1,0:T(8,128)S(1)} collective-permute-done((f32[64,256]{1,0:T(8,128)S(1)}, f32[64,256]{1,0:T(8,128)S(1)}, u32[]{:S(2)}, u32[]{:S(2)}) %collective-permute-start.2) | collective-permute-done | bytes 65568 | tf_op jit(solution)/shard_map/ppermute | solution.py:304
  10.0 0.0 copy-start.3
  10.0 0.0 copy-done.1
  10.0 0.0 copy-done.2
  10.0 0.6 copy-done.3
  10.7 1.9 %gate.1 = f32[64,40,128]{2,1,0:T(8,128)} custom-call(s32[2]{0:T(128)} %pad_add_fusion.place_ref, f32[64,256]{1,0:T(8,128)} %get-tuple-element.13.own_ref, f32[64,256]{1,0:T(8,128)} %copy-done.1, f32[64,256]{1,0:T(8,128)} %copy-done.2, f32[64,256]{1,0:T(8,128)} %copy-done.3, f32[64,40,128]{2,1,0:T(8,128)} %bitcast.15), custom_call_target="tpu_custom_call", output_to_operand_aliasing={{}: (5, {})} | custom-call | tf_op jit(solution)/shard_map/gate/pallas_call | solution.py:309
  12.5 46.7 %all_to_all.10 = f32[64,40,128]{2,1,0:T(8,128)} all-to-all(f32[64,40,128]{2,1,0:T(8,128)} %gate.1), channel_id=1, replica_groups=mesh['x'=4,'z'=8,'y'=2,'tp'=4] {'x','z','y'}, dimensions={0} | all-to-all | bytes 2621440 | tf_op jit(solution)/shard_map/all_to_all | solution.py:323
  59.2 6.1 %long.1 = f32[1600,128]{1,0:T(8,128)} custom-call(s32[2]{0:T(128)} %pad_add_fusion.place_ref, f32[2560,128]{1,0:T(8,128)} %bitcast.16, f32[3,3,256]{2,1,0:T(4,128)} %taps_ref.3, bf16[256,128]{1,0:T(8,128)(2,1)} %constant.51.clone.outer_h, bf16[256,128]{1,0:T(8,128)(2,1)} %constant.52.clone.outer_l, bf16[256,256]{1,0:T(8,128)(2,1)} %constant.53.clone.inner_h, ...), custom_call_target="tpu_custom_call" | custom-call | tf_op jit(solution)/shard_map/long/pallas_call | solution.py:324
  65.3 7.3 %all-to-all-start.1 = ((f32[64,25,1,128]{3,2,1,0:T(1,128)}), f32[64,25,1,128]{3,2,1,0:T(1,128)S(1)}, u32[]{:S(2)}, u32[]{:S(2)}) async-start(f32[64,25,1,128]{3,2,1,0:T(1,128)} %bitcast.17), calls=%async_computation.1 | async-start | bytes 1638400 | tf_op jit(solution)/shard_map/all_to_all | solution.py:332
  72.6 2.6 %prepare.1 = (f32[2,256,256]{2,1,0:T(8,128)}, f32[256,128]{1,0:T(8,128)}) custom-call(f32[3,256,256]{2,1,0:T(8,128)} %pre_ref.3, f32[3,3,256]{2,1,0:T(4,128)} %taps_ref.3), custom_call_target="tpu_custom_call" | custom-call | tf_op jit(solution)/shard_map/prepare/pallas_call | solution.py:333
  75.2 19.7 %all-to-all-done.1 = f32[64,25,1,128]{3,2,1,0:T(1,128)S(1)} async-done(((f32[64,25,1,128]{3,2,1,0:T(1,128)}), f32[64,25,1,128]{3,2,1,0:T(1,128)S(1)}, u32[]{:S(2)}, u32[]{:S(2)}) %all-to-all-start.1) | async-done | bytes 819232 | tf_op jit(solution)/shard_map/all_to_all | solution.py:332
  94.9 0.0 copy-start
  94.9 0.9 copy-done
  95.8 3.6 %finish.1 = (f32[3,256,256]{2,1,0:T(8,128)}, f32[256,256]{1,0:T(8,128)}, f32[3,3,256]{2,1,0:T(4,128)}) custom-call(f32[1600,128]{1,0:T(8,128)} %bitcast.18, f32[2,256,256]{2,1,0:T(8,128)} %get-tuple-element.8.pair_ref, f32[256,128]{1,0:T(8,128)} %get-tuple-element.9.cols_in_ref, f32[256,256]{1,0:T(8,128)} %get-tuple-element.10.env_ref), custom_call_target="tpu_custom_call" | custom-call | tf_op jit(solution)/shard_map/finish/pallas_call | solution.py:334
Async XLA Ops:
  2.2 6.6 %collective-permute-start = (f32[64,256]{1,0:T(8,128)S(1)}, f32[64,256]{1,0:T(8,128)S(1)}, u32[]{:S(2)}, u32[]{:S(2)}) collective-permute-start(f32[64,256]{1,0:T(8,128)S(1)} %get-tuple-element.12), channel_id=1, source_target_pairs={{0,1},{1,0},{2,3},{3,2},{4,5},{5,4},{6,7},{7,6},{8,9},{9,8},{10,11... | collective-permute-start | bytes 196616 | tf_op jit(solution)/shard_map/ppermute | solution.py:304
  2.3 6.6 %collective-permute-start.1 = (f32[64,256]{1,0:T(8,128)S(1)}, f32[64,256]{1,0:T(8,128)S(1)}, u32[]{:S(2)}, u32[]{:S(2)}) collective-permute-start(f32[64,256]{1,0:T(8,128)S(1)} %get-tuple-element.14), channel_id=1, source_target_pairs={{0,2},{1,3},{2,0},{3,1},{4,6},{5,7},{6,4},{7,5},{8,10},{9,11},{10,... | collective-permute-start | bytes 196616 | tf_op jit(solution)/shard_map/ppermute | solution.py:304
  4.5 5.5 %collective-permute-start.2 = (f32[64,256]{1,0:T(8,128)S(1)}, f32[64,256]{1,0:T(8,128)S(1)}, u32[]{:S(2)}, u32[]{:S(2)}) collective-permute-start(f32[64,256]{1,0:T(8,128)S(1)} %get-tuple-element.11), channel_id=1, source_target_pairs={{0,3},{1,2},{2,1},{3,0},{4,7},{5,6},{6,5},{7,4},{8,11},{9,10},{10,... | collective-permute-start | bytes 196616 | tf_op jit(solution)/shard_map/ppermute | solution.py:304
  8.9 1.2 %copy-start.1 = (f32[64,256]{1,0:T(8,128)}, f32[64,256]{1,0:T(8,128)S(1)}, u32[]{:S(2)}) copy-start(f32[64,256]{1,0:T(8,128)S(1)} %collective-permute-done.one_ref) | copy-start | bytes 196612
  8.9 1.1 %copy-start.2 = (f32[64,256]{1,0:T(8,128)}, f32[64,256]{1,0:T(8,128)S(1)}, u32[]{:S(2)}) copy-start(f32[64,256]{1,0:T(8,128)S(1)} %collective-permute-done.1.two_ref) | copy-start | bytes 196612
  10.0 0.6 copy-start.3
  65.3 29.6 %all-to-all-start.1 = ((f32[64,25,1,128]{3,2,1,0:T(1,128)}), f32[64,25,1,128]{3,2,1,0:T(1,128)S(1)}, u32[]{:S(2)}, u32[]{:S(2)}) async-start(f32[64,25,1,128]{3,2,1,0:T(1,128)} %bitcast.17), calls=%async_computation.1 | async-start | bytes 1638400 | tf_op jit(solution)/shard_map/all_to_all | solution.py:332
  94.9 0.9 copy-start

commit v4 on v3

--- a/solution.py
+++ b/solution.py
@@ -21,7 +21,7 @@
 GROUP = 16
 AFTER = 64
 FIRST = 88
-VMEM_LIMIT = 56 * 1024 * 1024
+VMEM_LIMIT = 24 * 1024 * 1024
 
 
 def rounded_pair(table):
@@ -136,17 +136,12 @@
         )
 
 
-def gate_body(place_ref, own_ref, one_ref, two_ref, three_ref, partial_ref, send_ref, rows_ref, block_ref, done):
+def gate_body(at_ref, own_ref, one_ref, two_ref, three_ref, partial_ref, send_ref, rows_ref):
     count = own_ref.shape[0]
     for d, ref in enumerate((own_ref, one_ref, two_ref, three_ref)):
-        base = pl.multiple_of((place_ref[1] ^ d) * count, count)
+        base = pl.multiple_of((at_ref[0] ^ d) * count, count)
         rows_ref[pl.ds(base, count), :] = ref[...]
-    put_rows(block_ref, 0, HALVES * CH, rows_ref[...].T)
-    move = pltpu.make_async_copy(
-        block_ref.reshape(PEERS, HALVES * CH, SIDE), send_ref.at[:, SENT - HALVES * CH :, :], done
-    )
-    move.start()
-    move.wait()
+    put_rows(send_ref, 4, SENT, rows_ref[...].T)
 
 
 def spectrum(signals, outer_h, outer_l, inner_h, inner_l, cos_t, sin_t):
@@ -278,61 +273,58 @@
         )
 
 
-def call(body, outs, scratch, name, place=0, operands=0):
-    whole = pl.BlockSpec(memory_space=pltpu.VMEM)
-    return pl.pallas_call(
-        body,
-        out_shape=tuple(jax.ShapeDtypeStruct(s, jnp.float32) for s in outs),
-        in_specs=[pl.BlockSpec(memory_space=pltpu.SMEM)] * place + [whole] * operands,
-        scratch_shapes=[pltpu.VMEM(s, jnp.float32) for s in scratch],
-        compiler_params=pltpu.CompilerParams(vmem_limit_bytes=VMEM_LIMIT),
-        name=name,
-    )
+def call(body, outs, scratch, name, place=0, held=True, aliases=None):
+    def run(*operands):
+        near = [
+            value if at < place else pltpu.with_memory_space_constraint(value, pltpu.VMEM)
+            for at, value in enumerate(operands)
+        ]
+        smem = pl.BlockSpec(memory_space=pltpu.SMEM)
+        vmem = pl.BlockSpec(memory_space=pltpu.VMEM)
+        kind = pltpu.VMEM if held else jax.ShapeDtypeStruct
+        return pl.pallas_call(
+            body,
+            out_shape=tuple(kind(s, jnp.float32) for s in outs),
+            in_specs=[smem] * place + [vmem] * (len(operands) - place),
+            out_specs=tuple(vmem for _ in outs),
+            scratch_shapes=[pltpu.VMEM(s, jnp.float32) for s in scratch],
+            input_output_aliases=aliases or {},
+            compiler_params=pltpu.CompilerParams(vmem_limit_bytes=VMEM_LIMIT),
+            name=name,
+        )(*near)
+
+    return run
 
 
 def local(pre, raw_filter, decay, taps, grad_out):
     chans, tok = raw_filter.shape
     wide = CH * SIDE
-    own = HALVES * CH
     tables = [jnp.asarray(t) for t in make_tables()]
-    tp_at = lax.axis_index("tp")
-    place = jnp.stack([lax.axis_index(CTX), tp_at]).astype(jnp.int32)
+    tp_at = lax.axis_index("tp").astype(jnp.int32)
+    place = lax.axis_index(CTX).astype(jnp.int32).reshape(1)
     turned = grad_out.T
     pieces = []
     for d in range(4):
         piece = lax.dynamic_slice_in_dim(turned, (tp_at ^ d) * chans, chans, axis=1)
         pieces.append(lax.ppermute(piece, "tp", [(k, k ^ d) for k in range(4)]) if d else piece)
-    partial, env = call(pack_body, ((PEERS * SENT, SIDE), (chans, tok)), [(SIDE, chans)], "pack", 1, 3)(
+    partial, env = call(pack_body, ((PEERS * SENT, SIDE), (chans, tok)), [(SIDE, chans)], "pack", 1)(
         place, pre, raw_filter, decay.reshape(1, chans)
     )
-    vmem = pl.BlockSpec(memory_space=pltpu.VMEM)
-    send = pl.pallas_call(
-        gate_body,
-        out_shape=jax.ShapeDtypeStruct((PEERS, SENT, SIDE), jnp.float32),
-        in_specs=[pl.BlockSpec(memory_space=pltpu.SMEM)] + [vmem] * 4 + [pl.BlockSpec(memory_space=pl.ANY)],
-        out_specs=pl.BlockSpec(memory_space=pl.ANY),
-        scratch_shapes=[
-            pltpu.VMEM((tok, chans), jnp.float32),
-            pltpu.VMEM((PEERS * own, SIDE), jnp.float32),
-            pltpu.SemaphoreType.DMA(()),
-        ],
-        input_output_aliases={5: 0},
-        compiler_params=pltpu.CompilerParams(vmem_limit_bytes=VMEM_LIMIT),
-        name="gate",
-    )(place, *pieces, partial.reshape(PEERS, SENT, SIDE))
-    recv = lax.all_to_all(send, CTX, 0, 0, tiled=True).reshape(PEERS * SENT, SIDE)
+    (send,) = call(gate_body, ((PEERS * SENT, SIDE),), [(tok, chans)], "gate", 1, aliases={5: 0})(
+        tp_at.reshape(1), *pieces, partial
+    )
+    recv = lax.all_to_all(send.reshape(PEERS, SENT, SIDE), CTX, 0, 0, tiled=True).reshape(PEERS * SENT, SIDE)
     (ret,) = call(
         long_body,
         ((PEERS * BACK, SIDE),),
         [(3, wide, 2 * SIDE), (9, SIDE, wide), (3, SIDE, wide), (SIDE, wide), (2 * SIDE, wide), (SIDE, SIDE)],
         "long",
         1,
-        12,
     )(place, recv, taps, *tables)
     back = lax.all_to_all(ret.reshape(PEERS, BACK, 1, SIDE), CTX, 0, 0, tiled=True).reshape(PEERS * BACK, SIDE)
-    pair, cols = call(prepare_body, ((2, chans, tok), (chans, SIDE)), [(SIDE, chans)], "prepare", 0, 2)(pre, taps)
+    pair, cols = call(prepare_body, ((2, chans, tok), (chans, SIDE)), [(SIDE, chans)], "prepare")(pre, taps)
     return call(
-        finish_body, ((3, chans, tok), (chans, tok), (3, 3, chans)), [(SIDE, SIDE)], "finish", 0, 4
+        finish_body, ((3, chans, tok), (chans, tok), (3, 3, chans)), [(SIDE, SIDE)], "finish", held=False
     )(back, pair, cols, env)
 
 

time: 100 us -> 93.9 us (0.939)
  Pallas kernels: 16.9 us -> 7.78 us
  waiting for transfers between devices: 20.8 us -> 23.2 us
    pallas_call x5, Pallas kernels: 16.9 us -> 7.78 us  [run(): pl.pallas_call(body, out_shape=tuple((kind(s, jnp.float32) for s in outs)...]
    all_to_all x1, waiting for transfers between devices: 19.7 us -> 21.6 us  [local(): lax.all_to_all(ret.reshape(PEERS, BACK, 1, SIDE), CTX, 0, 0, tiled=True)]
    unnamed x8 -> x30, local copies, waits for them, and re-layouts: 1.53 us -> 2.84 us
  transfers between devices with their start and end apart: 4 -> 4, of which waited for: 2 -> 2; matrix products, arithmetic and copies ran while one was open for 1% -> 0% of each run, Pallas kernels for 5% -> 1%
where the time goes in v4:
time: 93.9 us; the launch traced here: 92.9 us
  blocking collectives  46.4 us (49%)
  waiting for transfers between devices  23.2 us (25%)
  starting transfers between devices  10.9 us (12%)
  Pallas kernels  7.78 us (8%)
  local copies, waits for them, and re-layouts  3.8 us (4%)
    all_to_all x1, blocking collectives, local(): lax.all_to_all(send.reshape(PEERS, SENT, SIDE), CTX, 0, 0, tiled=True)  46.4 us
    all_to_all x1, waiting for transfers between devices, local(): lax.all_to_all(ret.reshape(PEERS, BACK, 1, SIDE), CTX, 0, 0, tiled=True)  21.6 us
    pallas_call x5, Pallas kernels, run(): pl.pallas_call(body, out_shape=tuple((kind(s, jnp.float32) for s in outs)...  7.78 us
    all_to_all x1, starting transfers between devices, local(): lax.all_to_all(ret.reshape(PEERS, BACK, 1, SIDE), CTX, 0, 0, tiled=True)  7.43 us
    ppermute x3, starting transfers between devices, local(): lax.ppermute(piece, 'tp', [(k, k ^ d) for k in range(4)])  3.44 us
    unnamed x30, local copies, waits for them, and re-layouts  2.84 us
  transfers between devices with their start and end apart: 4, of which 2 were waited for; matrix products, arithmetic and copies ran while one was open for 0% of the time, Pallas kernels for 1%

profile of v4, /device:TPU:8, one launch (start us, length us, event | category | flops | bytes accessed | tf_op | source)
XLA Modules:
  0.0 92.9 jit_solution(5864144473083436524)
XLA Ops:
  0.7 1.0 %dynamic-slice_bitcast_fusion = (f32[64,256]{1,0:T(8,128)S(1)}, f32[64,256]{1,0:T(8,128)S(1)}, f32[64,256]{1,0:T(8,128)S(1)}, f32[64,256]{1,0:T(8,128)S(1)}) fusion(f32[1024,64]{0,1:T(8,128)} %param.19, s32[]{:T(128)S(6)} %select_n.15, s32[]{:T(128)S(6)} %select_n.13, s32[]{:T(128)S(6)} %select_n.12, s32[]{:T(128)S(6)} %select_n.14), kind=kLoop, calls=%fused_computation | loop fusion | bytes 524304 | tf_op jit(solution)/shard_map/dynamic_slice | solution.py:308
  1.6 0.1 collective-permute-start
  1.7 2.4 %collective-permute-start.1 = (f32[64,256]{1,0:T(8,128)S(1)}, f32[64,256]{1,0:T(8,128)S(1)}, u32[]{:S(2)}, u32[]{:S(2)}) collective-permute-start(f32[64,256]{1,0:T(8,128)S(1)} %get-tuple-element.14), channel_id=1, source_target_pairs={{0,2},{1,3},{2,0},{3,1},{4,6},{5,7},{6,4},{7,5},{8,10},{9,11},{10,... | collective-permute-start | bytes 196616 | tf_op jit(solution)/shard_map/ppermute | solution.py:309
  4.1 1.0 %collective-permute-start.2 = (f32[64,256]{1,0:T(8,128)S(1)}, f32[64,256]{1,0:T(8,128)S(1)}, u32[]{:S(2)}, u32[]{:S(2)}) collective-permute-start(f32[64,256]{1,0:T(8,128)S(1)} %get-tuple-element.11), channel_id=1, source_target_pairs={{0,3},{1,2},{2,1},{3,0},{4,7},{5,6},{6,5},{7,4},{8,11},{9,10},{10,... | collective-permute-start | bytes 196616 | tf_op jit(solution)/shard_map/ppermute | solution.py:309
  5.1 1.1 %copy-done = f32[3,256,256]{2,1,0:T(8,128)S(1)} copy-done((f32[3,256,256]{2,1,0:T(8,128)S(1)}, f32[3,256,256]{2,1,0:T(8,128)}, u32[]{:S(2)}) %copy-start) | copy-done | bytes 786456
  6.2 0.9 %copy-done.2 = f32[256,256]{1,0:T(8,128)S(1)} copy-done((f32[256,256]{1,0:T(8,128)S(1)}, f32[256,256]{1,0:T(8,128)}, u32[]{:S(2)}) %copy-start.2) | copy-done | bytes 262168
  7.2 0.7 copy-done.14
  7.8 0.3 pack.1
  8.1 1.6 %collective-permute-done.2.three_ref = f32[64,256]{1,0:T(8,128)S(1)} collective-permute-done((f32[64,256]{1,0:T(8,128)S(1)}, f32[64,256]{1,0:T(8,128)S(1)}, u32[]{:S(2)}, u32[]{:S(2)}) %collective-permute-start.2) | collective-permute-done | bytes 65568 | tf_op jit(solution)/shard_map/ppermute | solution.py:309
  9.7 0.1 gate.1
  9.8 0.0 copy-start.3
  9.9 0.0 copy-start.4
  9.9 0.0 copy-start.6
  9.9 0.0 copy-start.7
  9.9 0.0 copy-start.8
  9.9 0.0 copy-start.9
  9.9 0.0 copy-start.11
  10.0 0.0 copy-start.12
  10.0 46.4 %all_to_all.10 = f32[64,40,128]{2,1,0:T(8,128)S(1)} all-to-all(f32[64,40,128]{2,1,0:T(8,128)S(1)} %bitcast.15), channel_id=1, replica_groups=mesh['x'=4,'z'=8,'y'=2,'tp'=4] {'x','z','y'}, dimensions={0} | all-to-all | bytes 2621440 | tf_op jit(solution)/shard_map/all_to_all | solution.py:316
  56.5 4.5 %long.1 = f32[1600,128]{1,0:T(8,128)} custom-call(s32[1]{0:T(128)} %bitcast.place_ref, f32[2560,128]{1,0:T(8,128)S(1)} %bitcast.16, f32[3,3,256]{2,1,0:T(4,128)S(1)} %copy-done.13, bf16[256,128]{1,0:T(8,128)(2,1)S(1)} %copy-done.7, bf16[256,128]{1,0:T(8,128)(2,1)S(1)} %copy-done.8, bf16[256,256]{1,0:T(8,128)(2,1)S(1)} %copy-done.3, ...), custom_call_target="tpu_custom_call" | custom-call | tf_op jit(solution)/shard_map/long/pallas_call | solution.py:285
  60.9 7.4 %all-to-all-start.1 = ((f32[64,25,1,128]{3,2,1,0:T(1,128)}), f32[64,25,1,128]{3,2,1,0:T(1,128)S(1)}, u32[]{:S(2)}, u32[]{:S(2)}) async-start(f32[64,25,1,128]{3,2,1,0:T(1,128)} %bitcast.9), calls=%async_computation.1 | async-start | bytes 1638400 | tf_op jit(solution)/shard_map/all_to_all | solution.py:324
  68.4 0.6 prepare.1
  69.0 21.6 %all-to-all-done.1 = f32[64,25,1,128]{3,2,1,0:T(1,128)S(1)} async-done(((f32[64,25,1,128]{3,2,1,0:T(1,128)}), f32[64,25,1,128]{3,2,1,0:T(1,128)S(1)}, u32[]{:S(2)}, u32[]{:S(2)}) %all-to-all-start.1) | async-done | bytes 819232 | tf_op jit(solution)/shard_map/all_to_all | solution.py:324
  90.7 2.2 %finish.1 = (f32[3,256,256]{2,1,0:T(8,128)}, f32[256,256]{1,0:T(8,128)}, f32[3,3,256]{2,1,0:T(4,128)}) custom-call(f32[1600,128]{1,0:T(8,128)S(1)} %bitcast.17, f32[2,256,256]{2,1,0:T(8,128)S(1)} %get-tuple-element.8.pair_ref, f32[256,128]{1,0:T(8,128)S(1)} %get-tuple-element.9.cols_in_ref, f32[256,256]{1,0:T(8,128)S(1)} %get-tuple-element.10.env_ref), custom_call_target="tpu_custom_call" | custom-call | tf_op jit(solution)/shard_map/finish/pallas_call | solution.py:285
  (21 shorter events, 0.1 us)
Async XLA Ops:
  1.6 6.5 %collective-permute-start = (f32[64,256]{1,0:T(8,128)S(1)}, f32[64,256]{1,0:T(8,128)S(1)}, u32[]{:S(2)}, u32[]{:S(2)}) collective-permute-start(f32[64,256]{1,0:T(8,128)S(1)} %get-tuple-element.12), channel_id=1, source_target_pairs={{0,1},{1,0},{2,3},{3,2},{4,5},{5,4},{6,7},{7,6},{8,9},{9,8},{10,11... | collective-permute-start | bytes 196616 | tf_op jit(solution)/shard_map/ppermute | solution.py:309
  1.7 6.4 %collective-permute-start.1 = (f32[64,256]{1,0:T(8,128)S(1)}, f32[64,256]{1,0:T(8,128)S(1)}, u32[]{:S(2)}, u32[]{:S(2)}) collective-permute-start(f32[64,256]{1,0:T(8,128)S(1)} %get-tuple-element.14), channel_id=1, source_target_pairs={{0,2},{1,3},{2,0},{3,1},{4,6},{5,7},{6,4},{7,5},{8,10},{9,11},{10,... | collective-permute-start | bytes 196616 | tf_op jit(solution)/shard_map/ppermute | solution.py:309
  4.1 5.6 %collective-permute-start.2 = (f32[64,256]{1,0:T(8,128)S(1)}, f32[64,256]{1,0:T(8,128)S(1)}, u32[]{:S(2)}, u32[]{:S(2)}) collective-permute-start(f32[64,256]{1,0:T(8,128)S(1)} %get-tuple-element.11), channel_id=1, source_target_pairs={{0,3},{1,2},{2,1},{3,0},{4,7},{5,6},{6,5},{7,4},{8,11},{9,10},{10,... | collective-permute-start | bytes 196616 | tf_op jit(solution)/shard_map/ppermute | solution.py:309
  5.1 1.1 %copy-start = (f32[3,256,256]{2,1,0:T(8,128)S(1)}, f32[3,256,256]{2,1,0:T(8,128)}, u32[]{:S(2)}) copy-start(f32[3,256,256]{2,1,0:T(8,128)} %pre_ref.3) | copy-start | bytes 2359300
  6.2 0.9 %copy-start.2 = (f32[256,256]{1,0:T(8,128)S(1)}, f32[256,256]{1,0:T(8,128)}, u32[]{:S(2)}) copy-start(f32[256,256]{1,0:T(8,128)} %raw_ref.1) | copy-start | bytes 786436
  7.2 0.7 copy-start.14
  9.8 46.5 %copy-start.3 = (bf16[256,256]{1,0:T(8,128)(2,1)S(1)}, bf16[256,256]{1,0:T(8,128)(2,1)}, u32[]{:S(2)}) copy-start(bf16[256,256]{1,0:T(8,128)(2,1)} %constant.53.clone.inner_h) | copy-start | bytes 393220
  9.9 46.5 %copy-start.4 = (bf16[256,256]{1,0:T(8,128)(2,1)S(1)}, bf16[256,256]{1,0:T(8,128)(2,1)}, u32[]{:S(2)}) copy-start(bf16[256,256]{1,0:T(8,128)(2,1)} %constant.54.clone.inner_l) | copy-start | bytes 393220
  9.9 46.5 %copy-start.5 = (bf16[256,256]{1,0:T(8,128)(2,1)S(1)}, bf16[256,256]{1,0:T(8,128)(2,1)}, u32[]{:S(2)}) copy-start(bf16[256,256]{1,0:T(8,128)(2,1)} %constant.55.clone.back_h) | copy-start | bytes 393220
  9.9 46.5 %copy-start.6 = (bf16[256,256]{1,0:T(8,128)(2,1)S(1)}, bf16[256,256]{1,0:T(8,128)(2,1)}, u32[]{:S(2)}) copy-start(bf16[256,256]{1,0:T(8,128)(2,1)} %constant.56.clone.back_l) | copy-start | bytes 393220
  9.9 46.5 %copy-start.7 = (bf16[256,128]{1,0:T(8,128)(2,1)S(1)}, bf16[256,128]{1,0:T(8,128)(2,1)}, u32[]{:S(2)}) copy-start(bf16[256,128]{1,0:T(8,128)(2,1)} %constant.51.clone.outer_h) | copy-start | bytes 196612
  9.9 46.5 %copy-start.8 = (bf16[256,128]{1,0:T(8,128)(2,1)S(1)}, bf16[256,128]{1,0:T(8,128)(2,1)}, u32[]{:S(2)}) copy-start(bf16[256,128]{1,0:T(8,128)(2,1)} %constant.52.clone.outer_l) | copy-start | bytes 196612
  9.9 46.5 %copy-start.9 = (bf16[128,256]{1,0:T(8,128)(2,1)S(1)}, bf16[128,256]{1,0:T(8,128)(2,1)}, u32[]{:S(2)}) copy-start(bf16[128,256]{1,0:T(8,128)(2,1)} %constant.57.clone.last_h) | copy-start | bytes 196612
  9.9 46.5 %copy-start.10 = (bf16[128,256]{1,0:T(8,128)(2,1)S(1)}, bf16[128,256]{1,0:T(8,128)(2,1)}, u32[]{:S(2)}) copy-start(bf16[128,256]{1,0:T(8,128)(2,1)} %constant.58.clone.last_l) | copy-start | bytes 196612
  9.9 46.5 %copy-start.11 = (f32[128,128]{1,0:T(8,128)S(1)}, f32[128,128]{1,0:T(8,128)}, u32[]{:S(2)}) copy-start(f32[128,128]{1,0:T(8,128)} %constant.59.clone.cos_ref) | copy-start | bytes 196612
  10.0 46.5 %copy-start.12 = (f32[128,128]{1,0:T(8,128)S(1)}, f32[128,128]{1,0:T(8,128)}, u32[]{:S(2)}) copy-start(f32[128,128]{1,0:T(8,128)} %constant.60.clone.sin_ref) | copy-start | bytes 196612
  10.0 46.5 %copy-start.13 = (f32[3,3,256]{2,1,0:T(4,128)S(1)}, f32[3,3,256]{2,1,0:T(4,128)}, u32[]{:S(2)}) copy-start(f32[3,3,256]{2,1,0:T(4,128)} %taps_ref.3) | copy-start | bytes 27652
  60.9 7.4 %copy-start.1 = (f32[3,256,256]{2,1,0:T(8,128)S(1)}, f32[3,256,256]{2,1,0:T(8,128)}, u32[]{:S(2)}) copy-start(f32[3,256,256]{2,1,0:T(8,128)} %pre_ref.3) | copy-start | bytes 2359300
  60.9 29.7 %all-to-all-start.1 = ((f32[64,25,1,128]{3,2,1,0:T(1,128)}), f32[64,25,1,128]{3,2,1,0:T(1,128)S(1)}, u32[]{:S(2)}, u32[]{:S(2)}) async-start(f32[64,25,1,128]{3,2,1,0:T(1,128)} %bitcast.9), calls=%async_computation.1 | async-start | bytes 1638400 | tf_op jit(solution)/shard_map/all_to_all | solution.py:324

commit v5 on v4

--- a/solution.py
+++ b/solution.py
@@ -7,10 +7,8 @@
 from jax import lax
 from jax.experimental import pallas as pl
 from jax.experimental.pallas import tpu as pltpu
-from jax.sharding import Mesh
 from jax.sharding import PartitionSpec as P
 
-CTX = ("x", "z", "y")
 PEERS = 64
 SIDE = 128
 CH = 4
@@ -33,7 +31,7 @@
 def make_tables():
     length = SIDE * SIDE
     row = np.arange(SIDE)
-    token_row = HALVES * (row % PEERS) + row // PEERS
+    token_row = HALVES * (PEERS - 1 - row % PEERS) + row // PEERS
     freq = np.arange(SIDE) + 0.25
     outer = 2.0 * np.pi * freq[:, None] * token_row[None, :] / SIDE
     outer_table = np.concatenate([np.cos(outer), np.sin(outer)], axis=0)
@@ -136,12 +134,17 @@
         )
 
 
-def gate_body(at_ref, own_ref, one_ref, two_ref, three_ref, partial_ref, send_ref, rows_ref):
+def gate_body(at_ref, own_ref, one_ref, two_ref, three_ref, partial_ref, send_ref, rows_ref, block_ref, done):
     count = own_ref.shape[0]
     for d, ref in enumerate((own_ref, one_ref, two_ref, three_ref)):
         base = pl.multiple_of((at_ref[0] ^ d) * count, count)
         rows_ref[pl.ds(base, count), :] = ref[...]
-    put_rows(send_ref, 4, SENT, rows_ref[...].T)
+    put_rows(block_ref, 0, HALVES * CH, rows_ref[...].T)
+    move = pltpu.make_async_copy(
+        block_ref.reshape(PEERS, HALVES * CH, SIDE), send_ref.at[:, SENT - HALVES * CH :, :], done
+    )
+    move.start()
+    move.wait()
 
 
 def spectrum(signals, outer_h, outer_l, inner_h, inner_l, cos_t, sin_t):
@@ -173,12 +176,12 @@
     for c in range(CH):
         for i in range(3):
             tap = jnp.sum(
-                jnp.where(lane_t == c * PEERS + place_ref[0], taps_ref[i], 0.0), axis=1, keepdims=True
+                jnp.where(lane_t == c * PEERS + PEERS - 1 - place_ref[0], taps_ref[i], 0.0), axis=1, keepdims=True
             )
             value = channel_of(recv_ref, 1 + i, c, SENT)
             low, high = value[:PEERS], value[PEERS:]
             carry = jnp.concatenate(
-                [jnp.where(row_h == 0, 0.0, pltpu.roll(high, 1, axis=0)), low], axis=0
+                [jnp.where(row_h == PEERS - 1, 0.0, pltpu.roll(high, PEERS - 1, axis=0)), low], axis=0
             )
             one = pltpu.roll(jnp.where(lane >= SIDE - 1, carry, value), 1, axis=1)
             two = pltpu.roll(jnp.where(lane >= SIDE - 2, carry, value), 2, axis=1)
@@ -228,7 +231,7 @@
             for c in range(CH):
                 after = placed(grad[:PEERS, lanes_of(c)], AFTER + 2 * (i * CH + c), after)
     totals = jnp.sum(sums_ref[...].T, axis=0, keepdims=True) * (1.0 / SIDE)
-    after = jnp.where(row_h == PEERS - 1, 0.0, pltpu.roll(after, PEERS - 1, axis=0))
+    after = jnp.where(row_h == 0, 0.0, pltpu.roll(after, 1, axis=0))
     ret_ref[rows_of(EXTRA_ROW, BACK), :] = jnp.where(
         lane_h < AFTER, jnp.broadcast_to(totals, (PEERS, SIDE)), jnp.where(lane_h < FIRST, after, edges)
     )
@@ -273,7 +276,7 @@
         )
 
 
-def call(body, outs, scratch, name, place=0, held=True, aliases=None):
+def call(body, outs, scratch, name, place=0, held=True):
     def run(*operands):
         near = [
             value if at < place else pltpu.with_memory_space_constraint(value, pltpu.VMEM)
@@ -288,12 +291,16 @@
             in_specs=[smem] * place + [vmem] * (len(operands) - place),
             out_specs=tuple(vmem for _ in outs),
             scratch_shapes=[pltpu.VMEM(s, jnp.float32) for s in scratch],
-            input_output_aliases=aliases or {},
             compiler_params=pltpu.CompilerParams(vmem_limit_bytes=VMEM_LIMIT),
             name=name,
         )(*near)
 
     return run
+
+
+def exchange(blocks):
+    order = [list(range(PEERS))[::-1]]
+    return lax.all_to_all(blocks, "ctx", 0, 0, tiled=True, axis_index_groups=order)
 
 
 def local(pre, raw_filter, decay, taps, grad_out):
@@ -301,7 +308,7 @@
     wide = CH * SIDE
     tables = [jnp.asarray(t) for t in make_tables()]
     tp_at = lax.axis_index("tp").astype(jnp.int32)
-    place = lax.axis_index(CTX).astype(jnp.int32).reshape(1)
+    place = lax.axis_index("ctx").astype(jnp.int32).reshape(1)
     turned = grad_out.T
     pieces = []
     for d in range(4):
@@ -310,10 +317,27 @@
     partial, env = call(pack_body, ((PEERS * SENT, SIDE), (chans, tok)), [(SIDE, chans)], "pack", 1)(
         place, pre, raw_filter, decay.reshape(1, chans)
     )
-    (send,) = call(gate_body, ((PEERS * SENT, SIDE),), [(tok, chans)], "gate", 1, aliases={5: 0})(
-        tp_at.reshape(1), *pieces, partial
-    )
-    recv = lax.all_to_all(send.reshape(PEERS, SENT, SIDE), CTX, 0, 0, tiled=True).reshape(PEERS * SENT, SIDE)
+    vmem = pl.BlockSpec(memory_space=pltpu.VMEM)
+    anywhere = pl.BlockSpec(memory_space=pl.ANY)
+    send = pl.pallas_call(
+        gate_body,
+        out_shape=jax.ShapeDtypeStruct((PEERS, SENT, SIDE), jnp.float32),
+        in_specs=[pl.BlockSpec(memory_space=pltpu.SMEM)] + [vmem] * 4 + [anywhere],
+        out_specs=anywhere,
+        scratch_shapes=[
+            pltpu.VMEM((tok, chans), jnp.float32),
+            pltpu.VMEM((PEERS * HALVES * CH, SIDE), jnp.float32),
+            pltpu.SemaphoreType.DMA(()),
+        ],
+        input_output_aliases={5: 0},
+        compiler_params=pltpu.CompilerParams(vmem_limit_bytes=VMEM_LIMIT),
+        name="gate",
+    )(
+        tp_at.reshape(1),
+        *[pltpu.with_memory_space_constraint(piece, pltpu.VMEM) for piece in pieces],
+        partial.reshape(PEERS, SENT, SIDE),
+    )
+    recv = exchange(send).reshape(PEERS * SENT, SIDE)
     (ret,) = call(
         long_body,
         ((PEERS * BACK, SIDE),),
@@ -321,7 +345,7 @@
         "long",
         1,
     )(place, recv, taps, *tables)
-    back = lax.all_to_all(ret.reshape(PEERS, BACK, 1, SIDE), CTX, 0, 0, tiled=True).reshape(PEERS * BACK, SIDE)
+    back = exchange(ret.reshape(PEERS, BACK, 1, SIDE)).reshape(PEERS * BACK, SIDE)
     pair, cols = call(prepare_body, ((2, chans, tok), (chans, SIDE)), [(SIDE, chans)], "prepare")(pre, taps)
     return call(
         finish_body, ((3, chans, tok), (chans, tok), (3, 3, chans)), [(SIDE, SIDE)], "finish", held=False
@@ -329,13 +353,12 @@
 
 
 def solution(mesh):
-    split = Mesh(mesh.devices.reshape(4, 8, 2, 4), CTX + ("tp",))
     in_specs = (
-        P(None, "tp", CTX),
-        P("tp", CTX),
+        P(None, "tp", "ctx"),
+        P("tp", "ctx"),
         P("tp"),
         P(None, None, "tp"),
-        P(None, CTX + ("tp",)),
-    )
-    out_specs = (P(None, "tp", CTX), P("tp", CTX), P(None, None, "tp"))
-    return jax.shard_map(local, mesh=split, in_specs=in_specs, out_specs=out_specs, check_vma=False)
+        P(None, ("ctx", "tp")),
+    )
+    out_specs = (P(None, "tp", "ctx"), P("tp", "ctx"), P(None, None, "tp"))
+    return jax.shard_map(local, mesh=mesh, in_specs=in_specs, out_specs=out_specs, check_vma=False)

time: 93.9 us -> 92.2 us (0.982)
  starting transfers between devices: 10.9 us -> 13.9 us
  waiting for transfers between devices: 23.2 us -> 20.9 us
  blocking collectives: 46.4 us -> 44.1 us
    all_to_all x1, starting transfers between devices: 7.43 us -> 10.5 us  [exchange(): lax.all_to_all(blocks, 'ctx', 0, 0, tiled=True, axis_index_groups=order)]
    all_to_all x1, waiting for transfers between devices: 21.6 us -> 19.3 us  [exchange(): lax.all_to_all(blocks, 'ctx', 0, 0, tiled=True, axis_index_groups=order)]
    all_to_all x1, blocking collectives: 46.4 us -> 44.1 us  [exchange(): lax.all_to_all(blocks, 'ctx', 0, 0, tiled=True, axis_index_groups=order)]
    pallas_call x5 -> x4, Pallas kernels: 7.78 us -> 7.65 us  [run(): pl.pallas_call(body, out_shape=tuple((kind(s, jnp.float32) for s in outs)...]
where the time goes in v5:
time: 92.2 us; the launch traced here: 91.4 us
  blocking collectives  44.1 us (48%)
  waiting for transfers between devices  20.9 us (23%)
  starting transfers between devices  13.9 us (15%)
  Pallas kernels  7.84 us (9%)
  local copies, waits for them, and re-layouts  3.8 us (4%)
    all_to_all x1, blocking collectives, exchange(): lax.all_to_all(blocks, 'ctx', 0, 0, tiled=True, axis_index_groups=order)  44.1 us
    all_to_all x1, waiting for transfers between devices, exchange(): lax.all_to_all(blocks, 'ctx', 0, 0, tiled=True, axis_index_groups=order)  19.3 us
    all_to_all x1, starting transfers between devices, exchange(): lax.all_to_all(blocks, 'ctx', 0, 0, tiled=True, axis_index_groups=order)  10.5 us
    pallas_call x4, Pallas kernels, run(): pl.pallas_call(body, out_shape=tuple((kind(s, jnp.float32) for s in outs)...  7.65 us
    ppermute x3, starting transfers between devices, local(): lax.ppermute(piece, 'tp', [(k, k ^ d) for k in range(4)])  3.44 us
    unnamed x30, local copies, waits for them, and re-layouts  2.84 us
  transfers between devices with their start and end apart: 4, of which 2 were waited for; matrix products, arithmetic and copies ran while one was open for 0% of the time, Pallas kernels for 1%

profile of v5, /device:TPU:8, one launch (start us, length us, event | category | flops | bytes accessed | tf_op | source)
XLA Modules:
  0.0 91.4 jit_solution(6857362913508202813)
XLA Ops:
  0.7 1.0 %dynamic-slice_bitcast_fusion = (f32[64,256]{1,0:T(8,128)S(1)}, f32[64,256]{1,0:T(8,128)S(1)}, f32[64,256]{1,0:T(8,128)S(1)}, f32[64,256]{1,0:T(8,128)S(1)}) fusion(f32[1024,64]{0,1:T(8,128)} %param.19, s32[]{:T(128)S(6)} %select_n.15, s32[]{:T(128)S(6)} %select_n.13, s32[]{:T(128)S(6)} %select_n.12, s32[]{:T(128)S(6)} %select_n.14), kind=kLoop, calls=%fused_computation | loop fusion | bytes 524304 | tf_op jit(solution)/shard_map/dynamic_slice | solution.py:315
  1.6 0.1 collective-permute-start
  1.7 2.4 %collective-permute-start.1 = (f32[64,256]{1,0:T(8,128)S(1)}, f32[64,256]{1,0:T(8,128)S(1)}, u32[]{:S(2)}, u32[]{:S(2)}) collective-permute-start(f32[64,256]{1,0:T(8,128)S(1)} %get-tuple-element.14), channel_id=1, source_target_pairs={{0,2},{1,3},{2,0},{3,1},{4,6},{5,7},{6,4},{7,5},{8,10},{9,11},{10,... | collective-permute-start | bytes 196616 | tf_op jit(solution)/shard_map/ppermute | solution.py:316
  4.1 1.0 %collective-permute-start.2 = (f32[64,256]{1,0:T(8,128)S(1)}, f32[64,256]{1,0:T(8,128)S(1)}, u32[]{:S(2)}, u32[]{:S(2)}) collective-permute-start(f32[64,256]{1,0:T(8,128)S(1)} %get-tuple-element.11), channel_id=1, source_target_pairs={{0,3},{1,2},{2,1},{3,0},{4,7},{5,6},{6,5},{7,4},{8,11},{9,10},{10,... | collective-permute-start | bytes 196616 | tf_op jit(solution)/shard_map/ppermute | solution.py:316
  5.1 1.1 %copy-done = f32[3,256,256]{2,1,0:T(8,128)S(1)} copy-done((f32[3,256,256]{2,1,0:T(8,128)S(1)}, f32[3,256,256]{2,1,0:T(8,128)}, u32[]{:S(2)}) %copy-start) | copy-done | bytes 786456
  6.2 0.9 %copy-done.2 = f32[256,256]{1,0:T(8,128)S(1)} copy-done((f32[256,256]{1,0:T(8,128)S(1)}, f32[256,256]{1,0:T(8,128)}, u32[]{:S(2)}) %copy-start.2) | copy-done | bytes 262168
  7.2 0.7 copy-done.14
  7.8 0.3 pack.1
  8.1 1.6 %collective-permute-done.2.three_ref = f32[64,256]{1,0:T(8,128)S(1)} collective-permute-done((f32[64,256]{1,0:T(8,128)S(1)}, f32[64,256]{1,0:T(8,128)S(1)}, u32[]{:S(2)}, u32[]{:S(2)}) %collective-permute-start.2) | collective-permute-done | bytes 65568 | tf_op jit(solution)/shard_map/ppermute | solution.py:316
  9.7 0.2 gate.1
  9.9 0.0 copy-start.3
  9.9 0.0 copy-start.4
  9.9 0.0 copy-start.6
  9.9 0.0 copy-start.7
  9.9 0.0 copy-start.8
  10.0 0.0 copy-start.9
  10.0 0.0 copy-start.10
  10.0 0.0 copy-start.11
  10.0 44.1 %all_to_all.10 = f32[64,40,128]{2,1,0:T(8,128)S(1)} all-to-all(f32[64,40,128]{2,1,0:T(8,128)S(1)} %gate.1), channel_id=1, replica_groups={{252,248,244,240,236,232,228,224,220,216,212,208,204,200,196,192,188,18..., dimensions={0} | all-to-all | bytes 2621440 | tf_op jit(solution)/shard_map/all_to_all | solution.py:303
  54.2 4.5 %long.1 = f32[1600,128]{1,0:T(8,128)} custom-call(s32[1]{0:T(128)} %bitcast.place_ref, f32[2560,128]{1,0:T(8,128)S(1)} %bitcast.16, f32[3,3,256]{2,1,0:T(4,128)S(1)} %copy-done.13, bf16[256,128]{1,0:T(8,128)(2,1)S(1)} %copy-done.7, bf16[256,128]{1,0:T(8,128)(2,1)S(1)} %copy-done.8, bf16[256,256]{1,0:T(8,128)(2,1)S(1)} %copy-done.3, ...), custom_call_target="tpu_custom_call" | custom-call | tf_op jit(solution)/shard_map/long/pallas_call | solution.py:288
  58.7 10.5 %all-to-all-start.1 = ((f32[64,25,1,128]{3,2,1,0:T(1,128)}), f32[64,25,1,128]{3,2,1,0:T(1,128)S(1)}, u32[]{:S(2)}, u32[]{:S(2)}) async-start(f32[64,25,1,128]{3,2,1,0:T(1,128)} %bitcast.9), calls=%async_computation.1 | async-start | bytes 1638400 | tf_op jit(solution)/shard_map/all_to_all | solution.py:303
  69.2 0.6 prepare.1
  69.9 19.3 %all-to-all-done.1 = f32[64,25,1,128]{3,2,1,0:T(1,128)S(1)} async-done(((f32[64,25,1,128]{3,2,1,0:T(1,128)}), f32[64,25,1,128]{3,2,1,0:T(1,128)S(1)}, u32[]{:S(2)}, u32[]{:S(2)}) %all-to-all-start.1) | async-done | bytes 819232 | tf_op jit(solution)/shard_map/all_to_all | solution.py:303
  89.2 2.2 %finish.1 = (f32[3,256,256]{2,1,0:T(8,128)}, f32[256,256]{1,0:T(8,128)}, f32[3,3,256]{2,1,0:T(4,128)}) custom-call(f32[1600,128]{1,0:T(8,128)S(1)} %bitcast.17, f32[2,256,256]{2,1,0:T(8,128)S(1)} %get-tuple-element.8.pair_ref, f32[256,128]{1,0:T(8,128)S(1)} %get-tuple-element.9.cols_in_ref, f32[256,256]{1,0:T(8,128)S(1)} %get-tuple-element.10.env_ref), custom_call_target="tpu_custom_call" | custom-call | tf_op jit(solution)/shard_map/finish/pallas_call | solution.py:288
  (21 shorter events, 0.1 us)
Async XLA Ops:
  1.6 6.5 %collective-permute-start = (f32[64,256]{1,0:T(8,128)S(1)}, f32[64,256]{1,0:T(8,128)S(1)}, u32[]{:S(2)}, u32[]{:S(2)}) collective-permute-start(f32[64,256]{1,0:T(8,128)S(1)} %get-tuple-element.12), channel_id=1, source_target_pairs={{0,1},{1,0},{2,3},{3,2},{4,5},{5,4},{6,7},{7,6},{8,9},{9,8},{10,11... | collective-permute-start | bytes 196616 | tf_op jit(solution)/shard_map/ppermute | solution.py:316
  1.7 6.4 %collective-permute-start.1 = (f32[64,256]{1,0:T(8,128)S(1)}, f32[64,256]{1,0:T(8,128)S(1)}, u32[]{:S(2)}, u32[]{:S(2)}) collective-permute-start(f32[64,256]{1,0:T(8,128)S(1)} %get-tuple-element.14), channel_id=1, source_target_pairs={{0,2},{1,3},{2,0},{3,1},{4,6},{5,7},{6,4},{7,5},{8,10},{9,11},{10,... | collective-permute-start | bytes 196616 | tf_op jit(solution)/shard_map/ppermute | solution.py:316
  4.1 5.6 %collective-permute-start.2 = (f32[64,256]{1,0:T(8,128)S(1)}, f32[64,256]{1,0:T(8,128)S(1)}, u32[]{:S(2)}, u32[]{:S(2)}) collective-permute-start(f32[64,256]{1,0:T(8,128)S(1)} %get-tuple-element.11), channel_id=1, source_target_pairs={{0,3},{1,2},{2,1},{3,0},{4,7},{5,6},{6,5},{7,4},{8,11},{9,10},{10,... | collective-permute-start | bytes 196616 | tf_op jit(solution)/shard_map/ppermute | solution.py:316
  5.1 1.1 %copy-start = (f32[3,256,256]{2,1,0:T(8,128)S(1)}, f32[3,256,256]{2,1,0:T(8,128)}, u32[]{:S(2)}) copy-start(f32[3,256,256]{2,1,0:T(8,128)} %pre_ref.3) | copy-start | bytes 2359300
  6.2 0.9 %copy-start.2 = (f32[256,256]{1,0:T(8,128)S(1)}, f32[256,256]{1,0:T(8,128)}, u32[]{:S(2)}) copy-start(f32[256,256]{1,0:T(8,128)} %raw_ref.1) | copy-start | bytes 786436
  7.2 0.7 copy-start.14
  9.9 44.2 %copy-start.3 = (bf16[256,256]{1,0:T(8,128)(2,1)S(1)}, bf16[256,256]{1,0:T(8,128)(2,1)}, u32[]{:S(2)}) copy-start(bf16[256,256]{1,0:T(8,128)(2,1)} %constant.43.clone.inner_h) | copy-start | bytes 393220
  9.9 44.2 %copy-start.4 = (bf16[256,256]{1,0:T(8,128)(2,1)S(1)}, bf16[256,256]{1,0:T(8,128)(2,1)}, u32[]{:S(2)}) copy-start(bf16[256,256]{1,0:T(8,128)(2,1)} %constant.44.clone.inner_l) | copy-start | bytes 393220
  9.9 44.2 %copy-start.5 = (bf16[256,256]{1,0:T(8,128)(2,1)S(1)}, bf16[256,256]{1,0:T(8,128)(2,1)}, u32[]{:S(2)}) copy-start(bf16[256,256]{1,0:T(8,128)(2,1)} %constant.45.clone.back_h) | copy-start | bytes 393220
  9.9 44.2 %copy-start.6 = (bf16[256,256]{1,0:T(8,128)(2,1)S(1)}, bf16[256,256]{1,0:T(8,128)(2,1)}, u32[]{:S(2)}) copy-start(bf16[256,256]{1,0:T(8,128)(2,1)} %constant.46.clone.back_l) | copy-start | bytes 393220
  9.9 44.2 %copy-start.7 = (bf16[256,128]{1,0:T(8,128)(2,1)S(1)}, bf16[256,128]{1,0:T(8,128)(2,1)}, u32[]{:S(2)}) copy-start(bf16[256,128]{1,0:T(8,128)(2,1)} %constant.41.clone.outer_h) | copy-start | bytes 196612
  9.9 44.2 %copy-start.8 = (bf16[256,128]{1,0:T(8,128)(2,1)S(1)}, bf16[256,128]{1,0:T(8,128)(2,1)}, u32[]{:S(2)}) copy-start(bf16[256,128]{1,0:T(8,128)(2,1)} %constant.42.clone.outer_l) | copy-start | bytes 196612
  10.0 44.2 %copy-start.9 = (bf16[128,256]{1,0:T(8,128)(2,1)S(1)}, bf16[128,256]{1,0:T(8,128)(2,1)}, u32[]{:S(2)}) copy-start(bf16[128,256]{1,0:T(8,128)(2,1)} %constant.47.clone.last_h) | copy-start | bytes 196612
  10.0 44.2 %copy-start.10 = (bf16[128,256]{1,0:T(8,128)(2,1)S(1)}, bf16[128,256]{1,0:T(8,128)(2,1)}, u32[]{:S(2)}) copy-start(bf16[128,256]{1,0:T(8,128)(2,1)} %constant.48.clone.last_l) | copy-start | bytes 196612
  10.0 44.2 %copy-start.11 = (f32[128,128]{1,0:T(8,128)S(1)}, f32[128,128]{1,0:T(8,128)}, u32[]{:S(2)}) copy-start(f32[128,128]{1,0:T(8,128)} %constant.49.clone.cos_ref) | copy-start | bytes 196612
  10.0 44.2 %copy-start.12 = (f32[128,128]{1,0:T(8,128)S(1)}, f32[128,128]{1,0:T(8,128)}, u32[]{:S(2)}) copy-start(f32[128,128]{1,0:T(8,128)} %constant.50.clone.sin_ref) | copy-start | bytes 196612
  10.0 44.2 %copy-start.13 = (f32[3,3,256]{2,1,0:T(4,128)S(1)}, f32[3,3,256]{2,1,0:T(4,128)}, u32[]{:S(2)}) copy-start(f32[3,3,256]{2,1,0:T(4,128)} %taps_ref.3) | copy-start | bytes 27652
  58.7 10.5 %copy-start.1 = (f32[3,256,256]{2,1,0:T(8,128)S(1)}, f32[3,256,256]{2,1,0:T(8,128)}, u32[]{:S(2)}) copy-start(f32[3,256,256]{2,1,0:T(8,128)} %pre_ref.3) | copy-start | bytes 2359300
  58.7 30.5 %all-to-all-start.1 = ((f32[64,25,1,128]{3,2,1,0:T(1,128)}), f32[64,25,1,128]{3,2,1,0:T(1,128)S(1)}, u32[]{:S(2)}, u32[]{:S(2)}) async-start(f32[64,25,1,128]{3,2,1,0:T(1,128)} %bitcast.9), calls=%async_computation.1 | async-start | bytes 1638400 | tf_op jit(solution)/shard_map/all_to_all | solution.py:303

commit v6 on v5

--- a/solution.py
+++ b/solution.py
@@ -16,6 +16,8 @@
 SENT = 40
 BACK = 25
 EXTRA_ROW = 24
+XS, ZS, YS = 4, 8, 2
+ORDER = [x * ZS * YS + z * YS + y for z in range(ZS) for y in range(YS) for x in range(XS)][::-1]
 GROUP = 16
 AFTER = 64
 FIRST = 88
@@ -31,7 +33,7 @@
 def make_tables():
     length = SIDE * SIDE
     row = np.arange(SIDE)
-    token_row = HALVES * (PEERS - 1 - row % PEERS) + row // PEERS
+    token_row = HALVES * np.array(ORDER)[row % PEERS] + row // PEERS
     freq = np.arange(SIDE) + 0.25
     outer = 2.0 * np.pi * freq[:, None] * token_row[None, :] / SIDE
     outer_table = np.concatenate([np.cos(outer), np.sin(outer)], axis=0)
@@ -147,6 +149,22 @@
     move.wait()
 
 
+def earlier(value):
+    at = row_index(value.shape)
+    moved = jnp.where(
+        at >= PEERS - XS,
+        pltpu.roll(value, PEERS - XS - 1, axis=0),
+        pltpu.roll(value, PEERS - XS, axis=0),
+    )
+    return jnp.where(at == PEERS - 1, 0.0, moved)
+
+
+def later(value):
+    at = row_index(value.shape)
+    moved = jnp.where(at < XS, pltpu.roll(value, XS + 1, axis=0), pltpu.roll(value, XS, axis=0))
+    return jnp.where(at == 0, 0.0, moved)
+
+
 def spectrum(signals, outer_h, outer_l, inner_h, inner_l, cos_t, sin_t):
     wide = product_left(outer_h, outer_l, signals)
     turned = []
@@ -165,6 +183,8 @@
     row_h = row_index((PEERS, SIDE))
     lane_h = lane_index((PEERS, SIDE))
     lane_t = lane_index(taps_ref.shape[1:])
+    here = place_ref[0]
+    slot = PEERS - 1 - ((here // YS) % ZS * YS * XS + here % YS * XS + here // (ZS * YS))
 
     def placed(value, at, into):
         moved = pltpu.roll(value, at, axis=1)
@@ -176,12 +196,12 @@
     for c in range(CH):
         for i in range(3):
             tap = jnp.sum(
-                jnp.where(lane_t == c * PEERS + PEERS - 1 - place_ref[0], taps_ref[i], 0.0), axis=1, keepdims=True
+                jnp.where(lane_t == c * PEERS + slot, taps_ref[i], 0.0), axis=1, keepdims=True
             )
             value = channel_of(recv_ref, 1 + i, c, SENT)
             low, high = value[:PEERS], value[PEERS:]
             carry = jnp.concatenate(
-                [jnp.where(row_h == PEERS - 1, 0.0, pltpu.roll(high, PEERS - 1, axis=0)), low], axis=0
+                [earlier(high), low], axis=0
             )
             one = pltpu.roll(jnp.where(lane >= SIDE - 1, carry, value), 1, axis=1)
             two = pltpu.roll(jnp.where(lane >= SIDE - 2, carry, value), 2, axis=1)
@@ -231,7 +251,7 @@
             for c in range(CH):
                 after = placed(grad[:PEERS, lanes_of(c)], AFTER + 2 * (i * CH + c), after)
     totals = jnp.sum(sums_ref[...].T, axis=0, keepdims=True) * (1.0 / SIDE)
-    after = jnp.where(row_h == 0, 0.0, pltpu.roll(after, 1, axis=0))
+    after = later(after)
     ret_ref[rows_of(EXTRA_ROW, BACK), :] = jnp.where(
         lane_h < AFTER, jnp.broadcast_to(totals, (PEERS, SIDE)), jnp.where(lane_h < FIRST, after, edges)
     )
@@ -299,8 +319,7 @@
 
 
 def exchange(blocks):
-    order = [list(range(PEERS))[::-1]]
-    return lax.all_to_all(blocks, "ctx", 0, 0, tiled=True, axis_index_groups=order)
+    return lax.all_to_all(blocks, "ctx", 0, 0, tiled=True, axis_index_groups=[ORDER])
 
 
 def local(pre, raw_filter, decay, taps, grad_out):

time: 92.2 us -> 91.7 us (level)
  waiting for transfers between devices: 20.9 us -> 19.9 us
    all_to_all x1, waiting for transfers between devices: 19.3 us -> 18.4 us  [exchange(): lax.all_to_all(blocks, 'ctx', 0, 0, tiled=True, axis_index_groups=[ORDER])]
where the time goes in v6:
time: 91.7 us; the launch traced here: 90.3 us
  blocking collectives  43.9 us (48%)
  waiting for transfers between devices  19.9 us (22%)
  starting transfers between devices  14 us (15%)
  Pallas kernels  7.84 us (9%)
  local copies, waits for them, and re-layouts  3.8 us (4%)
    all_to_all x1, blocking collectives, exchange(): lax.all_to_all(blocks, 'ctx', 0, 0, tiled=True, axis_index_groups=[ORDER])  43.9 us
    all_to_all x1, waiting for transfers between devices, exchange(): lax.all_to_all(blocks, 'ctx', 0, 0, tiled=True, axis_index_groups=[ORDER])  18.4 us
    all_to_all x1, starting transfers between devices, exchange(): lax.all_to_all(blocks, 'ctx', 0, 0, tiled=True, axis_index_groups=[ORDER])  10.6 us
    pallas_call x4, Pallas kernels, run(): pl.pallas_call(body, out_shape=tuple((kind(s, jnp.float32) for s in outs)...  7.66 us
    ppermute x3, starting transfers between devices, local(): lax.ppermute(piece, 'tp', [(k, k ^ d) for k in range(4)])  3.44 us
    unnamed x30, local copies, waits for them, and re-layouts  2.84 us
  transfers between devices with their start and end apart: 4, of which 2 were waited for; matrix products, arithmetic and copies ran while one was open for 0% of the time, Pallas kernels for 1%

profile of v6, /device:TPU:8, one launch (start us, length us, event | category | flops | bytes accessed | tf_op | source)
XLA Modules:
  0.0 90.3 jit_solution(8419657224089873796)
XLA Ops:
  0.7 1.0 %dynamic-slice_bitcast_fusion = (f32[64,256]{1,0:T(8,128)S(1)}, f32[64,256]{1,0:T(8,128)S(1)}, f32[64,256]{1,0:T(8,128)S(1)}, f32[64,256]{1,0:T(8,128)S(1)}) fusion(f32[1024,64]{0,1:T(8,128)} %param.19, s32[]{:T(128)S(6)} %select_n.15, s32[]{:T(128)S(6)} %select_n.13, s32[]{:T(128)S(6)} %select_n.12, s32[]{:T(128)S(6)} %select_n.14), kind=kLoop, calls=%fused_computation | loop fusion | bytes 524304 | tf_op jit(solution)/shard_map/dynamic_slice | solution.py:334
  1.6 0.1 collective-permute-start
  1.7 2.4 %collective-permute-start.1 = (f32[64,256]{1,0:T(8,128)S(1)}, f32[64,256]{1,0:T(8,128)S(1)}, u32[]{:S(2)}, u32[]{:S(2)}) collective-permute-start(f32[64,256]{1,0:T(8,128)S(1)} %get-tuple-element.14), channel_id=1, source_target_pairs={{0,2},{1,3},{2,0},{3,1},{4,6},{5,7},{6,4},{7,5},{8,10},{9,11},{10,... | collective-permute-start | bytes 196616 | tf_op jit(solution)/shard_map/ppermute | solution.py:335
  4.1 1.0 %collective-permute-start.2 = (f32[64,256]{1,0:T(8,128)S(1)}, f32[64,256]{1,0:T(8,128)S(1)}, u32[]{:S(2)}, u32[]{:S(2)}) collective-permute-start(f32[64,256]{1,0:T(8,128)S(1)} %get-tuple-element.11), channel_id=1, source_target_pairs={{0,3},{1,2},{2,1},{3,0},{4,7},{5,6},{6,5},{7,4},{8,11},{9,10},{10,... | collective-permute-start | bytes 196616 | tf_op jit(solution)/shard_map/ppermute | solution.py:335
  5.1 1.1 %copy-done = f32[3,256,256]{2,1,0:T(8,128)S(1)} copy-done((f32[3,256,256]{2,1,0:T(8,128)S(1)}, f32[3,256,256]{2,1,0:T(8,128)}, u32[]{:S(2)}) %copy-start) | copy-done | bytes 786456
  6.2 0.9 %copy-done.2 = f32[256,256]{1,0:T(8,128)S(1)} copy-done((f32[256,256]{1,0:T(8,128)S(1)}, f32[256,256]{1,0:T(8,128)}, u32[]{:S(2)}) %copy-start.2) | copy-done | bytes 262168
  7.2 0.7 copy-done.14
  7.8 0.3 pack.1
  8.1 1.6 %collective-permute-done.2.three_ref = f32[64,256]{1,0:T(8,128)S(1)} collective-permute-done((f32[64,256]{1,0:T(8,128)S(1)}, f32[64,256]{1,0:T(8,128)S(1)}, u32[]{:S(2)}, u32[]{:S(2)}) %collective-permute-start.2) | collective-permute-done | bytes 65568 | tf_op jit(solution)/shard_map/ppermute | solution.py:335
  9.7 0.2 gate.1
  9.9 0.0 copy-start.3
  9.9 0.0 copy-start.4
  9.9 0.0 copy-start.5
  9.9 0.0 copy-start.7
  9.9 0.0 copy-start.8
  10.0 0.0 copy-start.9
  10.0 0.0 copy-start.10
  10.0 0.0 copy-start.11
  10.0 43.9 %all_to_all.10 = f32[64,40,128]{2,1,0:T(8,128)S(1)} all-to-all(f32[64,40,128]{2,1,0:T(8,128)S(1)} %gate.1), channel_id=1, replica_groups={{252,188,124,60,248,184,120,56,244,180,116,52,240,176,112,48,236,172,10..., dimensions={0} | all-to-all | bytes 2621440 | tf_op jit(solution)/shard_map/all_to_all | solution.py:322
  54.0 4.5 %long.1 = f32[1600,128]{1,0:T(8,128)} custom-call(s32[1]{0:T(128)} %bitcast.place_ref, f32[2560,128]{1,0:T(8,128)S(1)} %bitcast.16, f32[3,3,256]{2,1,0:T(4,128)S(1)} %copy-done.13, bf16[256,128]{1,0:T(8,128)(2,1)S(1)} %copy-done.7, bf16[256,128]{1,0:T(8,128)(2,1)S(1)} %copy-done.8, bf16[256,256]{1,0:T(8,128)(2,1)S(1)} %copy-done.3, ...), custom_call_target="tpu_custom_call" | custom-call | tf_op jit(solution)/shard_map/long/pallas_call | solution.py:308
  58.5 10.6 %all-to-all-start.1 = ((f32[64,25,1,128]{3,2,1,0:T(1,128)}), f32[64,25,1,128]{3,2,1,0:T(1,128)S(1)}, u32[]{:S(2)}, u32[]{:S(2)}) async-start(f32[64,25,1,128]{3,2,1,0:T(1,128)} %bitcast.9), calls=%async_computation.1 | async-start | bytes 1638400 | tf_op jit(solution)/shard_map/all_to_all | solution.py:322
  69.1 0.6 prepare.1
  69.7 18.4 %all-to-all-done.1 = f32[64,25,1,128]{3,2,1,0:T(1,128)S(1)} async-done(((f32[64,25,1,128]{3,2,1,0:T(1,128)}), f32[64,25,1,128]{3,2,1,0:T(1,128)S(1)}, u32[]{:S(2)}, u32[]{:S(2)}) %all-to-all-start.1) | async-done | bytes 819232 | tf_op jit(solution)/shard_map/all_to_all | solution.py:322
  88.1 2.2 %finish.1 = (f32[3,256,256]{2,1,0:T(8,128)}, f32[256,256]{1,0:T(8,128)}, f32[3,3,256]{2,1,0:T(4,128)}) custom-call(f32[1600,128]{1,0:T(8,128)S(1)} %bitcast.17, f32[2,256,256]{2,1,0:T(8,128)S(1)} %get-tuple-element.8.pair_ref, f32[256,128]{1,0:T(8,128)S(1)} %get-tuple-element.9.cols_in_ref, f32[256,256]{1,0:T(8,128)S(1)} %get-tuple-element.10.env_ref), custom_call_target="tpu_custom_call" | custom-call | tf_op jit(solution)/shard_map/finish/pallas_call | solution.py:308
  (21 shorter events, 0.1 us)
Async XLA Ops:
  1.6 6.5 %collective-permute-start = (f32[64,256]{1,0:T(8,128)S(1)}, f32[64,256]{1,0:T(8,128)S(1)}, u32[]{:S(2)}, u32[]{:S(2)}) collective-permute-start(f32[64,256]{1,0:T(8,128)S(1)} %get-tuple-element.12), channel_id=1, source_target_pairs={{0,1},{1,0},{2,3},{3,2},{4,5},{5,4},{6,7},{7,6},{8,9},{9,8},{10,11... | collective-permute-start | bytes 196616 | tf_op jit(solution)/shard_map/ppermute | solution.py:335
  1.7 6.4 %collective-permute-start.1 = (f32[64,256]{1,0:T(8,128)S(1)}, f32[64,256]{1,0:T(8,128)S(1)}, u32[]{:S(2)}, u32[]{:S(2)}) collective-permute-start(f32[64,256]{1,0:T(8,128)S(1)} %get-tuple-element.14), channel_id=1, source_target_pairs={{0,2},{1,3},{2,0},{3,1},{4,6},{5,7},{6,4},{7,5},{8,10},{9,11},{10,... | collective-permute-start | bytes 196616 | tf_op jit(solution)/shard_map/ppermute | solution.py:335
  4.1 5.6 %collective-permute-start.2 = (f32[64,256]{1,0:T(8,128)S(1)}, f32[64,256]{1,0:T(8,128)S(1)}, u32[]{:S(2)}, u32[]{:S(2)}) collective-permute-start(f32[64,256]{1,0:T(8,128)S(1)} %get-tuple-element.11), channel_id=1, source_target_pairs={{0,3},{1,2},{2,1},{3,0},{4,7},{5,6},{6,5},{7,4},{8,11},{9,10},{10,... | collective-permute-start | bytes 196616 | tf_op jit(solution)/shard_map/ppermute | solution.py:335
  5.1 1.1 %copy-start = (f32[3,256,256]{2,1,0:T(8,128)S(1)}, f32[3,256,256]{2,1,0:T(8,128)}, u32[]{:S(2)}) copy-start(f32[3,256,256]{2,1,0:T(8,128)} %pre_ref.3) | copy-start | bytes 2359300
  6.2 0.9 %copy-start.2 = (f32[256,256]{1,0:T(8,128)S(1)}, f32[256,256]{1,0:T(8,128)}, u32[]{:S(2)}) copy-start(f32[256,256]{1,0:T(8,128)} %raw_ref.1) | copy-start | bytes 786436
  7.2 0.7 copy-start.14
  9.9 44.0 %copy-start.3 = (bf16[256,256]{1,0:T(8,128)(2,1)S(1)}, bf16[256,256]{1,0:T(8,128)(2,1)}, u32[]{:S(2)}) copy-start(bf16[256,256]{1,0:T(8,128)(2,1)} %constant.43.clone.inner_h) | copy-start | bytes 393220
  9.9 44.0 %copy-start.4 = (bf16[256,256]{1,0:T(8,128)(2,1)S(1)}, bf16[256,256]{1,0:T(8,128)(2,1)}, u32[]{:S(2)}) copy-start(bf16[256,256]{1,0:T(8,128)(2,1)} %constant.44.clone.inner_l) | copy-start | bytes 393220
  9.9 44.0 %copy-start.5 = (bf16[256,256]{1,0:T(8,128)(2,1)S(1)}, bf16[256,256]{1,0:T(8,128)(2,1)}, u32[]{:S(2)}) copy-start(bf16[256,256]{1,0:T(8,128)(2,1)} %constant.45.clone.back_h) | copy-start | bytes 393220
  9.9 44.0 %copy-start.6 = (bf16[256,256]{1,0:T(8,128)(2,1)S(1)}, bf16[256,256]{1,0:T(8,128)(2,1)}, u32[]{:S(2)}) copy-start(bf16[256,256]{1,0:T(8,128)(2,1)} %constant.46.clone.back_l) | copy-start | bytes 393220
  9.9 44.0 %copy-start.7 = (bf16[256,128]{1,0:T(8,128)(2,1)S(1)}, bf16[256,128]{1,0:T(8,128)(2,1)}, u32[]{:S(2)}) copy-start(bf16[256,128]{1,0:T(8,128)(2,1)} %constant.41.clone.outer_h) | copy-start | bytes 196612
  9.9 44.0 %copy-start.8 = (bf16[256,128]{1,0:T(8,128)(2,1)S(1)}, bf16[256,128]{1,0:T(8,128)(2,1)}, u32[]{:S(2)}) copy-start(bf16[256,128]{1,0:T(8,128)(2,1)} %constant.42.clone.outer_l) | copy-start | bytes 196612
  10.0 44.0 %copy-start.9 = (bf16[128,256]{1,0:T(8,128)(2,1)S(1)}, bf16[128,256]{1,0:T(8,128)(2,1)}, u32[]{:S(2)}) copy-start(bf16[128,256]{1,0:T(8,128)(2,1)} %constant.47.clone.last_h) | copy-start | bytes 196612
  10.0 44.0 %copy-start.10 = (bf16[128,256]{1,0:T(8,128)(2,1)S(1)}, bf16[128,256]{1,0:T(8,128)(2,1)}, u32[]{:S(2)}) copy-start(bf16[128,256]{1,0:T(8,128)(2,1)} %constant.48.clone.last_l) | copy-start | bytes 196612
  10.0 44.0 %copy-start.11 = (f32[128,128]{1,0:T(8,128)S(1)}, f32[128,128]{1,0:T(8,128)}, u32[]{:S(2)}) copy-start(f32[128,128]{1,0:T(8,128)} %constant.49.clone.cos_ref) | copy-start | bytes 196612
  10.0 44.0 %copy-start.12 = (f32[128,128]{1,0:T(8,128)S(1)}, f32[128,128]{1,0:T(8,128)}, u32[]{:S(2)}) copy-start(f32[128,128]{1,0:T(8,128)} %constant.50.clone.sin_ref) | copy-start | bytes 196612
  10.0 44.0 %copy-start.13 = (f32[3,3,256]{2,1,0:T(4,128)S(1)}, f32[3,3,256]{2,1,0:T(4,128)}, u32[]{:S(2)}) copy-start(f32[3,3,256]{2,1,0:T(4,128)} %taps_ref.3) | copy-start | bytes 27652
  58.5 10.6 %copy-start.1 = (f32[3,256,256]{2,1,0:T(8,128)S(1)}, f32[3,256,256]{2,1,0:T(8,128)}, u32[]{:S(2)}) copy-start(f32[3,256,256]{2,1,0:T(8,128)} %pre_ref.3) | copy-start | bytes 2359300
  58.5 29.6 %all-to-all-start.1 = ((f32[64,25,1,128]{3,2,1,0:T(1,128)}), f32[64,25,1,128]{3,2,1,0:T(1,128)S(1)}, u32[]{:S(2)}, u32[]{:S(2)}) async-start(f32[64,25,1,128]{3,2,1,0:T(1,128)} %bitcast.9), calls=%async_computation.1 | async-start | bytes 1638400 | tf_op jit(solution)/shard_map/all_to_all | solution.py:322

commit v7 on v6

--- a/solution.py
+++ b/solution.py
@@ -136,7 +136,7 @@
         )
 
 
-def gate_body(at_ref, own_ref, one_ref, two_ref, three_ref, partial_ref, send_ref, rows_ref, block_ref, done):
+def gate_body(at_ref, three_ref, two_ref, one_ref, own_ref, partial_ref, send_ref, rows_ref, block_ref, done):
     count = own_ref.shape[0]
     for d, ref in enumerate((own_ref, one_ref, two_ref, three_ref)):
         base = pl.multiple_of((at_ref[0] ^ d) * count, count)
@@ -329,10 +329,10 @@
     tp_at = lax.axis_index("tp").astype(jnp.int32)
     place = lax.axis_index("ctx").astype(jnp.int32).reshape(1)
     turned = grad_out.T
-    pieces = []
-    for d in range(4):
+    pieces = [None] * 4
+    for d in (3, 2, 1, 0):
         piece = lax.dynamic_slice_in_dim(turned, (tp_at ^ d) * chans, chans, axis=1)
-        pieces.append(lax.ppermute(piece, "tp", [(k, k ^ d) for k in range(4)]) if d else piece)
+        pieces[d] = lax.ppermute(piece, "tp", [(k, k ^ d) for k in range(4)]) if d else piece
     partial, env = call(pack_body, ((PEERS * SENT, SIDE), (chans, tok)), [(SIDE, chans)], "pack", 1)(
         place, pre, raw_filter, decay.reshape(1, chans)
     )
@@ -353,7 +353,7 @@
         name="gate",
     )(
         tp_at.reshape(1),
-        *[pltpu.with_memory_space_constraint(piece, pltpu.VMEM) for piece in pieces],
+        *[pltpu.with_memory_space_constraint(piece, pltpu.VMEM) for piece in pieces[::-1]],
         partial.reshape(PEERS, SENT, SIDE),
     )
     recv = exchange(send).reshape(PEERS * SENT, SIDE)

time: 91.7 us -> 91.2 us (level)
  no operation moved by 1% of the time
where the time goes in v7:
time: 91.2 us; the launch traced here: 89.8 us
  blocking collectives  43.7 us (48%)
  waiting for transfers between devices  19.7 us (22%)
  starting transfers between devices  13.9 us (15%)
  Pallas kernels  7.84 us (9%)
  local copies, waits for them, and re-layouts  3.8 us (4%)
    all_to_all x1, blocking collectives, exchange(): lax.all_to_all(blocks, 'ctx', 0, 0, tiled=True, axis_index_groups=[ORDER])  43.7 us
    all_to_all x1, waiting for transfers between devices, exchange(): lax.all_to_all(blocks, 'ctx', 0, 0, tiled=True, axis_index_groups=[ORDER])  18.2 us
    all_to_all x1, starting transfers between devices, exchange(): lax.all_to_all(blocks, 'ctx', 0, 0, tiled=True, axis_index_groups=[ORDER])  10.4 us
    pallas_call x4, Pallas kernels, run(): pl.pallas_call(body, out_shape=tuple((kind(s, jnp.float32) for s in outs)...  7.66 us
    ppermute x3, starting transfers between devices, local(): lax.ppermute(piece, 'tp', [(k, k ^ d) for k in range(4)])  3.45 us
    unnamed x30, local copies, waits for them, and re-layouts  2.84 us
  transfers between devices with their start and end apart: 4, of which 2 were waited for; matrix products, arithmetic and copies ran while one was open for 0% of the time, Pallas kernels for 1%

profile of v7, /device:TPU:8, one launch (start us, length us, event | category | flops | bytes accessed | tf_op | source)
XLA Modules:
  0.0 89.8 jit_solution(15197589087236154611)
XLA Ops:
  0.7 1.0 %dynamic-slice_bitcast_fusion = (f32[64,256]{1,0:T(8,128)S(1)}, f32[64,256]{1,0:T(8,128)S(1)}, f32[64,256]{1,0:T(8,128)S(1)}, f32[64,256]{1,0:T(8,128)S(1)}) fusion(f32[1024,64]{0,1:T(8,128)} %param.19, s32[]{:T(128)S(6)} %select_n.15, s32[]{:T(128)S(6)} %select_n.13, s32[]{:T(128)S(6)} %select_n.12, s32[]{:T(128)S(6)} %select_n.14), kind=kLoop, calls=%fused_computation | loop fusion | bytes 524304 | tf_op jit(solution)/shard_map/dynamic_slice | solution.py:334
  1.6 1.8 %collective-permute-start = (f32[64,256]{1,0:T(8,128)S(1)}, f32[64,256]{1,0:T(8,128)S(1)}, u32[]{:S(2)}, u32[]{:S(2)}) collective-permute-start(f32[64,256]{1,0:T(8,128)S(1)} %get-tuple-element.13), channel_id=1, source_target_pairs={{0,3},{1,2},{2,1},{3,0},{4,7},{5,6},{6,5},{7,4},{8,11},{9,10},{10,... | collective-permute-start | bytes 196616 | tf_op jit(solution)/shard_map/ppermute | solution.py:335
  3.4 1.2 %collective-permute-start.1 = (f32[64,256]{1,0:T(8,128)S(1)}, f32[64,256]{1,0:T(8,128)S(1)}, u32[]{:S(2)}, u32[]{:S(2)}) collective-permute-start(f32[64,256]{1,0:T(8,128)S(1)} %get-tuple-element.12), channel_id=1, source_target_pairs={{0,2},{1,3},{2,0},{3,1},{4,6},{5,7},{6,4},{7,5},{8,10},{9,11},{10,... | collective-permute-start | bytes 196616 | tf_op jit(solution)/shard_map/ppermute | solution.py:335
  4.7 0.4 collective-permute-start.2
  5.1 1.1 %copy-done = f32[3,256,256]{2,1,0:T(8,128)S(1)} copy-done((f32[3,256,256]{2,1,0:T(8,128)S(1)}, f32[3,256,256]{2,1,0:T(8,128)}, u32[]{:S(2)}) %copy-start) | copy-done | bytes 786456
  6.2 0.9 %copy-done.2 = f32[256,256]{1,0:T(8,128)S(1)} copy-done((f32[256,256]{1,0:T(8,128)S(1)}, f32[256,256]{1,0:T(8,128)}, u32[]{:S(2)}) %copy-start.2) | copy-done | bytes 262168
  7.2 0.7 copy-done.14
  7.8 0.3 pack.1
  8.1 1.5 %collective-permute-done.1.two_ref = f32[64,256]{1,0:T(8,128)S(1)} collective-permute-done((f32[64,256]{1,0:T(8,128)S(1)}, f32[64,256]{1,0:T(8,128)S(1)}, u32[]{:S(2)}, u32[]{:S(2)}) %collective-permute-start.1) | collective-permute-done | bytes 65568 | tf_op jit(solution)/shard_map/ppermute | solution.py:335
  9.6 0.2 gate.1
  9.8 0.0 copy-start.3
  9.8 0.0 copy-start.4
  9.9 0.0 copy-start.6
  9.9 0.0 copy-start.7
  9.9 0.0 copy-start.8
  9.9 0.0 copy-start.9
  9.9 0.0 copy-start.10
  9.9 0.0 copy-start.11
  10.0 43.7 %all_to_all.10 = f32[64,40,128]{2,1,0:T(8,128)S(1)} all-to-all(f32[64,40,128]{2,1,0:T(8,128)S(1)} %gate.1), channel_id=1, replica_groups={{252,188,124,60,248,184,120,56,244,180,116,52,240,176,112,48,236,172,10..., dimensions={0} | all-to-all | bytes 2621440 | tf_op jit(solution)/shard_map/all_to_all | solution.py:322
  53.7 4.5 %long.1 = f32[1600,128]{1,0:T(8,128)} custom-call(s32[1]{0:T(128)} %bitcast.place_ref, f32[2560,128]{1,0:T(8,128)S(1)} %bitcast.16, f32[3,3,256]{2,1,0:T(4,128)S(1)} %copy-done.13, bf16[256,128]{1,0:T(8,128)(2,1)S(1)} %copy-done.7, bf16[256,128]{1,0:T(8,128)(2,1)S(1)} %copy-done.8, bf16[256,256]{1,0:T(8,128)(2,1)S(1)} %copy-done.3, ...), custom_call_target="tpu_custom_call" | custom-call | tf_op jit(solution)/shard_map/long/pallas_call | solution.py:308
  58.3 10.4 %all-to-all-start.1 = ((f32[64,25,1,128]{3,2,1,0:T(1,128)}), f32[64,25,1,128]{3,2,1,0:T(1,128)S(1)}, u32[]{:S(2)}, u32[]{:S(2)}) async-start(f32[64,25,1,128]{3,2,1,0:T(1,128)} %bitcast.9), calls=%async_computation.1 | async-start | bytes 1638400 | tf_op jit(solution)/shard_map/all_to_all | solution.py:322
  68.7 0.6 prepare.1
  69.4 18.2 %all-to-all-done.1 = f32[64,25,1,128]{3,2,1,0:T(1,128)S(1)} async-done(((f32[64,25,1,128]{3,2,1,0:T(1,128)}), f32[64,25,1,128]{3,2,1,0:T(1,128)S(1)}, u32[]{:S(2)}, u32[]{:S(2)}) %all-to-all-start.1) | async-done | bytes 819232 | tf_op jit(solution)/shard_map/all_to_all | solution.py:322
  87.6 2.2 %finish.1 = (f32[3,256,256]{2,1,0:T(8,128)}, f32[256,256]{1,0:T(8,128)}, f32[3,3,256]{2,1,0:T(4,128)}) custom-call(f32[1600,128]{1,0:T(8,128)S(1)} %bitcast.17, f32[2,256,256]{2,1,0:T(8,128)S(1)} %get-tuple-element.8.pair_ref, f32[256,128]{1,0:T(8,128)S(1)} %get-tuple-element.9.cols_in_ref, f32[256,256]{1,0:T(8,128)S(1)} %get-tuple-element.10.env_ref), custom_call_target="tpu_custom_call" | custom-call | tf_op jit(solution)/shard_map/finish/pallas_call | solution.py:308
  (21 shorter events, 0.1 us)
Async XLA Ops:
  1.6 6.5 %collective-permute-start = (f32[64,256]{1,0:T(8,128)S(1)}, f32[64,256]{1,0:T(8,128)S(1)}, u32[]{:S(2)}, u32[]{:S(2)}) collective-permute-start(f32[64,256]{1,0:T(8,128)S(1)} %get-tuple-element.13), channel_id=1, source_target_pairs={{0,3},{1,2},{2,1},{3,0},{4,7},{5,6},{6,5},{7,4},{8,11},{9,10},{10,... | collective-permute-start | bytes 196616 | tf_op jit(solution)/shard_map/ppermute | solution.py:335
  3.4 6.2 %collective-permute-start.1 = (f32[64,256]{1,0:T(8,128)S(1)}, f32[64,256]{1,0:T(8,128)S(1)}, u32[]{:S(2)}, u32[]{:S(2)}) collective-permute-start(f32[64,256]{1,0:T(8,128)S(1)} %get-tuple-element.12), channel_id=1, source_target_pairs={{0,2},{1,3},{2,0},{3,1},{4,6},{5,7},{6,4},{7,5},{8,10},{9,11},{10,... | collective-permute-start | bytes 196616 | tf_op jit(solution)/shard_map/ppermute | solution.py:335
  4.7 4.9 %collective-permute-start.2 = (f32[64,256]{1,0:T(8,128)S(1)}, f32[64,256]{1,0:T(8,128)S(1)}, u32[]{:S(2)}, u32[]{:S(2)}) collective-permute-start(f32[64,256]{1,0:T(8,128)S(1)} %get-tuple-element.14), channel_id=1, source_target_pairs={{0,1},{1,0},{2,3},{3,2},{4,5},{5,4},{6,7},{7,6},{8,9},{9,8},{10,11... | collective-permute-start | bytes 196616 | tf_op jit(solution)/shard_map/ppermute | solution.py:335
  5.1 1.1 %copy-start = (f32[3,256,256]{2,1,0:T(8,128)S(1)}, f32[3,256,256]{2,1,0:T(8,128)}, u32[]{:S(2)}) copy-start(f32[3,256,256]{2,1,0:T(8,128)} %pre_ref.3) | copy-start | bytes 2359300
  6.2 0.9 %copy-start.2 = (f32[256,256]{1,0:T(8,128)S(1)}, f32[256,256]{1,0:T(8,128)}, u32[]{:S(2)}) copy-start(f32[256,256]{1,0:T(8,128)} %raw_ref.1) | copy-start | bytes 786436
  7.2 0.7 copy-start.14
  9.8 43.8 %copy-start.3 = (bf16[256,256]{1,0:T(8,128)(2,1)S(1)}, bf16[256,256]{1,0:T(8,128)(2,1)}, u32[]{:S(2)}) copy-start(bf16[256,256]{1,0:T(8,128)(2,1)} %constant.43.clone.inner_h) | copy-start | bytes 393220
  9.8 43.8 %copy-start.4 = (bf16[256,256]{1,0:T(8,128)(2,1)S(1)}, bf16[256,256]{1,0:T(8,128)(2,1)}, u32[]{:S(2)}) copy-start(bf16[256,256]{1,0:T(8,128)(2,1)} %constant.44.clone.inner_l) | copy-start | bytes 393220
  9.8 43.8 %copy-start.5 = (bf16[256,256]{1,0:T(8,128)(2,1)S(1)}, bf16[256,256]{1,0:T(8,128)(2,1)}, u32[]{:S(2)}) copy-start(bf16[256,256]{1,0:T(8,128)(2,1)} %constant.45.clone.back_h) | copy-start | bytes 393220
  9.9 43.8 %copy-start.6 = (bf16[256,256]{1,0:T(8,128)(2,1)S(1)}, bf16[256,256]{1,0:T(8,128)(2,1)}, u32[]{:S(2)}) copy-start(bf16[256,256]{1,0:T(8,128)(2,1)} %constant.46.clone.back_l) | copy-start | bytes 393220
  9.9 43.8 %copy-start.7 = (bf16[256,128]{1,0:T(8,128)(2,1)S(1)}, bf16[256,128]{1,0:T(8,128)(2,1)}, u32[]{:S(2)}) copy-start(bf16[256,128]{1,0:T(8,128)(2,1)} %constant.41.clone.outer_h) | copy-start | bytes 196612
  9.9 43.8 %copy-start.8 = (bf16[256,128]{1,0:T(8,128)(2,1)S(1)}, bf16[256,128]{1,0:T(8,128)(2,1)}, u32[]{:S(2)}) copy-start(bf16[256,128]{1,0:T(8,128)(2,1)} %constant.42.clone.outer_l) | copy-start | bytes 196612
  9.9 43.8 %copy-start.9 = (bf16[128,256]{1,0:T(8,128)(2,1)S(1)}, bf16[128,256]{1,0:T(8,128)(2,1)}, u32[]{:S(2)}) copy-start(bf16[128,256]{1,0:T(8,128)(2,1)} %constant.47.clone.last_h) | copy-start | bytes 196612
  9.9 43.8 %copy-start.10 = (bf16[128,256]{1,0:T(8,128)(2,1)S(1)}, bf16[128,256]{1,0:T(8,128)(2,1)}, u32[]{:S(2)}) copy-start(bf16[128,256]{1,0:T(8,128)(2,1)} %constant.48.clone.last_l) | copy-start | bytes 196612
  9.9 43.8 %copy-start.11 = (f32[128,128]{1,0:T(8,128)S(1)}, f32[128,128]{1,0:T(8,128)}, u32[]{:S(2)}) copy-start(f32[128,128]{1,0:T(8,128)} %constant.49.clone.cos_ref) | copy-start | bytes 196612
  9.9 43.8 %copy-start.12 = (f32[128,128]{1,0:T(8,128)S(1)}, f32[128,128]{1,0:T(8,128)}, u32[]{:S(2)}) copy-start(f32[128,128]{1,0:T(8,128)} %constant.50.clone.sin_ref) | copy-start | bytes 196612
  9.9 43.8 %copy-start.13 = (f32[3,3,256]{2,1,0:T(4,128)S(1)}, f32[3,3,256]{2,1,0:T(4,128)}, u32[]{:S(2)}) copy-start(f32[3,3,256]{2,1,0:T(4,128)} %taps_ref.3) | copy-start | bytes 27652
  58.3 10.4 %copy-start.1 = (f32[3,256,256]{2,1,0:T(8,128)S(1)}, f32[3,256,256]{2,1,0:T(8,128)}, u32[]{:S(2)}) copy-start(f32[3,256,256]{2,1,0:T(8,128)} %pre_ref.3) | copy-start | bytes 2359300
  58.3 29.4 %all-to-all-start.1 = ((f32[64,25,1,128]{3,2,1,0:T(1,128)}), f32[64,25,1,128]{3,2,1,0:T(1,128)S(1)}, u32[]{:S(2)}, u32[]{:S(2)}) async-start(f32[64,25,1,128]{3,2,1,0:T(1,128)} %bitcast.9), calls=%async_computation.1 | async-start | bytes 1638400 | tf_op jit(solution)/shard_map/all_to_all | solution.py:322

commit v8 on v7

--- a/solution.py
+++ b/solution.py
@@ -55,6 +55,9 @@
 def product_left(high_ref, low_ref, value):
     high, low = halves_of(value)
     dot = functools.partial(jnp.dot, preferred_element_type=jnp.float32)
+    if value.shape[0] == SIDE:
+        twice = jnp.concatenate([high_ref[...], high_ref[...]], axis=1)
+        return dot(twice, jnp.concatenate([high, low], axis=0)) + dot(low_ref[...], high)
     return dot(high_ref[...], high) + (dot(high_ref[...], low) + dot(low_ref[...], high))
 
 

time: 91.2 us -> 91 us (level)
  no operation moved by 1% of the time
where the time goes in v8:
time: 91 us; the launch traced here: 89.6 us
  blocking collectives  43.7 us (48%)
  waiting for transfers between devices  19.7 us (22%)
  starting transfers between devices  13.9 us (15%)
  Pallas kernels  7.65 us (8%)
  local copies, waits for them, and re-layouts  3.8 us (4%)
    all_to_all x1, blocking collectives, exchange(): lax.all_to_all(blocks, 'ctx', 0, 0, tiled=True, axis_index_groups=[ORDER])  43.7 us
    all_to_all x1, waiting for transfers between devices, exchange(): lax.all_to_all(blocks, 'ctx', 0, 0, tiled=True, axis_index_groups=[ORDER])  18.2 us
    all_to_all x1, starting transfers between devices, exchange(): lax.all_to_all(blocks, 'ctx', 0, 0, tiled=True, axis_index_groups=[ORDER])  10.4 us
    pallas_call x4, Pallas kernels, run(): pl.pallas_call(body, out_shape=tuple((kind(s, jnp.float32) for s in outs)...  7.46 us
    ppermute x3, starting transfers between devices, local(): lax.ppermute(piece, 'tp', [(k, k ^ d) for k in range(4)])  3.45 us
    unnamed x30, local copies, waits for them, and re-layouts  2.84 us
  transfers between devices with their start and end apart: 4, of which 2 were waited for; matrix products, arithmetic and copies ran while one was open for 0% of the time, Pallas kernels for 1%

profile of v8, /device:TPU:8, one launch (start us, length us, event | category | flops | bytes accessed | tf_op | source)
XLA Modules:
  0.0 89.6 jit_solution(16811415811102736841)
XLA Ops:
  0.7 1.0 %dynamic-slice_bitcast_fusion = (f32[64,256]{1,0:T(8,128)S(1)}, f32[64,256]{1,0:T(8,128)S(1)}, f32[64,256]{1,0:T(8,128)S(1)}, f32[64,256]{1,0:T(8,128)S(1)}) fusion(f32[1024,64]{0,1:T(8,128)} %param.19, s32[]{:T(128)S(6)} %select_n.15, s32[]{:T(128)S(6)} %select_n.13, s32[]{:T(128)S(6)} %select_n.12, s32[]{:T(128)S(6)} %select_n.14), kind=kLoop, calls=%fused_computation | loop fusion | bytes 524304 | tf_op jit(solution)/shard_map/dynamic_slice | solution.py:337
  1.6 1.8 %collective-permute-start = (f32[64,256]{1,0:T(8,128)S(1)}, f32[64,256]{1,0:T(8,128)S(1)}, u32[]{:S(2)}, u32[]{:S(2)}) collective-permute-start(f32[64,256]{1,0:T(8,128)S(1)} %get-tuple-element.13), channel_id=1, source_target_pairs={{0,3},{1,2},{2,1},{3,0},{4,7},{5,6},{6,5},{7,4},{8,11},{9,10},{10,... | collective-permute-start | bytes 196616 | tf_op jit(solution)/shard_map/ppermute | solution.py:338
  3.4 1.2 %collective-permute-start.1 = (f32[64,256]{1,0:T(8,128)S(1)}, f32[64,256]{1,0:T(8,128)S(1)}, u32[]{:S(2)}, u32[]{:S(2)}) collective-permute-start(f32[64,256]{1,0:T(8,128)S(1)} %get-tuple-element.12), channel_id=1, source_target_pairs={{0,2},{1,3},{2,0},{3,1},{4,6},{5,7},{6,4},{7,5},{8,10},{9,11},{10,... | collective-permute-start | bytes 196616 | tf_op jit(solution)/shard_map/ppermute | solution.py:338
  4.7 0.4 collective-permute-start.2
  5.1 1.1 %copy-done = f32[3,256,256]{2,1,0:T(8,128)S(1)} copy-done((f32[3,256,256]{2,1,0:T(8,128)S(1)}, f32[3,256,256]{2,1,0:T(8,128)}, u32[]{:S(2)}) %copy-start) | copy-done | bytes 786456
  6.2 0.9 %copy-done.2 = f32[256,256]{1,0:T(8,128)S(1)} copy-done((f32[256,256]{1,0:T(8,128)S(1)}, f32[256,256]{1,0:T(8,128)}, u32[]{:S(2)}) %copy-start.2) | copy-done | bytes 262168
  7.2 0.7 copy-done.14
  7.8 0.3 pack.1
  8.1 1.5 %collective-permute-done.1.two_ref = f32[64,256]{1,0:T(8,128)S(1)} collective-permute-done((f32[64,256]{1,0:T(8,128)S(1)}, f32[64,256]{1,0:T(8,128)S(1)}, u32[]{:S(2)}, u32[]{:S(2)}) %collective-permute-start.1) | collective-permute-done | bytes 65568 | tf_op jit(solution)/shard_map/ppermute | solution.py:338
  9.6 0.2 gate.1
  9.8 0.0 copy-start.4
  9.8 0.0 copy-start.5
  9.9 0.0 copy-start.6
  9.9 0.0 copy-start.7
  9.9 0.0 copy-start.9
  9.9 0.0 copy-start.10
  9.9 0.0 copy-start.11
  9.9 0.0 copy-start.12
  10.0 43.7 %all_to_all.10 = f32[64,40,128]{2,1,0:T(8,128)S(1)} all-to-all(f32[64,40,128]{2,1,0:T(8,128)S(1)} %gate.1), channel_id=1, replica_groups={{252,188,124,60,248,184,120,56,244,180,116,52,240,176,112,48,236,172,10..., dimensions={0} | all-to-all | bytes 2621440 | tf_op jit(solution)/shard_map/all_to_all | solution.py:325
  53.7 4.3 %long.1 = f32[1600,128]{1,0:T(8,128)} custom-call(s32[1]{0:T(128)} %bitcast.place_ref, f32[2560,128]{1,0:T(8,128)S(1)} %bitcast.16, f32[3,3,256]{2,1,0:T(4,128)S(1)} %copy-done.13, bf16[256,128]{1,0:T(8,128)(2,1)S(1)} %copy-done.7, bf16[256,128]{1,0:T(8,128)(2,1)S(1)} %copy-done.8, bf16[256,256]{1,0:T(8,128)(2,1)S(1)} %copy-done.3, ...), custom_call_target="tpu_custom_call" | custom-call | tf_op jit(solution)/shard_map/long/pallas_call | solution.py:311
  58.1 10.4 %all-to-all-start.1 = ((f32[64,25,1,128]{3,2,1,0:T(1,128)}), f32[64,25,1,128]{3,2,1,0:T(1,128)S(1)}, u32[]{:S(2)}, u32[]{:S(2)}) async-start(f32[64,25,1,128]{3,2,1,0:T(1,128)} %bitcast.9), calls=%async_computation.1 | async-start | bytes 1638400 | tf_op jit(solution)/shard_map/all_to_all | solution.py:325
  68.5 0.6 prepare.1
  69.2 18.2 %all-to-all-done.1 = f32[64,25,1,128]{3,2,1,0:T(1,128)S(1)} async-done(((f32[64,25,1,128]{3,2,1,0:T(1,128)}), f32[64,25,1,128]{3,2,1,0:T(1,128)S(1)}, u32[]{:S(2)}, u32[]{:S(2)}) %all-to-all-start.1) | async-done | bytes 819232 | tf_op jit(solution)/shard_map/all_to_all | solution.py:325
  87.4 2.2 %finish.1 = (f32[3,256,256]{2,1,0:T(8,128)}, f32[256,256]{1,0:T(8,128)}, f32[3,3,256]{2,1,0:T(4,128)}) custom-call(f32[1600,128]{1,0:T(8,128)S(1)} %bitcast.17, f32[2,256,256]{2,1,0:T(8,128)S(1)} %get-tuple-element.8.pair_ref, f32[256,128]{1,0:T(8,128)S(1)} %get-tuple-element.9.cols_in_ref, f32[256,256]{1,0:T(8,128)S(1)} %get-tuple-element.10.env_ref), custom_call_target="tpu_custom_call" | custom-call | tf_op jit(solution)/shard_map/finish/pallas_call | solution.py:311
  (21 shorter events, 0.1 us)
Async XLA Ops:
  1.6 6.5 %collective-permute-start = (f32[64,256]{1,0:T(8,128)S(1)}, f32[64,256]{1,0:T(8,128)S(1)}, u32[]{:S(2)}, u32[]{:S(2)}) collective-permute-start(f32[64,256]{1,0:T(8,128)S(1)} %get-tuple-element.13), channel_id=1, source_target_pairs={{0,3},{1,2},{2,1},{3,0},{4,7},{5,6},{6,5},{7,4},{8,11},{9,10},{10,... | collective-permute-start | bytes 196616 | tf_op jit(solution)/shard_map/ppermute | solution.py:338
  3.4 6.2 %collective-permute-start.1 = (f32[64,256]{1,0:T(8,128)S(1)}, f32[64,256]{1,0:T(8,128)S(1)}, u32[]{:S(2)}, u32[]{:S(2)}) collective-permute-start(f32[64,256]{1,0:T(8,128)S(1)} %get-tuple-element.12), channel_id=1, source_target_pairs={{0,2},{1,3},{2,0},{3,1},{4,6},{5,7},{6,4},{7,5},{8,10},{9,11},{10,... | collective-permute-start | bytes 196616 | tf_op jit(solution)/shard_map/ppermute | solution.py:338
  4.7 4.9 %collective-permute-start.2 = (f32[64,256]{1,0:T(8,128)S(1)}, f32[64,256]{1,0:T(8,128)S(1)}, u32[]{:S(2)}, u32[]{:S(2)}) collective-permute-start(f32[64,256]{1,0:T(8,128)S(1)} %get-tuple-element.14), channel_id=1, source_target_pairs={{0,1},{1,0},{2,3},{3,2},{4,5},{5,4},{6,7},{7,6},{8,9},{9,8},{10,11... | collective-permute-start | bytes 196616 | tf_op jit(solution)/shard_map/ppermute | solution.py:338
  5.1 1.1 %copy-start = (f32[3,256,256]{2,1,0:T(8,128)S(1)}, f32[3,256,256]{2,1,0:T(8,128)}, u32[]{:S(2)}) copy-start(f32[3,256,256]{2,1,0:T(8,128)} %pre_ref.3) | copy-start | bytes 2359300
  6.2 0.9 %copy-start.2 = (f32[256,256]{1,0:T(8,128)S(1)}, f32[256,256]{1,0:T(8,128)}, u32[]{:S(2)}) copy-start(f32[256,256]{1,0:T(8,128)} %raw_ref.1) | copy-start | bytes 786436
  7.2 0.7 copy-start.14
  9.8 43.8 %copy-start.3 = (bf16[256,256]{1,0:T(8,128)(2,1)S(1)}, bf16[256,256]{1,0:T(8,128)(2,1)}, u32[]{:S(2)}) copy-start(bf16[256,256]{1,0:T(8,128)(2,1)} %constant.43.clone.inner_h) | copy-start | bytes 393220
  9.8 43.8 %copy-start.4 = (bf16[256,256]{1,0:T(8,128)(2,1)S(1)}, bf16[256,256]{1,0:T(8,128)(2,1)}, u32[]{:S(2)}) copy-start(bf16[256,256]{1,0:T(8,128)(2,1)} %constant.44.clone.inner_l) | copy-start | bytes 393220
  9.8 43.8 %copy-start.5 = (bf16[256,256]{1,0:T(8,128)(2,1)S(1)}, bf16[256,256]{1,0:T(8,128)(2,1)}, u32[]{:S(2)}) copy-start(bf16[256,256]{1,0:T(8,128)(2,1)} %constant.45.clone.back_h) | copy-start | bytes 393220
  9.9 43.8 %copy-start.6 = (bf16[256,256]{1,0:T(8,128)(2,1)S(1)}, bf16[256,256]{1,0:T(8,128)(2,1)}, u32[]{:S(2)}) copy-start(bf16[256,256]{1,0:T(8,128)(2,1)} %constant.46.clone.back_l) | copy-start | bytes 393220
  9.9 43.8 %copy-start.7 = (bf16[256,128]{1,0:T(8,128)(2,1)S(1)}, bf16[256,128]{1,0:T(8,128)(2,1)}, u32[]{:S(2)}) copy-start(bf16[256,128]{1,0:T(8,128)(2,1)} %constant.41.clone.outer_h) | copy-start | bytes 196612
  9.9 43.8 %copy-start.8 = (bf16[256,128]{1,0:T(8,128)(2,1)S(1)}, bf16[256,128]{1,0:T(8,128)(2,1)}, u32[]{:S(2)}) copy-start(bf16[256,128]{1,0:T(8,128)(2,1)} %constant.42.clone.outer_l) | copy-start | bytes 196612
  9.9 43.8 %copy-start.9 = (bf16[128,256]{1,0:T(8,128)(2,1)S(1)}, bf16[128,256]{1,0:T(8,128)(2,1)}, u32[]{:S(2)}) copy-start(bf16[128,256]{1,0:T(8,128)(2,1)} %constant.47.clone.last_h) | copy-start | bytes 196612
  9.9 43.8 %copy-start.10 = (bf16[128,256]{1,0:T(8,128)(2,1)S(1)}, bf16[128,256]{1,0:T(8,128)(2,1)}, u32[]{:S(2)}) copy-start(bf16[128,256]{1,0:T(8,128)(2,1)} %constant.48.clone.last_l) | copy-start | bytes 196612
  9.9 43.8 %copy-start.11 = (f32[128,128]{1,0:T(8,128)S(1)}, f32[128,128]{1,0:T(8,128)}, u32[]{:S(2)}) copy-start(f32[128,128]{1,0:T(8,128)} %constant.49.clone.cos_ref) | copy-start | bytes 196612
  9.9 43.8 %copy-start.12 = (f32[128,128]{1,0:T(8,128)S(1)}, f32[128,128]{1,0:T(8,128)}, u32[]{:S(2)}) copy-start(f32[128,128]{1,0:T(8,128)} %constant.50.clone.sin_ref) | copy-start | bytes 196612
  9.9 43.8 %copy-start.13 = (f32[3,3,256]{2,1,0:T(4,128)S(1)}, f32[3,3,256]{2,1,0:T(4,128)}, u32[]{:S(2)}) copy-start(f32[3,3,256]{2,1,0:T(4,128)} %taps_ref.3) | copy-start | bytes 27652
  58.1 10.4 %copy-start.1 = (f32[3,256,256]{2,1,0:T(8,128)S(1)}, f32[3,256,256]{2,1,0:T(8,128)}, u32[]{:S(2)}) copy-start(f32[3,256,256]{2,1,0:T(8,128)} %pre_ref.3) | copy-start | bytes 2359300
  58.1 29.3 %all-to-all-start.1 = ((f32[64,25,1,128]{3,2,1,0:T(1,128)}), f32[64,25,1,128]{3,2,1,0:T(1,128)S(1)}, u32[]{:S(2)}, u32[]{:S(2)}) async-start(f32[64,25,1,128]{3,2,1,0:T(1,128)} %bitcast.9), calls=%async_computation.1 | async-start | bytes 1638400 | tf_op jit(solution)/shard_map/all_to_all | solution.py:325
